TPU v7x, 32 devices: a whole 2x2x4 slice. The times are simulated.
32 devices in a mesh: rep: 4 (over y, x), shard: 4 (over z), seq: 2 (over core).
Axes of the slice: x: 2, y: 2, z: 4, core: 2. Of those that a mesh axis runs over, the one named last changes fastest.
Arguments:
- inputs: bfloat16 [16, 1024, 1024], P(('rep', 'shard'), 'seq'), may hold values from -6 to 6
- documents: int32 [16, 1024], P(('rep', 'shard')), may hold values from 0 to 3, never falling along the last dimension, each value on 1 to 512 neighbouring positions
- norm_attn_one: float32 [1024], P(('shard', 'seq')), may hold values from 0.25 to 1.75
- query_one: float32 [1024, 1024], P(('shard', 'seq')), may hold values from -0.1875 to 0.1875
- key_one: float32 [1024, 1024], P(('shard', 'seq')), may hold values from -0.1875 to 0.1875
- value_one: float32 [1024, 1024], P(('shard', 'seq')), may hold values from -0.1875 to 0.1875
- proj_one: float32 [1024, 1024], P(('shard', 'seq')), may hold values from -0.75 to 0.75
- norm_ffn_one: float32 [1024], P(('shard', 'seq')), may hold values from 0.25 to 1.75
- gate_one: float32 [1024, 2816], P(('shard', 'seq')), may hold values from -0.1875 to 0.1875
- upward_one: float32 [1024, 2816], P(('shard', 'seq')), may hold values from -0.1875 to 0.1875
- down_one: float32 [2816, 1024], P(('shard', 'seq')), may hold values from -0.109375 to 0.109375
- norm_attn_two: float32 [1024], P(('shard', 'seq')), may hold values from 0.25 to 1.75
- query_two: float32 [1024, 1024], P(('shard', 'seq')), may hold values from -0.1875 to 0.1875
- key_two: float32 [1024, 1024], P(('shard', 'seq')), may hold values from -0.1875 to 0.1875
- value_two: float32 [1024, 1024], P(('shard', 'seq')), may hold values from -0.1875 to 0.1875
- proj_two: float32 [1024, 1024], P(('shard', 'seq')), may hold values from -0.75 to 0.75
- norm_ffn_two: float32 [1024], P(('shard', 'seq')), may hold values from 0.25 to 1.75
- gate_two: float32 [1024, 2816], P(('shard', 'seq')), may hold values from -0.1875 to 0.1875
- upward_two: float32 [1024, 2816], P(('shard', 'seq')), may hold values from -0.1875 to 0.1875
- down_two: float32 [2816, 1024], P(('shard', 'seq')), may hold values from -0.109375 to 0.109375
- cotangent: bfloat16 [16, 1024, 1024], P(('rep', 'shard'), 'seq'), may hold values from -6 to 6
Outputs:
- outputs: bfloat16 [16, 1024, 1024], P(('rep', 'shard'), 'seq')
- grad_input: float32 [16, 1024, 1024], P(('rep', 'shard'), 'seq')
- grad_norm_attn_one: float32 [1024], P(('shard', 'seq'))
- grad_query_one: float32 [1024, 1024], P(('shard', 'seq'))
- grad_key_one: float32 [1024, 1024], P(('shard', 'seq'))
- grad_value_one: float32 [1024, 1024], P(('shard', 'seq'))
- grad_proj_one: float32 [1024, 1024], P(('shard', 'seq'))
- grad_norm_ffn_one: float32 [1024], P(('shard', 'seq'))
- grad_gate_one: float32 [1024, 2816], P(('shard', 'seq'))
- grad_upward_one: float32 [1024, 2816], P(('shard', 'seq'))
- grad_down_one: float32 [2816, 1024], P(('shard', 'seq'))
- grad_norm_attn_two: float32 [1024], P(('shard', 'seq'))
- grad_query_two: float32 [1024, 1024], P(('shard', 'seq'))
- grad_key_two: float32 [1024, 1024], P(('shard', 'seq'))
- grad_value_two: float32 [1024, 1024], P(('shard', 'seq'))
- grad_proj_two: float32 [1024, 1024], P(('shard', 'seq'))
- grad_norm_ffn_two: float32 [1024], P(('shard', 'seq'))
- grad_gate_two: float32 [1024, 2816], P(('shard', 'seq'))
- grad_upward_two: float32 [1024, 2816], P(('shard', 'seq'))
- grad_down_two: float32 [2816, 1024], P(('shard', 'seq'))
Inputs may be any that keep to these rules, and one draw needn't show every extreme that they name: `documents`: ids never fall along a sequence; a document holds 1 to 512 tokens.
All inputs are finite; a program needn't handle non-finite values.
Results may differ from a plain program's by a relative error of at most 0.033.
Values may be sent and summed in bfloat16 or wider, within the bound.
No kernel may reach another device: no remote copies, remote signals or barrier semaphores. Data moves between devices by JAX's collectives and lax.ppermute only.
A program may use at most 200 MiB of HBM per device.

v0:
```python
import jax
import jax.numpy as jnp
from jax import lax
from jax.sharding import PartitionSpec as P

HEADS = 16
HD = 64
BLOCK = 256


eps_norm = 1e-05
rope_base = 10000.0
mask_fill = -1000000000.0
group_heads = 4


def shifted(x, axis, by):
    count = lax.axis_size(axis)
    pairs = [(i, i + by) for i in range(count) if 0 <= i + by < count]
    return lax.ppermute(x, axis, pairs)


def norm_ahead(values, gain_row):
    factor = lax.rsqrt(jnp.mean(values * values, axis=-1, keepdims=True) + eps_norm)
    return ((values * factor * gain_row.astype(jnp.float32)).astype(jnp.bfloat16), factor)


def norm_back(values, factor, gain_row, upstream):
    scaled = upstream * gain_row.astype(jnp.float32)
    gain_grad = jnp.sum(upstream * values * factor, axis=0)
    inner_mean = jnp.mean(scaled * values, axis=-1, keepdims=True)
    return (factor * scaled - values * (factor * factor * factor) * inner_mean, gain_grad)


def rotate_rows(flat, batch_size, cosine_table, sine_table, inverse):
    shaped = flat.reshape(batch_size, -1, HEADS, HD)
    half_size = HD // 2
    first_half = shaped[..., :half_size]
    second_half = shaped[..., half_size:]
    if inverse:
        turned = jnp.concatenate(
            [
                first_half * cosine_table + second_half * sine_table,
                second_half * cosine_table - first_half * sine_table,
            ],
            axis=-1,
        )
    else:
        turned = jnp.concatenate(
            [
                first_half * cosine_table - second_half * sine_table,
                second_half * cosine_table + first_half * sine_table,
            ],
            axis=-1,
        )
    return turned.reshape(flat.shape)


def split_groups(values):
    batch_size, length_rows, feature_count = values.shape
    group_count = HEADS // group_heads
    shaped = values.reshape(batch_size, length_rows, group_count, group_heads, HD)
    return shaped.transpose(0, 2, 1, 3, 4).reshape(
        batch_size * group_count, length_rows, group_heads, HD
    )


def merge_groups(values, batch_size):
    item_count, length_rows = (values.shape[0], values.shape[1])
    group_count = item_count // batch_size
    shaped = values.reshape(batch_size, group_count, length_rows, group_heads, HD)
    return shaped.transpose(0, 2, 1, 3, 4).reshape(
        batch_size, length_rows, group_count * group_heads * HD
    )


def masked_scores(query_group, key_group, allowed):
    scores = jnp.einsum(
        "qhd,khd->hqk", query_group, key_group, preferred_element_type=jnp.float32
    ) * HD ** (-0.5)
    return jnp.where(allowed[None], scores, mask_fill)


def attend_ahead(query_group, key_group, value_group, allowed):
    scores = masked_scores(query_group, key_group, allowed)
    top_score = jnp.max(scores, axis=-1, keepdims=True)
    exp_scores = jnp.exp(scores - top_score)
    total = jnp.sum(exp_scores, axis=-1, keepdims=True)
    attn_weights = (exp_scores / total).astype(jnp.bfloat16)
    attended = jnp.einsum(
        "hqk,khd->qhd", attn_weights, value_group, preferred_element_type=jnp.float32
    )
    return (attended.astype(jnp.bfloat16), top_score + jnp.log(total))


def attend_back(query_group, key_group, value_group, allowed, grad_group, log_total):
    scores = masked_scores(query_group, key_group, allowed)
    attn_weights = jnp.exp(scores - log_total)
    grad_weights = jnp.einsum(
        "qhd,khd->hqk", grad_group, value_group, preferred_element_type=jnp.float32
    )
    row_delta = jnp.sum(attn_weights * grad_weights, axis=-1, keepdims=True)
    grad_scores = (attn_weights * (grad_weights - row_delta) * HD ** (-0.5)).astype(jnp.bfloat16)
    grad_queries = jnp.einsum(
        "hqk,khd->qhd", grad_scores, key_group, preferred_element_type=jnp.float32
    )
    grad_keys = jnp.einsum(
        "hqk,qhd->khd", grad_scores, query_group, preferred_element_type=jnp.float32
    )
    grad_values = jnp.einsum(
        "hqk,qhd->khd",
        attn_weights.astype(jnp.bfloat16),
        grad_group,
        preferred_element_type=jnp.float32,
    )
    return (grad_queries, grad_keys, grad_values)


def attention_ahead(query_rows, key_rows, value_rows, masks):
    batch_size = query_rows.shape[0]
    group_count = HEADS // group_heads
    seq_picks = jnp.arange(batch_size * group_count, dtype=jnp.int32) // group_count

    def one_group(packed):
        query_group, key_group, value_group, seq_pick = packed
        allowed = lax.dynamic_index_in_dim(masks, seq_pick, 0, keepdims=False)
        return attend_ahead(query_group, key_group, value_group, allowed)

    attended, log_total = lax.map(
        one_group,
        (split_groups(query_rows), split_groups(key_rows), split_groups(value_rows), seq_picks),
    )
    return (merge_groups(attended, batch_size), log_total)


def attention_back(query_rows, key_rows, value_rows, masks, grad_rows, log_total):
    batch_size = query_rows.shape[0]
    group_count = HEADS // group_heads
    seq_picks = jnp.arange(batch_size * group_count, dtype=jnp.int32) // group_count

    def one_group(packed):
        query_group, key_group, value_group, grad_group, total_group, seq_pick = packed
        allowed = lax.dynamic_index_in_dim(masks, seq_pick, 0, keepdims=False)
        return attend_back(query_group, key_group, value_group, allowed, grad_group, total_group)

    grad_queries, grad_keys, grad_values = lax.map(
        one_group,
        (
            split_groups(query_rows),
            split_groups(key_rows),
            split_groups(value_rows),
            split_groups(grad_rows),
            log_total,
            seq_picks,
        ),
    )
    return (
        merge_groups(grad_queries, batch_size),
        merge_groups(grad_keys, batch_size),
        merge_groups(grad_values, batch_size),
    )


def gather_ahead(masters):
    gain_attn, w_query, w_key, w_value, w_proj, gain_ffn, w_gate, w_upward, w_down = masters
    return (
        lax.all_gather(gain_attn.astype(jnp.bfloat16), ("shard", "seq"), axis=0, tiled=True),
        lax.all_gather(w_query.astype(jnp.bfloat16), ("shard", "seq"), axis=0, tiled=True),
        lax.all_gather(w_key.astype(jnp.bfloat16), ("shard", "seq"), axis=0, tiled=True),
        lax.all_gather(w_value.astype(jnp.bfloat16), ("shard", "seq"), axis=0, tiled=True),
        lax.all_gather(w_proj.astype(jnp.bfloat16), ("shard", "seq"), axis=0, tiled=True),
        lax.all_gather(gain_ffn.astype(jnp.bfloat16), ("shard", "seq"), axis=0, tiled=True),
        lax.all_gather(w_gate.astype(jnp.bfloat16), ("shard", "seq"), axis=0, tiled=True),
        lax.all_gather(w_upward.astype(jnp.bfloat16), ("shard", "seq"), axis=0, tiled=True),
        lax.all_gather(w_down.astype(jnp.bfloat16), ("shard", "seq"), axis=0, tiled=True),
    )


def gather_back(masters):
    gain_attn, w_query, w_key, w_value, w_proj, gain_ffn, w_gate, w_upward, w_down = masters
    return (
        lax.all_gather(gain_attn.astype(jnp.bfloat16), ("shard", "seq"), axis=0, tiled=True),
        lax.all_gather(w_query.astype(jnp.bfloat16), ("shard", "seq"), axis=0, tiled=True),
        lax.all_gather(w_key.astype(jnp.bfloat16), ("shard", "seq"), axis=0, tiled=True),
        lax.all_gather(w_value.astype(jnp.bfloat16), ("shard", "seq"), axis=0, tiled=True),
        lax.all_gather(w_proj.astype(jnp.bfloat16), ("shard", "seq"), axis=0, tiled=True),
        lax.all_gather(gain_ffn.astype(jnp.bfloat16), ("shard", "seq"), axis=0, tiled=True),
        lax.all_gather(w_gate.astype(jnp.bfloat16), ("shard", "seq"), axis=0, tiled=True),
        lax.all_gather(w_upward.astype(jnp.bfloat16), ("shard", "seq"), axis=0, tiled=True),
        lax.all_gather(w_down.astype(jnp.bfloat16), ("shard", "seq"), axis=0, tiled=True),
    )


def reduce_grads(grads):
    (
        grad_gain_attn,
        grad_query,
        grad_key,
        grad_value,
        grad_proj,
        grad_gain_ffn,
        grad_gate,
        grad_upward,
        grad_down,
    ) = grads
    owned_rows = (
        lax.psum_scatter(
            grad_gain_attn.astype(jnp.bfloat16), ("shard", "seq"), scatter_dimension=0, tiled=True
        ).astype(jnp.float32),
        lax.psum_scatter(
            grad_query.astype(jnp.bfloat16), ("shard", "seq"), scatter_dimension=0, tiled=True
        ).astype(jnp.float32),
        lax.psum_scatter(
            grad_key.astype(jnp.bfloat16), ("shard", "seq"), scatter_dimension=0, tiled=True
        ).astype(jnp.float32),
        lax.psum_scatter(
            grad_value.astype(jnp.bfloat16), ("shard", "seq"), scatter_dimension=0, tiled=True
        ).astype(jnp.float32),
        lax.psum_scatter(
            grad_proj.astype(jnp.bfloat16), ("shard", "seq"), scatter_dimension=0, tiled=True
        ).astype(jnp.float32),
        lax.psum_scatter(
            grad_gain_ffn.astype(jnp.bfloat16), ("shard", "seq"), scatter_dimension=0, tiled=True
        ).astype(jnp.float32),
        lax.psum_scatter(
            grad_gate.astype(jnp.bfloat16), ("shard", "seq"), scatter_dimension=0, tiled=True
        ).astype(jnp.float32),
        lax.psum_scatter(
            grad_upward.astype(jnp.bfloat16), ("shard", "seq"), scatter_dimension=0, tiled=True
        ).astype(jnp.float32),
        lax.psum_scatter(
            grad_down.astype(jnp.bfloat16), ("shard", "seq"), scatter_dimension=0, tiled=True
        ).astype(jnp.float32),
    )
    summed = (
        lax.psum(owned_rows[0].astype(jnp.bfloat16), "rep").astype(jnp.float32),
        lax.psum(owned_rows[1].astype(jnp.bfloat16), "rep").astype(jnp.float32),
        lax.psum(owned_rows[2].astype(jnp.bfloat16), "rep").astype(jnp.float32),
        lax.psum(owned_rows[3].astype(jnp.bfloat16), "rep").astype(jnp.float32),
        lax.psum(owned_rows[4].astype(jnp.bfloat16), "rep").astype(jnp.float32),
        lax.psum(owned_rows[5].astype(jnp.bfloat16), "rep").astype(jnp.float32),
        lax.psum(owned_rows[6].astype(jnp.bfloat16), "rep").astype(jnp.float32),
        lax.psum(owned_rows[7].astype(jnp.bfloat16), "rep").astype(jnp.float32),
        lax.psum(owned_rows[8].astype(jnp.bfloat16), "rep").astype(jnp.float32),
    )
    return tuple(summed)


def layer_ahead(flat, weights, value_first, context):
    gain_attn, w_query, w_key, w_value, w_proj, gain_ffn, w_gate, w_upward, w_down = weights
    batch_size, masks, cosine_table, sine_table = context
    normed, factor_attn = norm_ahead(flat, gain_attn)
    query_flat = rotate_rows(
        jnp.dot(normed, w_query, preferred_element_type=jnp.float32),
        batch_size,
        cosine_table,
        sine_table,
        False,
    ).astype(jnp.bfloat16)
    key_flat = rotate_rows(
        jnp.dot(normed, w_key, preferred_element_type=jnp.float32),
        batch_size,
        cosine_table,
        sine_table,
        False,
    ).astype(jnp.bfloat16)
    projected = jnp.dot(normed, w_value, preferred_element_type=jnp.float32)
    if value_first is None:
        value_mix = projected.astype(jnp.bfloat16)
    else:
        value_mix = (0.5 * projected + 0.5 * value_first.astype(jnp.float32)).astype(jnp.bfloat16)
    key_before, value_before = shifted((key_flat, value_mix), "seq", 1)
    shape_rows = (batch_size, -1, flat.shape[1])
    key_rows = jnp.concatenate(
        [key_before.reshape(shape_rows), key_flat.reshape(shape_rows)], axis=1
    )
    value_rows = jnp.concatenate(
        [value_before.reshape(shape_rows), value_mix.reshape(shape_rows)], axis=1
    )
    query_rows = query_flat.reshape(shape_rows)
    attended, log_total = attention_ahead(query_rows, key_rows, value_rows, masks)
    attended = attended.reshape(flat.shape)
    middle = flat + jnp.dot(attended, w_proj, preferred_element_type=jnp.float32)
    normed_ffn, factor_ffn = norm_ahead(middle, gain_ffn)
    gate_pre = jnp.dot(normed_ffn, w_gate, preferred_element_type=jnp.float32)
    upward_pre = jnp.dot(normed_ffn, w_upward, preferred_element_type=jnp.float32)
    inner = (jax.nn.silu(gate_pre) * upward_pre).astype(jnp.bfloat16)
    result = middle + jnp.dot(inner, w_down, preferred_element_type=jnp.float32)
    kept = (
        flat,
        factor_attn,
        normed,
        query_rows,
        key_rows,
        value_rows,
        log_total,
        attended,
        middle,
        factor_ffn,
        normed_ffn,
        gate_pre,
        upward_pre,
        inner,
    )
    return (result, value_mix, kept)


def layer_back(upstream, weights, kept, value_extra, context):
    gain_attn, w_query, w_key, w_value, w_proj, gain_ffn, w_gate, w_upward, w_down = weights
    batch_size, masks, cosine_table, sine_table = context
    (
        flat,
        factor_attn,
        normed,
        query_rows,
        key_rows,
        value_rows,
        log_total,
        attended,
        middle,
        factor_ffn,
        normed_ffn,
        gate_pre,
        upward_pre,
        inner,
    ) = kept
    grad_down_in = upstream.astype(jnp.bfloat16)
    grad_w_down = jnp.einsum("nf,nd->fd", inner, grad_down_in, preferred_element_type=jnp.float32)
    grad_inner = jnp.einsum("nd,fd->nf", grad_down_in, w_down, preferred_element_type=jnp.float32)
    sigmoid_gate = jax.nn.sigmoid(gate_pre)
    grad_gate = (
        grad_inner * upward_pre * sigmoid_gate * (1.0 + gate_pre * (1.0 - sigmoid_gate))
    ).astype(jnp.bfloat16)
    grad_upward = (grad_inner * gate_pre * sigmoid_gate).astype(jnp.bfloat16)
    grad_w_gate = jnp.einsum("nd,nf->df", normed_ffn, grad_gate, preferred_element_type=jnp.float32)
    grad_w_upward = jnp.einsum(
        "nd,nf->df", normed_ffn, grad_upward, preferred_element_type=jnp.float32
    )
    grad_normed_ffn = jnp.einsum(
        "nf,df->nd", grad_gate, w_gate, preferred_element_type=jnp.float32
    ) + jnp.einsum("nf,df->nd", grad_upward, w_upward, preferred_element_type=jnp.float32)
    grad_part_ffn, grad_gain_ffn = norm_back(middle, factor_ffn, gain_ffn, grad_normed_ffn)
    grad_middle = upstream + grad_part_ffn
    grad_branch = grad_middle.astype(jnp.bfloat16)
    grad_w_proj = jnp.einsum("nd,ne->de", attended, grad_branch, preferred_element_type=jnp.float32)
    grad_attended = jnp.einsum(
        "ne,de->nd", grad_branch, w_proj, preferred_element_type=jnp.float32
    ).astype(jnp.bfloat16)
    shape_rows = (batch_size, -1, flat.shape[1])
    grad_query_rot, grad_key_all, grad_value_all = attention_back(
        query_rows, key_rows, value_rows, masks, grad_attended.reshape(shape_rows), log_total
    )
    row_count = query_rows.shape[1]
    key_sent, value_sent = (
        shifted(grad_key_all[:, :row_count].astype(jnp.bfloat16), "seq", -1).astype(jnp.float32),
        shifted(grad_value_all[:, :row_count].astype(jnp.bfloat16), "seq", -1).astype(jnp.float32),
    )
    grad_key_rot = (grad_key_all[:, row_count:] + key_sent).reshape(flat.shape)
    grad_value_mix = (grad_value_all[:, row_count:] + value_sent).reshape(flat.shape)
    if value_extra is None:
        grad_projected = (0.5 * grad_value_mix).astype(jnp.bfloat16)
        passed = 0.5 * grad_value_mix
    else:
        grad_projected = (grad_value_mix + value_extra).astype(jnp.bfloat16)
        passed = None
    grad_queries = rotate_rows(
        grad_query_rot.reshape(flat.shape), batch_size, cosine_table, sine_table, True
    ).astype(jnp.bfloat16)
    grad_keys = rotate_rows(grad_key_rot, batch_size, cosine_table, sine_table, True).astype(
        jnp.bfloat16
    )
    grad_w_query = jnp.einsum("nd,ne->de", normed, grad_queries, preferred_element_type=jnp.float32)
    grad_w_key = jnp.einsum("nd,ne->de", normed, grad_keys, preferred_element_type=jnp.float32)
    grad_w_value = jnp.einsum(
        "nd,ne->de", normed, grad_projected, preferred_element_type=jnp.float32
    )
    grad_normed = (
        jnp.einsum("ne,de->nd", grad_queries, w_query, preferred_element_type=jnp.float32)
        + jnp.einsum("ne,de->nd", grad_keys, w_key, preferred_element_type=jnp.float32)
        + jnp.einsum("ne,de->nd", grad_projected, w_value, preferred_element_type=jnp.float32)
    )
    grad_part_attn, grad_gain_attn = norm_back(flat, factor_attn, gain_attn, grad_normed)
    grad_flat = grad_middle + grad_part_attn
    grads = (
        grad_gain_attn,
        grad_w_query,
        grad_w_key,
        grad_w_value,
        grad_w_proj,
        grad_gain_ffn,
        grad_w_gate,
        grad_w_upward,
        grad_w_down,
    )
    return (grad_flat, grads, passed)


def shards(
    inputs,
    documents,
    norm_attn_one,
    query_one,
    key_one,
    value_one,
    proj_one,
    norm_ffn_one,
    gate_one,
    upward_one,
    down_one,
    norm_attn_two,
    query_two,
    key_two,
    value_two,
    proj_two,
    norm_ffn_two,
    gate_two,
    upward_two,
    down_two,
    cotangent,
):
    batch_size, row_count, feature_count = inputs.shape
    seq_index = lax.axis_index("seq")
    row_start = seq_index * row_count
    query_pos = row_start + jnp.arange(row_count, dtype=jnp.int32)
    key_pos = jnp.concatenate([query_pos - row_count, query_pos])
    docs_query = lax.dynamic_slice_in_dim(documents, row_start, row_count, 1)
    docs_before = lax.dynamic_slice_in_dim(
        documents, jnp.maximum(row_start - row_count, 0), row_count, 1
    )
    docs_key = jnp.concatenate([docs_before, docs_query], axis=1)
    masks = (
        (key_pos[None, None, :] >= 0)
        & (key_pos[None, None, :] // BLOCK <= query_pos[None, :, None] // BLOCK)
        & (docs_key[:, None, :] == docs_query[:, :, None])
    )
    frequencies = rope_base ** (-(jnp.arange(HD // 2, dtype=jnp.float32) * 2.0 / HD))
    angles = query_pos.astype(jnp.float32)[:, None] * frequencies[None, :]
    cosine_table = jnp.cos(angles)[None, :, None, :]
    sine_table = jnp.sin(angles)[None, :, None, :]
    context = (batch_size, masks, cosine_table, sine_table)
    masters_one = (
        norm_attn_one,
        query_one,
        key_one,
        value_one,
        proj_one,
        norm_ffn_one,
        gate_one,
        upward_one,
        down_one,
    )
    masters_two = (
        norm_attn_two,
        query_two,
        key_two,
        value_two,
        proj_two,
        norm_ffn_two,
        gate_two,
        upward_two,
        down_two,
    )
    flat = inputs.reshape(batch_size * row_count, feature_count).astype(jnp.float32)
    weights_one = gather_ahead(masters_one)
    middle_one, value_first, kept_one = layer_ahead(flat, weights_one, None, context)
    weights_two = gather_ahead(masters_two)
    final, unused, kept_two = layer_ahead(middle_one, weights_two, value_first, context)
    outputs = final.astype(jnp.bfloat16).reshape(batch_size, row_count, feature_count)
    back_two = gather_back(masters_two)
    upstream = cotangent.reshape(batch_size * row_count, feature_count).astype(jnp.float32)
    grad_middle, grads_two, value_extra = layer_back(upstream, back_two, kept_two, None, context)
    reduced_two = reduce_grads(grads_two)
    back_one = gather_back(masters_one)
    grad_flat, grads_one, unused_extra = layer_back(
        grad_middle, back_one, kept_one, value_extra, context
    )
    reduced_one = reduce_grads(grads_one)
    grad_input = grad_flat.reshape(batch_size, row_count, feature_count)
    return (outputs, grad_input) + reduced_one + reduced_two


def solution(mesh):
    return jax.shard_map(
        shards,
        mesh=mesh,
        in_specs=(
            P(("rep", "shard"), "seq", None),
            P(("rep", "shard"), None),
            P(("shard", "seq")),
            P(("shard", "seq"), None),
            P(("shard", "seq"), None),
            P(("shard", "seq"), None),
            P(("shard", "seq"), None),
            P(("shard", "seq")),
            P(("shard", "seq"), None),
            P(("shard", "seq"), None),
            P(("shard", "seq"), None),
            P(("shard", "seq")),
            P(("shard", "seq"), None),
            P(("shard", "seq"), None),
            P(("shard", "seq"), None),
            P(("shard", "seq"), None),
            P(("shard", "seq")),
            P(("shard", "seq"), None),
            P(("shard", "seq"), None),
            P(("shard", "seq"), None),
            P(("rep", "shard"), "seq", None),
        ),
        out_specs=(
            P(("rep", "shard"), "seq", None),
            P(("rep", "shard"), "seq", None),
            P(("shard", "seq")),
            P(("shard", "seq"), None),
            P(("shard", "seq"), None),
            P(("shard", "seq"), None),
            P(("shard", "seq"), None),
            P(("shard", "seq")),
            P(("shard", "seq"), None),
            P(("shard", "seq"), None),
            P(("shard", "seq"), None),
            P(("shard", "seq")),
            P(("shard", "seq"), None),
            P(("shard", "seq"), None),
            P(("shard", "seq"), None),
            P(("shard", "seq"), None),
            P(("shard", "seq")),
            P(("shard", "seq"), None),
            P(("shard", "seq"), None),
            P(("shard", "seq"), None),
        ),
        check_vma=False,
    )
```

profile of v0, /device:TPU:0, one launch (start us, length us, event | category | flops | bytes accessed | tf_op | source)
XLA Modules:
  0.0 1870.6 jit_solution(15795709616958572673)
XLA Ops:
  23.5 13.5 all-gather
  37.9 8.6 all-gather.1
  46.6 10.1 all-gather.2
  56.8 8.8 all-gather.3
  81.0 22.9 %all-gather.21.cloned.1.call-done = bf16[1024,1024]{1,0:T(8,128)(2,1)} async-done(((bf16[128,1024]{1,0:T(8,128)(2,1)}), bf16[1024,1024]{1,0:T(8,128)(2,1)}) %all-gather.21.cloned.1.call-update) | async-done | bytes 2097168 | tf_op jit(solution)/shard_map/all_gather | solution.py:168
  127.0 39.7 %while.60 = (s32[]{:T(128)}, bf16[4,512,4,64]{1,3,2,0:T(8,128)(2,1)}, f32[4,4,512,1]{2,1,3,0:T(4,128)S(1)}, bf16[4,1024,4,64]{1,3,2,0:T(8,128)(2,1)}, bf16[4,512...) while((s32[]{:T(128)}, ...), condition=%wide.region_4.5_spmd.clone, body=%wide.region_1.4_spmd.clone.sunk | while | flops 564262912 | bytes 28916864 | solution.py:129
  172.4 24.2 %all-gather.27.cloned.1.call-done = bf16[1024,2816]{1,0:T(8,128)(2,1)} async-done(((bf16[128,2816]{1,0:T(8,128)(2,1)}), bf16[1024,2816]{1,0:T(8,128)(2,1)}) %all-gather.27.cloned.1.call-update) | async-done | bytes 5767184 | tf_op jit(solution)/shard_map/all_gather | solution.py:173
  196.6 7.6 fusion.270
  204.2 53.0 %all-gather.29.cloned.1.call-done = bf16[1024,2816]{1,0:T(8,128)(2,1)} async-done(((bf16[128,2816]{1,0:T(8,128)(2,1)}), bf16[1024,2816]{1,0:T(8,128)(2,1)}) %all-gather.29.cloned.1.call-update) | async-done | bytes 5767184 | tf_op jit(solution)/shard_map/all_gather | solution.py:174
  257.2 9.0 multiply_convert_fusion.7
  266.2 51.8 %all-gather.31.cloned.1.call-done = bf16[2816,1024]{1,0:T(8,128)(2,1)} async-done(((bf16[352,1024]{1,0:T(8,128)(2,1)}), bf16[2816,1024]{1,0:T(8,128)(2,1)}) %all-gather.31.cloned.1.call-update) | async-done | bytes 5767184 | tf_op jit(solution)/shard_map/all_gather | solution.py:175
  326.0 22.0 %all-gather.33.cloned.1.call-done = bf16[1024,1024]{1,0:T(8,128)(2,1)} async-done(((bf16[128,1024]{1,0:T(8,128)(2,1)}), bf16[1024,1024]{1,0:T(8,128)(2,1)}) %all-gather.33.cloned.1.call-update) | async-done | bytes 2097168 | tf_op jit(solution)/shard_map/all_gather | solution.py:170
  355.3 23.6 %all-gather.37.cloned.1.call-done = bf16[1024,1024]{1,0:T(8,128)(2,1)} async-done(((bf16[128,1024]{1,0:T(8,128)(2,1)}), bf16[1024,1024]{1,0:T(8,128)(2,1)}) %all-gather.37.cloned.1.call-update) | async-done | bytes 2097168 | tf_op jit(solution)/shard_map/all_gather | solution.py:169
  386.9 22.6 %all-gather.35.cloned.1.call-done = bf16[1024,1024]{1,0:T(8,128)(2,1)} async-done(((bf16[128,1024]{1,0:T(8,128)(2,1)}), bf16[1024,1024]{1,0:T(8,128)(2,1)}) %all-gather.35.cloned.1.call-update) | async-done | bytes 2097168 | tf_op jit(solution)/shard_map/all_gather | solution.py:168
  421.7 37.2 %while.61 = (s32[]{:T(128)}, bf16[4,512,4,64]{1,3,2,0:T(8,128)(2,1)S(1)}, f32[4,4,512,1]{2,1,3,0:T(4,128)S(1)}, bf16[4,1024,4,64]{1,3,2,0:T(8,128)(2,1)}, bf16[4...) while((s32[]{:T(128)}, ...), condition=%wide.region_10.11_spmd.clone, body=%wide.region_7.10_spmd.clone.sunk | while | flops 564262912 | bytes 28916864 | solution.py:129
  464.6 37.2 %all-gather.41.cloned.1.call-done = bf16[1024,2816]{1,0:T(8,128)(2,1)} async-done(((bf16[128,2816]{1,0:T(8,128)(2,1)}), bf16[1024,2816]{1,0:T(8,128)(2,1)}) %all-gather.41.cloned.1.call-update) | async-done | bytes 5767184 | tf_op jit(solution)/shard_map/all_gather | solution.py:173
  501.8 7.6 fusion.273
  509.4 53.2 %all-gather.43.cloned.1.call-done = bf16[1024,2816]{1,0:T(8,128)(2,1)} async-done(((bf16[128,2816]{1,0:T(8,128)(2,1)}), bf16[1024,2816]{1,0:T(8,128)(2,1)}) %all-gather.43.cloned.1.call-update) | async-done | bytes 5767184 | tf_op jit(solution)/shard_map/all_gather | solution.py:174
  562.6 8.7 fusion.274
  571.3 52.0 %all-gather.45.cloned.1.call-done = bf16[2816,1024]{1,0:T(8,128)(2,1)} async-done(((bf16[352,1024]{1,0:T(8,128)(2,1)}), bf16[2816,1024]{1,0:T(8,128)(2,1)}) %all-gather.45.cloned.1.call-update) | async-done | bytes 5767184 | tf_op jit(solution)/shard_map/all_gather | solution.py:175
  623.2 11.3 multiply_convert_fusion.4
  634.5 7.3 fusion.275
  657.0 221.9 %while.62 = (s32[]{:T(128)}, f32[4,512,4,64]{1,3,2,0:T(8,128)}, f32[4,1024,4,64]{1,3,2,0:T(8,128)}, f32[4,1024,4,64]{1,3,2,0:T(8,128)}, bf16[4,1024,4,64]{1,3,2,...) while((s32[]{:T(128)}, f32[4,512,4,64]{1,3,2,0:T(8,128)}, ...), condition=%wide.region_15.16_spmd.clone, body=%wide.region_13.15_spmd.clone.sunk | while | flops 1398806528 | bytes 100739224 | solution.py:146
  669.2 17.9 fusion.407
  687.1 18.9 %fusion.408 = f32[4,1024,4,64]{1,3,2,0:T(8,128)} fusion(f32[4,1024,4,64]{1,3,2,0:T(8,128)} %get-tuple-element.1168, s32[]{:T(128)S(6)} %copy.117, f32[4,512,1024]{2,1,0:T(8,128)} %fusion.405, f32[4,512,1024]{2,1,0:T(8,128)} %fusion.406, f32[4,512]{1,0:T(4,128)S(1)} %dynamic-slice_bitcast_fusion.4, pred[512,1024]{1,0:T(8,128)(4,1)S(1)} %and_bitcast_fusion.10, ...), kind=kOutput, calls=%fused_computation.70.clone.1 | convolution fusion | flops 291507200 | bytes 35931136 | tf_op jit(solution)/shard_map/while/body/eval_jaxpr/hqk,qhd->khd/dot_general | solution.py:107
  705.9 6.8 fusion.409
  724.7 17.9 fusion.407
  742.5 18.8 %fusion.408 = f32[4,1024,4,64]{1,3,2,0:T(8,128)} fusion(f32[4,1024,4,64]{1,3,2,0:T(8,128)} %get-tuple-element.1168, s32[]{:T(128)S(6)} %copy.117, f32[4,512,1024]{2,1,0:T(8,128)} %fusion.405, f32[4,512,1024]{2,1,0:T(8,128)} %fusion.406, f32[4,512]{1,0:T(4,128)S(1)} %dynamic-slice_bitcast_fusion.4, pred[512,1024]{1,0:T(8,128)(4,1)S(1)} %and_bitcast_fusion.10, ...), kind=kOutput, calls=%fused_computation.70.clone.1 | convolution fusion | flops 291507200 | bytes 35931136 | tf_op jit(solution)/shard_map/while/body/eval_jaxpr/hqk,qhd->khd/dot_general | solution.py:107
  780.0 17.9 fusion.407
  797.9 18.8 %fusion.408 = f32[4,1024,4,64]{1,3,2,0:T(8,128)} fusion(f32[4,1024,4,64]{1,3,2,0:T(8,128)} %get-tuple-element.1168, s32[]{:T(128)S(6)} %copy.117, f32[4,512,1024]{2,1,0:T(8,128)} %fusion.405, f32[4,512,1024]{2,1,0:T(8,128)} %fusion.406, f32[4,512]{1,0:T(4,128)S(1)} %dynamic-slice_bitcast_fusion.4, pred[512,1024]{1,0:T(8,128)(4,1)S(1)} %and_bitcast_fusion.10, ...), kind=kOutput, calls=%fused_computation.70.clone.1 | convolution fusion | flops 291507200 | bytes 35931136 | tf_op jit(solution)/shard_map/while/body/eval_jaxpr/hqk,qhd->khd/dot_general | solution.py:107
  816.7 6.8 fusion.409
  835.4 17.9 fusion.407
  853.3 18.9 %fusion.408 = f32[4,1024,4,64]{1,3,2,0:T(8,128)} fusion(f32[4,1024,4,64]{1,3,2,0:T(8,128)} %get-tuple-element.1168, s32[]{:T(128)S(6)} %copy.117, f32[4,512,1024]{2,1,0:T(8,128)} %fusion.405, f32[4,512,1024]{2,1,0:T(8,128)} %fusion.406, f32[4,512]{1,0:T(4,128)S(1)} %dynamic-slice_bitcast_fusion.4, pred[512,1024]{1,0:T(8,128)(4,1)S(1)} %and_bitcast_fusion.10, ...), kind=kOutput, calls=%fused_computation.70.clone.1 | convolution fusion | flops 291507200 | bytes 35931136 | tf_op jit(solution)/shard_map/while/body/eval_jaxpr/hqk,qhd->khd/dot_general | solution.py:107
  904.4 11.3 multiply_convert_fusion.2
  954.6 225.4 %while.63 = (s32[]{:T(128)}, f32[4,512,4,64]{1,3,2,0:T(8,128)}, f32[4,1024,4,64]{1,3,2,0:T(8,128)}, f32[4,1024,4,64]{1,3,2,0:T(8,128)}, bf16[4,1024,4,64]{1,3,2,...) while((s32[]{:T(128)}, f32[4,512,4,64]{1,3,2,0:T(8,128)}, ...), condition=%wide.region_20.21_spmd.clone, body=%wide.region_18.20_spmd.clone.sunk | while | flops 1398806528 | bytes 100739224 | solution.py:146
  967.4 18.0 fusion.422
  985.5 19.1 %fusion.423 = f32[4,1024,4,64]{1,3,2,0:T(8,128)} fusion(f32[4,1024,4,64]{1,3,2,0:T(8,128)} %get-tuple-element.1213, s32[]{:T(128)S(6)} %copy.129, f32[4,512,1024]{2,1,0:T(8,128)} %fusion.420, f32[4,512,1024]{2,1,0:T(8,128)} %fusion.421, f32[4,512]{1,0:T(4,128)S(1)} %dynamic-slice_bitcast_fusion.5, pred[512,1024]{1,0:T(8,128)(4,1)S(1)} %and_bitcast_fusion.11, ...), kind=kOutput, calls=%fused_computation.125.clone.1 | convolution fusion | flops 291507200 | bytes 35931136 | tf_op jit(solution)/shard_map/while/body/eval_jaxpr/hqk,qhd->khd/dot_general | solution.py:107
  1004.5 6.8 fusion.424
  1024.0 18.0 fusion.422
  1042.0 19.0 %fusion.423 = f32[4,1024,4,64]{1,3,2,0:T(8,128)} fusion(f32[4,1024,4,64]{1,3,2,0:T(8,128)} %get-tuple-element.1213, s32[]{:T(128)S(6)} %copy.129, f32[4,512,1024]{2,1,0:T(8,128)} %fusion.420, f32[4,512,1024]{2,1,0:T(8,128)} %fusion.421, f32[4,512]{1,0:T(4,128)S(1)} %dynamic-slice_bitcast_fusion.5, pred[512,1024]{1,0:T(8,128)(4,1)S(1)} %and_bitcast_fusion.11, ...), kind=kOutput, calls=%fused_computation.125.clone.1 | convolution fusion | flops 291507200 | bytes 35931136 | tf_op jit(solution)/shard_map/while/body/eval_jaxpr/hqk,qhd->khd/dot_general | solution.py:107
  1061.0 6.8 fusion.424
  1080.5 17.9 fusion.422
  1098.4 18.8 %fusion.423 = f32[4,1024,4,64]{1,3,2,0:T(8,128)} fusion(f32[4,1024,4,64]{1,3,2,0:T(8,128)} %get-tuple-element.1213, s32[]{:T(128)S(6)} %copy.129, f32[4,512,1024]{2,1,0:T(8,128)} %fusion.420, f32[4,512,1024]{2,1,0:T(8,128)} %fusion.421, f32[4,512]{1,0:T(4,128)S(1)} %dynamic-slice_bitcast_fusion.5, pred[512,1024]{1,0:T(8,128)(4,1)S(1)} %and_bitcast_fusion.11, ...), kind=kOutput, calls=%fused_computation.125.clone.1 | convolution fusion | flops 291507200 | bytes 35931136 | tf_op jit(solution)/shard_map/while/body/eval_jaxpr/hqk,qhd->khd/dot_general | solution.py:107
  1136.5 17.8 fusion.422
  1154.4 18.8 %fusion.423 = f32[4,1024,4,64]{1,3,2,0:T(8,128)} fusion(f32[4,1024,4,64]{1,3,2,0:T(8,128)} %get-tuple-element.1213, s32[]{:T(128)S(6)} %copy.129, f32[4,512,1024]{2,1,0:T(8,128)} %fusion.420, f32[4,512,1024]{2,1,0:T(8,128)} %fusion.421, f32[4,512]{1,0:T(4,128)S(1)} %dynamic-slice_bitcast_fusion.5, pred[512,1024]{1,0:T(8,128)(4,1)S(1)} %and_bitcast_fusion.11, ...), kind=kOutput, calls=%fused_computation.125.clone.1 | convolution fusion | flops 291507200 | bytes 35931136 | tf_op jit(solution)/shard_map/while/body/eval_jaxpr/hqk,qhd->khd/dot_general | solution.py:107
  1173.2 6.7 fusion.424
  1213.2 6.8 convolution_convert_fusion.2
  1220.1 7.0 convolution_convert_fusion.1
  1228.3 6.9 convolution_convert_fusion
  1236.6 6.8 convolution_convert_fusion.5
  1243.5 6.9 convolution_convert_fusion.4
  1251.9 6.9 convolution_convert_fusion.3
  1259.0 7.0 reduce-scatter.17.cloned.1.call-done
  1266.0 36.8 %reduce-scatter.19.cloned.1.call-done = bf16[128,1024]{1,0:T(8,128)(2,1)} async-done(((bf16[1024,1024]{1,0:T(8,128)(2,1)}), bf16[128,1024]{1,0:T(8,128)(2,1)}) %reduce-scatter.19.cloned.1.call-update) | async-done | bytes 262160 | tf_op jit(solution)/shard_map/reduce_scatter | solution.py:216
  1302.8 65.9 %reduce-scatter.37.cloned.1.call-done = bf16[128,2816]{1,0:T(8,128)(2,1)} async-done(((bf16[1024,2816]{1,0:T(8,128)(2,1)}), bf16[128,2816]{1,0:T(8,128)(2,1)}) %reduce-scatter.37.cloned.1.call-update) | async-done | bytes 720912 | tf_op jit(solution)/shard_map/reduce_scatter | solution.py:225
  1368.7 65.4 %reduce-scatter.39.cloned.1.call-done = bf16[128,2816]{1,0:T(8,128)(2,1)} async-done(((bf16[1024,2816]{1,0:T(8,128)(2,1)}), bf16[128,2816]{1,0:T(8,128)(2,1)}) %reduce-scatter.39.cloned.1.call-update) | async-done | bytes 720912 | tf_op jit(solution)/shard_map/reduce_scatter | solution.py:228
  1434.1 65.6 %reduce-scatter.41.cloned.1.call-done = bf16[352,1024]{1,0:T(8,128)(2,1)} async-done(((bf16[2816,1024]{1,0:T(8,128)(2,1)}), bf16[352,1024]{1,0:T(8,128)(2,1)}) %reduce-scatter.41.cloned.1.call-update) | async-done | bytes 720912 | tf_op jit(solution)/shard_map/reduce_scatter | solution.py:231
  1499.6 65.4 %reduce-scatter.23.cloned.1.call-done = bf16[128,2816]{1,0:T(8,128)(2,1)} async-done(((bf16[1024,2816]{1,0:T(8,128)(2,1)}), bf16[128,2816]{1,0:T(8,128)(2,1)}) %reduce-scatter.23.cloned.1.call-update) | async-done | bytes 720912 | tf_op jit(solution)/shard_map/reduce_scatter | solution.py:225
  1565.1 65.4 %reduce-scatter.25.cloned.1.call-done = bf16[128,2816]{1,0:T(8,128)(2,1)} async-done(((bf16[1024,2816]{1,0:T(8,128)(2,1)}), bf16[128,2816]{1,0:T(8,128)(2,1)}) %reduce-scatter.25.cloned.1.call-update) | async-done | bytes 720912 | tf_op jit(solution)/shard_map/reduce_scatter | solution.py:228
  1630.5 65.6 %reduce-scatter.27.cloned.1.call-done = bf16[352,1024]{1,0:T(8,128)(2,1)} async-done(((bf16[2816,1024]{1,0:T(8,128)(2,1)}), bf16[352,1024]{1,0:T(8,128)(2,1)}) %reduce-scatter.27.cloned.1.call-update) | async-done | bytes 720912 | tf_op jit(solution)/shard_map/reduce_scatter | solution.py:231
  1698.0 7.8 fusion.225
  1712.4 13.9 all-reduce.4
  1726.7 9.9 all-reduce.5
  1742.1 104.6 %all-reduce.9.cloned.1.call-done = (bf16[128,1024]{1,0:T(8,128)(2,1)}, bf16[128,1024]{1,0:T(8,128)(2,1)}, bf16[128,1024]{1,0:T(8,128)(2,1)}, bf16[128,1024]{1,0:...) async-done(((bf16[128,1024]{1,0:T(8,128)(2,1)}, ...) | async-done | bytes 6422544 | tf_op jit(solution)/shard_map/psum | solution.py:237
  (543 shorter events, 444.3 us)
Async XLA Ops:
  7.2 59.3 %all-gather.19.cloned.1.call-start = ((), (), s32[]{:S(2)}) async-start(), calls=%async_computation.14 | async-start | bytes 2359296 | tf_op jit(solution)/shard_map/all_gather | solution.py:170
  9.2 64.4 %all-gather.23.cloned.1.call-start = ((), (), s32[]{:S(2)}) async-start(), calls=%async_computation.16 | async-start | bytes 2359296 | tf_op jit(solution)/shard_map/all_gather | solution.py:169
  11.1 92.9 %all-gather.21.cloned.1.call-start = ((), (), s32[]{:S(2)}) async-start(), calls=%async_computation.15 | async-start | bytes 2359296 | tf_op jit(solution)/shard_map/all_gather | solution.py:168
  11.9 154.8 %all-gather.25.cloned.1.call-start = ((), (), s32[]{:S(2)}) async-start(), calls=%async_computation.17 | async-start | bytes 2359296 | tf_op jit(solution)/shard_map/all_gather | solution.py:171
  12.7 183.9 %all-gather.27.cloned.1.call-start = ((), (), s32[]{:S(2)}) async-start(), calls=%async_computation.18 | async-start | bytes 6488064 | tf_op jit(solution)/shard_map/all_gather | solution.py:173
  13.7 243.5 %all-gather.29.cloned.1.call-start = ((), (), s32[]{:S(2)}) async-start(), calls=%async_computation.19 | async-start | bytes 6488064 | tf_op jit(solution)/shard_map/all_gather | solution.py:174
  14.8 303.2 %all-gather.31.cloned.1.call-start = ((), (), s32[]{:S(2)}) async-start(), calls=%async_computation.20 | async-start | bytes 6488064 | tf_op jit(solution)/shard_map/all_gather | solution.py:175
  16.4 331.6 %all-gather.33.cloned.1.call-start = ((), (), s32[]{:S(2)}) async-start(), calls=%async_computation.21 | async-start | bytes 2359296 | tf_op jit(solution)/shard_map/all_gather | solution.py:170
  17.3 361.6 %all-gather.37.cloned.1.call-start = ((), (), s32[]{:S(2)}) async-start(), calls=%async_computation.23 | async-start | bytes 2359296 | tf_op jit(solution)/shard_map/all_gather | solution.py:169
  18.1 391.4 %all-gather.35.cloned.1.call-start = ((), (), s32[]{:S(2)}) async-start(), calls=%async_computation.22 | async-start | bytes 2359296 | tf_op jit(solution)/shard_map/all_gather | solution.py:168
  18.9 440.0 %all-gather.39.cloned.1.call-start = ((), (), s32[]{:S(2)}) async-start(), calls=%async_computation.24 | async-start | bytes 2359296 | tf_op jit(solution)/shard_map/all_gather | solution.py:171
  19.7 482.0 %all-gather.41.cloned.1.call-start = ((), (), s32[]{:S(2)}) async-start(), calls=%async_computation.25 | async-start | bytes 6488064 | tf_op jit(solution)/shard_map/all_gather | solution.py:173
  20.8 541.8 %all-gather.43.cloned.1.call-start = ((), (), s32[]{:S(2)}) async-start(), calls=%async_computation.26 | async-start | bytes 6488064 | tf_op jit(solution)/shard_map/all_gather | solution.py:174
  21.8 15.3 copy-start.8
  21.8 16.1 copy-start.104
  21.8 24.8 %copy-start.105 = (f32[128]{0:T(128)S(1)}, f32[128]{0:T(128)}, u32[]{:S(2)}) copy-start(f32[128]{0:T(128)} %param.40) | copy-start | bytes 1540
  21.8 34.9 %copy-start.106 = (f32[128]{0:T(128)S(1)}, f32[128]{0:T(128)}, u32[]{:S(2)}) copy-start(f32[128]{0:T(128)} %param.45) | copy-start | bytes 1540
  21.8 44.6 %copy-start.96 = (s32[1,1024]{1,0:T(1,128)S(1)}, s32[1,1024]{1,0:T(1,128)}, u32[]{:S(2)}) copy-start(s32[1,1024]{1,0:T(1,128)} %param.30) | copy-start | bytes 12292
  21.8 601.4 %all-gather.45.cloned.1.call-start = ((), (), s32[]{:S(2)}) async-start(), calls=%async_computation.27 | async-start | bytes 6488064 | tf_op jit(solution)/shard_map/all_gather | solution.py:175
  23.4 1235.5 %reduce-scatter.35.cloned.1.call-start = ((), (), s32[]{:S(2)}) async-start(), calls=%async_computation.38 | async-start | bytes 2359296 | tf_op jit(solution)/shard_map/reduce_scatter | solution.py:219
  37.0 74.0 %copy-start.81 = (f32[8,1,128]{2,1,0:T(1,128)}, f32[8,1,128]{2,1,0:T(1,128)S(1)}, u32[]{:S(2)}) copy-start(f32[8,1,128]{2,1,0:T(1,128)S(1)} %convert_element_type.589) | copy-start | bytes 12292
  37.9 73.1 %copy-start.88 = (f32[512]{0:T(512)}, f32[512]{0:T(512)S(1)}, u32[]{:S(2)}) copy-start(f32[512]{0:T(512)S(1)} %get-tuple-element.746) | copy-start | bytes 6148
  46.6 124.8 %copy-start.84 = (f32[8,1,128]{2,1,0:T(1,128)}, f32[8,1,128]{2,1,0:T(1,128)S(1)}, u32[]{:S(2)}) copy-start(f32[8,1,128]{2,1,0:T(1,128)S(1)} %convert_element_type.590) | copy-start | bytes 12292
  56.8 268.3 %copy-start.79 = (f32[8,1,128]{2,1,0:T(1,128)}, f32[8,1,128]{2,1,0:T(1,128)S(1)}, u32[]{:S(2)}) copy-start(f32[8,1,128]{2,1,0:T(1,128)S(1)} %convert_element_type.591) | copy-start | bytes 12292
  66.4 346.0 %copy-start.29 = (f32[512,32]{0,1:T(8,128)}, f32[512,32]{0,1:T(8,128)S(1)}, u32[]{:S(2)}) copy-start(f32[512,32]{0,1:T(8,128)S(1)} %get-tuple-element.743) | copy-start | bytes 196612
  66.4 346.0 %copy-start.32 = (f32[512,32]{0,1:T(8,128)}, f32[512,32]{0,1:T(8,128)S(1)}, u32[]{:S(2)}) copy-start(f32[512,32]{0,1:T(8,128)S(1)} %get-tuple-element.744) | copy-start | bytes 196612
  70.4 48.6 %collective-permute-start = (bf16[512,1024]{1,0:T(8,128)(2,1)}, bf16[512,1024]{1,0:T(8,128)(2,1)}, u32[]{:S(2)}, u32[]{:S(2)}) collective-permute-start(bf16[512,1024]{1,0:T(8,128)(2,1)} %convolution_convert_fusion.16), channel_id=1, source_target_pairs={{0,1},{2,3},{4,5},{6,7},{8,9},{10,11},{12,13},{14,15},{16,17},{18,... | collective-permute-start | bytes 3145736 | tf_op jit(solution)/shard_map/ppermute | solution.py:20
  78.3 29.5 %copy-start.25 = (bf16[1,512,16,64]{1,3,2,0:T(8,128)(2,1)}, bf16[1,512,16,64]{1,3,2,0:T(8,128)(2,1)S(1)}, u32[]{:S(2)}) copy-start(bf16[1,512,16,64]{1,3,2,0:T(8,128)(2,1)S(1)} %maximum_convert_fusion) | copy-start | bytes 3145732
  107.9 16.5 collective-permute-start.1
  171.4 32.8 %copy-start.90 = (f32[512]{0:T(512)}, f32[512]{0:T(512)S(1)}, u32[]{:S(2)}) copy-start(f32[512]{0:T(512)S(1)} %get-tuple-element.748) | copy-start | bytes 6148
  172.4 84.9 %copy-start.47 = (bf16[512,1024]{1,0:T(8,128)(2,1)}, bf16[512,1024]{1,0:T(8,128)(2,1)S(1)}, u32[]{:S(2)}) copy-start(bf16[512,1024]{1,0:T(8,128)(2,1)S(1)} %multiply_convert_fusion.11) | copy-start | bytes 3145732
  204.2 113.8 %copy-start.6 = (f32[512,1024]{1,0:T(8,128)S(1)}, f32[512,1024]{1,0:T(8,128)}, u32[]{:S(2)}) copy-start(f32[512,1024]{1,0:T(8,128)} %copy-done.5) | copy-start | bytes 6291460
  325.0 27.1 %copy-start.86 = (f32[512]{0:T(512)}, f32[512]{0:T(512)S(1)}, u32[]{:S(2)}) copy-start(f32[512]{0:T(512)S(1)} %get-tuple-element.750) | copy-start | bytes 6148
  326.0 83.5 %copy-start.51 = (bf16[512,1024]{1,0:T(8,128)(2,1)}, bf16[512,1024]{1,0:T(8,128)(2,1)S(1)}, u32[]{:S(2)}) copy-start(bf16[512,1024]{1,0:T(8,128)(2,1)S(1)} %multiply_convert_fusion.10) | copy-start | bytes 3145732
  352.1 64.9 %collective-permute-start.2 = (bf16[512,1024]{1,0:T(8,128)(2,1)}, bf16[512,1024]{1,0:T(8,128)(2,1)}, u32[]{:S(2)}, u32[]{:S(2)}) collective-permute-start(bf16[512,1024]{1,0:T(8,128)(2,1)} %multiply_convert_fusion.9), channel_id=1, source_target_pairs={{0,1},{2,3},{4,5},{6,7},{8,9},{10,11},{12,13},{14,15},{16,17},{18,... | collective-permute-start | bytes 3145736 | tf_op jit(solution)/shard_map/ppermute | solution.py:20
  383.7 36.4 %collective-permute-start.3 = (bf16[512,1024]{0,1:T(8,128)(2,1)S(1)}, bf16[512,1024]{0,1:T(8,128)(2,1)}, u32[]{:S(2)}, u32[]{:S(2)}) collective-permute-start(bf16[512,1024]{0,1:T(8,128)(2,1)S(1)} %bitcast.464), channel_id=1, source_target_pairs={{0,1},{2,3},{4,5},{6,7},{8,9},{10,11},{12,13},{14,15},{16,17},{18,... | collective-permute-start | bytes 3145736 | tf_op jit(solution)/shard_map/ppermute | solution.py:20
  464.6 37.2 %copy-start.49 = (bf16[512,1024]{1,0:T(8,128)(2,1)}, bf16[512,1024]{1,0:T(8,128)(2,1)S(1)}, u32[]{:S(2)}) copy-start(bf16[512,1024]{1,0:T(8,128)(2,1)S(1)} %multiply_convert_fusion.8) | copy-start | bytes 3145732
  509.4 113.9 %copy-start.45 = (bf16[1,512,1024]{2,1,0:T(8,128)(2,1)S(1)}, bf16[1,512,1024]{2,1,0:T(8,128)(2,1)}, u32[]{:S(2)}) copy-start(bf16[1,512,1024]{2,1,0:T(8,128)(2,1)} %param.49) | copy-start | bytes 3145732
  881.8 8.2 collective-permute-start.4
  885.8 12.8 collective-permute-start.5
  889.9 369.0 %reduce-scatter.21.cloned.1.call-start = ((), (), s32[]{:S(2)}) async-start(), calls=%async_computation.31 | async-start | bytes 2359296 | tf_op jit(solution)/shard_map/reduce_scatter | solution.py:219
  901.4 42.3 %copy-start.21 = (bf16[1,512,1024]{1,2,0:T(8,128)(2,1)}, bf16[1,512,1024]{1,2,0:T(8,128)(2,1)S(1)}, u32[]{:S(2)}) copy-start(bf16[1,512,1024]{1,2,0:T(8,128)(2,1)S(1)} %collective-permute-done.5) | copy-start | bytes 3145732
  903.8 11.9 slice-start
  903.8 17.1 slice-start.2
  904.4 20.7 %copy-start.19 = (f32[512,1024]{1,0:T(8,128)}, f32[512,1024]{1,0:T(8,128)S(1)}, u32[]{:S(2)}) copy-start(f32[512,1024]{1,0:T(8,128)S(1)} %subtract_add_fusion.1) | copy-start | bytes 6291460
  904.4 11.3 slice-start.1
  904.4 16.5 slice-start.3
  926.3 11.2 copy-start.15
  928.9 330.0 %reduce-scatter.29.cloned.1.call-start = ((), (), s32[]{:S(2)}) async-start(), calls=%async_computation.35 | async-start | bytes 2359296 | tf_op jit(solution)/shard_map/reduce_scatter | solution.py:210
  933.2 325.8 %reduce-scatter.31.cloned.1.call-start = ((), (), s32[]{:S(2)}) async-start(), calls=%async_computation.36 | async-start | bytes 2359296 | tf_op jit(solution)/shard_map/reduce_scatter | solution.py:213
  937.4 321.6 %reduce-scatter.33.cloned.1.call-start = ((), (), s32[]{:S(2)}) async-start(), calls=%async_computation.37 | async-start | bytes 2359296 | tf_op jit(solution)/shard_map/reduce_scatter | solution.py:216
  948.0 311.0 %reduce-scatter.15.cloned.1.call-start = ((), (), s32[]{:S(2)}) async-start(), calls=%async_computation.28 | async-start | bytes 2359296 | tf_op jit(solution)/shard_map/reduce_scatter | solution.py:210
  1181.7 5.9 collective-permute-start.6
  1194.8 71.2 %reduce-scatter.17.cloned.1.call-start = ((), (), s32[]{:S(2)}) async-start(), calls=%async_computation.29 | async-start | bytes 2359296 | tf_op jit(solution)/shard_map/reduce_scatter | solution.py:213
  1198.7 104.0 %reduce-scatter.19.cloned.1.call-start = ((), (), s32[]{:S(2)}) async-start(), calls=%async_computation.30 | async-start | bytes 2359296 | tf_op jit(solution)/shard_map/reduce_scatter | solution.py:216
  1200.6 4.6 collective-permute-start.7
  1212.0 156.7 %reduce-scatter.37.cloned.1.call-start = ((), (), s32[]{:S(2)}) async-start(), calls=%async_computation.39 | async-start | bytes 6488064 | tf_op jit(solution)/shard_map/reduce_scatter | solution.py:225
  1220.1 214.0 %reduce-scatter.39.cloned.1.call-start = ((), (), s32[]{:S(2)}) async-start(), calls=%async_computation.40 | async-start | bytes 6488064 | tf_op jit(solution)/shard_map/reduce_scatter | solution.py:228
  1227.1 272.5 %reduce-scatter.41.cloned.1.call-start = ((), (), s32[]{:S(2)}) async-start(), calls=%async_computation.41 | async-start | bytes 6488064 | tf_op jit(solution)/shard_map/reduce_scatter | solution.py:231
  1235.2 329.8 %reduce-scatter.23.cloned.1.call-start = ((), (), s32[]{:S(2)}) async-start(), calls=%async_computation.32 | async-start | bytes 6488064 | tf_op jit(solution)/shard_map/reduce_scatter | solution.py:225
  1243.4 387.1 %reduce-scatter.25.cloned.1.call-start = ((), (), s32[]{:S(2)}) async-start(), calls=%async_computation.33 | async-start | bytes 6488064 | tf_op jit(solution)/shard_map/reduce_scatter | solution.py:228
  1250.3 445.7 %reduce-scatter.27.cloned.1.call-start = ((), (), s32[]{:S(2)}) async-start(), calls=%async_computation.34 | async-start | bytes 6488064 | tf_op jit(solution)/shard_map/reduce_scatter | solution.py:231
  1258.8 587.9 %all-reduce.9.cloned.1.call-start = ((), (), s32[]{:S(2)}) async-start(), calls=%async_computation.42 | async-start | bytes 12845056 | tf_op jit(solution)/shard_map/psum | solution.py:237
  1710.4 28.2 %copy-start.92 = (f32[512]{0:T(512)S(1)}, f32[512]{0:T(512)}, u32[]{:S(2)}) copy-start(f32[512]{0:T(512)} %get-tuple-element.745) | copy-start | bytes 6148
  (90 other events, 321.5 us)
Sparse Core Ops, SparseCore 0:
  10.2 31.8 all-gather.18
  44.3 28.6 all-gather.22
  75.1 28.7 all-gather.20
  106.0 28.5 all-gather.24
  136.6 59.9 all-gather.26
  198.1 59.0 all-gather.28
  258.9 59.0 all-gather.30
  320.2 27.7 all-gather.32
  350.2 28.5 all-gather.36
  380.9 28.5 all-gather.34
  411.7 28.6 all-gather.38
  441.8 59.9 all-gather.40
  503.4 59.0 all-gather.42
  564.1 59.1 all-gather.44
  890.0 36.3 reduce-scatter.34
  929.0 36.2 reduce-scatter.20
  967.5 34.6 reduce-scatter.28
  1004.4 34.3 reduce-scatter.30
  1041.1 34.5 reduce-scatter.32
  1194.9 34.2 reduce-scatter.14
  1231.5 34.5 reduce-scatter.16
  1268.3 34.4 reduce-scatter.18
  1305.1 63.5 reduce-scatter.36
  1370.8 63.2 reduce-scatter.38
  1436.4 63.2 reduce-scatter.40
  1501.8 63.2 reduce-scatter.22
  1567.2 63.2 reduce-scatter.24
  1632.8 63.2 reduce-scatter.26
  1702.3 144.3 all-reduce.8
where the time goes:
time: 1880 us; the launch traced here: 1870 us
  waiting for transfers between devices  912 us (49%)
  matrix products  690 us (37%)
  other arithmetic  91.1 us (5%)
  local copies, waits for them, and re-layouts  74.9 us (4%)
  blocking collectives  64.9 us (3%)
  starting transfers between devices  20 us (1%)
    dot_general x8, matrix products, attend_back(): jnp.einsum('hqk,qhd->khd', grad_scores, query_group, preferred_element_ty...  151 us
    dot_general x8, matrix products, attend_back(): jnp.einsum('hqk,khd->qhd', grad_scores, key_group, preferred_element_type...  143 us
    reduce_scatter x2, waiting for transfers between devices, reduce_grads(): lax.psum_scatter(grad_gate.astype(jnp.bfloat16), ('shard', 'seq'), scatte...  131 us
    reduce_scatter x2, waiting for transfers between devices, reduce_grads(): lax.psum_scatter(grad_down.astype(jnp.bfloat16), ('shard', 'seq'), scatte...  131 us
    reduce_scatter x2, waiting for transfers between devices, reduce_grads(): lax.psum_scatter(grad_upward.astype(jnp.bfloat16), ('shard', 'seq'), scat...  131 us
    all_gather x2, waiting for transfers between devices, gather_ahead(): lax.all_gather(w_upward.astype(jnp.bfloat16), ('shard', 'seq'), axis=0, t...  106 us
    psum x1, waiting for transfers between devices, reduce_grads(): lax.psum(owned_rows[1].astype(jnp.bfloat16), 'rep').astype(jnp.float32)  105 us
    all_gather x2, waiting for transfers between devices, gather_ahead(): lax.all_gather(w_down.astype(jnp.bfloat16), ('shard', 'seq'), axis=0, til...  104 us
  transfers between devices with their start and end apart: 37, of which 21 were waited for; matrix products, arithmetic and copies ran while one was open for 30% of the time, Pallas kernels for 0%

commit v1 on v0

v1 whole, which is shorter than its diff:
```python
import functools
import jax
import jax.numpy as jnp
from jax import lax
from jax.experimental import pallas as pl
from jax.experimental.pallas import tpu as pltpu
from jax.sharding import PartitionSpec as P

HD = 64
BLOCK = 256
LANES = 128
FLAT = 512
eps_norm = 1e-05
rope_base = 10000.0
mask_fill = -1000000000.0


def window(block):
    return max(0, block - 2)


def swap_halves(x):
    lane = lax.broadcasted_iota(jnp.int32, x.shape, 1)
    ahead = pltpu.roll(x, LANES - HD // 2, axis=1)
    behind = pltpu.roll(x, HD // 2, axis=1)
    return jnp.where(lane % HD < HD // 2, ahead, behind)


def fill_bias(bias, docs_column, docs_row, blocks):
    at = 0
    for i in range(blocks):
        first = window(i)
        rows = (i + 1 - first) * BLOCK
        same = (
            docs_column[pl.ds(first * BLOCK, rows), 0:1]
            == docs_row[0:1, pl.ds(i * BLOCK, BLOCK)]
        )
        bias[pl.ds(at, rows), :] = jnp.where(same, 0.0, mask_fill)
        at += rows


def ahead_kernel(blocks, mixed, half_ref, tokens_ref, weight_ref, *rest):
    if mixed:
        first_ref, rest = rest[0], rest[1:]
    cos_ref, sin_ref, column_ref, row_ref, kept_ref, out_ref, lse_ref, bias = rest
    spin = half_ref[0] * (blocks // 2)

    @pl.when(pl.program_id(0) == 0)
    def _():
        fill_bias(bias, column_ref, row_ref, blocks)

    def place(b):
        return pl.multiple_of(lax.rem(b + spin, blocks) * BLOCK, BLOCK)

    for b in range(blocks):
        rows = pl.ds(b * BLOCK, BLOCK)
        cosine, sine = cos_ref[rows, :], sin_ref[rows, :]
        raw = jnp.dot(
            tokens_ref[pl.ds(place(b), BLOCK), :], weight_ref[...], preferred_element_type=jnp.float32
        )
        for part in range(2):
            one = raw[:, part * LANES : (part + 1) * LANES]
            turned = one * cosine + swap_halves(one) * sine
            kept_ref[rows, part * LANES : (part + 1) * LANES] = turned.astype(jnp.bfloat16)
        value = raw[:, 2 * LANES :]
        if mixed:
            value = 0.5 * value + 0.5 * first_ref[rows, 2 * LANES :].astype(jnp.float32)
        kept_ref[rows, 2 * LANES :] = value.astype(jnp.bfloat16)

    value_turned = kept_ref[:, 2 * LANES :].T
    head_lane = lax.broadcasted_iota(jnp.int32, (BLOCK, LANES), 1) // HD
    at = 0
    for i in range(blocks):
        first = window(i)
        count = (i + 1 - first) * BLOCK
        rows = pl.ds(i * BLOCK, BLOCK)
        query = kept_ref[rows, 0:LANES] * jnp.bfloat16(HD**-0.5)
        keys = kept_ref[pl.ds(first * BLOCK, count), LANES : 2 * LANES]
        fill = bias[pl.ds(at, count), :]
        at += count
        outs = []
        for head in range(LANES // HD):
            one = jnp.where(head_lane == head, query, jnp.bfloat16(0))
            scores = (
                lax.dot_general(keys, one, (((1,), (1,)), ((), ())), preferred_element_type=jnp.float32)
                + fill
            )
            top = jnp.max(scores, axis=0, keepdims=True)
            powers = jnp.exp(scores - top)
            total = jnp.sum(powers, axis=0, keepdims=True)
            weights = (powers * (1.0 / total)).astype(jnp.bfloat16)
            outs.append(
                jnp.dot(
                    value_turned[head * HD : (head + 1) * HD, first * BLOCK : first * BLOCK + count],
                    weights,
                    preferred_element_type=jnp.float32,
                )
            )
            lse_ref[0, head : head + 1, rows] = top + jnp.log(total)
        merged = jnp.concatenate(outs, axis=0)
        out_ref[pl.ds(place(i), BLOCK), :] = merged.T.astype(jnp.bfloat16)


def back_kernel(blocks, mixed, half_ref, kept_ref, grad_ref, lse_ref, *rest):
    if not mixed:
        extra_ref, rest = rest[0], rest[1:]
    cos_ref, sin_ref, column_ref, row_ref, out_ref, *rest = rest
    if mixed:
        passed_ref, rest = rest[0], rest[1:]
    bias, key_sum, value_sum = rest
    spin = half_ref[0] * (blocks // 2)

    @pl.when(pl.program_id(0) == 0)
    def _():
        fill_bias(bias, column_ref, row_ref, blocks)

    def place(b):
        return pl.multiple_of(lax.rem(b + spin, blocks) * BLOCK, BLOCK)

    def unrotate(x, rows):
        return x * cos_ref[rows, :] - swap_halves(x) * sin_ref[rows, :]

    keys_turned = kept_ref[:, LANES : 2 * LANES].T
    head_lane = lax.broadcasted_iota(jnp.int32, (BLOCK, LANES), 1) // HD
    at = 0
    for i in range(blocks):
        first = window(i)
        count = (i + 1 - first) * BLOCK
        rows = pl.ds(i * BLOCK, BLOCK)
        span = pl.ds(first * BLOCK, count)
        query = kept_ref[rows, 0:LANES] * jnp.bfloat16(HD**-0.5)
        grad = grad_ref[pl.ds(place(i), BLOCK), :]
        keys = kept_ref[span, LANES : 2 * LANES]
        values = kept_ref[span, 2 * LANES :]
        fill = bias[pl.ds(at, count), :]
        at += count
        outs = []
        key_add, value_add = [], []
        for head in range(LANES // HD):
            pick = head_lane == head
            one = jnp.where(pick, query, jnp.bfloat16(0))
            grad_one = jnp.where(pick, grad, jnp.bfloat16(0))
            scores = (
                lax.dot_general(keys, one, (((1,), (1,)), ((), ())), preferred_element_type=jnp.float32)
                + fill
            )
            weights = jnp.exp(scores - lse_ref[0, head : head + 1, rows])
            grad_weights = lax.dot_general(
                values, grad_one, (((1,), (1,)), ((), ())), preferred_element_type=jnp.float32
            )
            delta = jnp.sum(weights * grad_weights, axis=0, keepdims=True)
            grad_scores = (weights * (grad_weights - delta)).astype(jnp.bfloat16)
            value_add.append(
                jnp.dot(weights.astype(jnp.bfloat16), grad_one, preferred_element_type=jnp.float32)
            )
            key_add.append(jnp.dot(grad_scores, one, preferred_element_type=jnp.float32))
            outs.append(
                jnp.dot(
                    keys_turned[head * HD : (head + 1) * HD, first * BLOCK : first * BLOCK + count],
                    grad_scores,
                    preferred_element_type=jnp.float32,
                )
            )
        key_add, value_add = sum(key_add[1:], key_add[0]), sum(value_add[1:], value_add[0])
        old = count - BLOCK
        if old:
            key_sum[pl.ds(first * BLOCK, old), :] += key_add[:old]
            value_sum[pl.ds(first * BLOCK, old), :] += value_add[:old]
        key_sum[rows, :] = key_add[old:]
        value_sum[rows, :] = value_add[old:]
        grad_query = jnp.concatenate(outs, axis=0).T * HD**-0.5
        out_ref[pl.ds(place(i), BLOCK), 0:LANES] = unrotate(grad_query, rows).astype(jnp.bfloat16)
    for b in range(blocks):
        rows = pl.ds(b * BLOCK, BLOCK)
        there = pl.ds(place(b), BLOCK)
        out_ref[there, LANES : 2 * LANES] = unrotate(key_sum[rows, :], rows).astype(jnp.bfloat16)
        value_grad = value_sum[rows, :]
        if mixed:
            value_grad = 0.5 * value_grad
            passed_ref[rows, :] = value_grad
        else:
            value_grad = value_grad + extra_ref[rows, :]
        out_ref[there, 2 * LANES :] = value_grad.astype(jnp.bfloat16)


def bias_rows(blocks):
    return sum(i + 1 - window(i) for i in range(blocks)) * BLOCK


def whole(shape):
    return pl.BlockSpec(shape, lambda h, s: (0,) * len(shape))


def attend_ahead(tokens, weight, first_kept, tables, half):
    cosine, sine, column, row = tables
    length, width = tokens.shape[0], weight.shape[1]
    pairs, blocks = width // (3 * LANES), length // BLOCK
    mixed = first_kept is not None
    wide = pl.BlockSpec((length, 3 * LANES), lambda h, s: (0, h))
    slim = pl.BlockSpec((length, LANES), lambda h, s: (0, h))
    return pl.pallas_call(
        functools.partial(ahead_kernel, blocks, mixed),
        out_shape=(
            jax.ShapeDtypeStruct((length, width), jnp.bfloat16),
            jax.ShapeDtypeStruct((length, pairs * LANES), jnp.bfloat16),
            jax.ShapeDtypeStruct((pairs, LANES // HD, length), jnp.float32),
        ),
        grid_spec=pltpu.PrefetchScalarGridSpec(
            num_scalar_prefetch=1,
            grid=(pairs,),
            in_specs=[whole(tokens.shape), pl.BlockSpec((weight.shape[0], 3 * LANES), lambda h, s: (0, h))]
            + ([wide] if mixed else [])
            + [whole(cosine.shape), whole(sine.shape), whole(column.shape), whole(row.shape)],
            out_specs=(wide, slim, pl.BlockSpec((1, LANES // HD, length), lambda h, s: (h, 0, 0))),
            scratch_shapes=[pltpu.VMEM((bias_rows(blocks), BLOCK), jnp.float32)],
        ),
        compiler_params=pltpu.CompilerParams(dimension_semantics=("arbitrary",), vmem_limit_bytes=48 << 20),
        cost_estimate=pl.CostEstimate(flops=0, transcendentals=0, bytes_accessed=0),
        name="attend_ahead",
    )(half, tokens, weight, *((first_kept,) if mixed else ()), cosine, sine, column, row)


def attend_back(kept, grad, lse, extra, tables, half):
    cosine, sine, column, row = tables
    length, width = kept.shape
    pairs, blocks = width // (3 * LANES), length // BLOCK
    mixed = extra is None
    wide = pl.BlockSpec((length, 3 * LANES), lambda h, s: (0, h))
    slim = pl.BlockSpec((length, LANES), lambda h, s: (0, h))
    outs = [jax.ShapeDtypeStruct((length, width), jnp.bfloat16)]
    out_specs = [wide]
    if mixed:
        outs.append(jax.ShapeDtypeStruct((length, pairs * LANES), jnp.float32))
        out_specs.append(slim)
    result = pl.pallas_call(
        functools.partial(back_kernel, blocks, mixed),
        out_shape=tuple(outs),
        grid_spec=pltpu.PrefetchScalarGridSpec(
            num_scalar_prefetch=1,
            grid=(pairs,),
            in_specs=[wide, slim, pl.BlockSpec((1, LANES // HD, length), lambda h, s: (h, 0, 0))]
            + ([] if mixed else [slim])
            + [whole(cosine.shape), whole(sine.shape), whole(column.shape), whole(row.shape)],
            out_specs=tuple(out_specs),
            scratch_shapes=[
                pltpu.VMEM((bias_rows(blocks), BLOCK), jnp.float32),
                pltpu.VMEM((length, LANES), jnp.float32),
                pltpu.VMEM((length, LANES), jnp.float32),
            ],
        ),
        compiler_params=pltpu.CompilerParams(dimension_semantics=("arbitrary",), vmem_limit_bytes=48 << 20),
        cost_estimate=pl.CostEstimate(flops=0, transcendentals=0, bytes_accessed=0),
        name="attend_back",
    )(half, kept, grad, lse, *(() if mixed else (extra,)), cosine, sine, column, row)
    return result if mixed else (result[0], None)


def swap_cores(x):
    return lax.ppermute(x, "seq", [(0, 1), (1, 0)])


def exchange(x, mask):
    count = lax.axis_size("rep")
    return lax.ppermute(x, "rep", [(i, i ^ mask) for i in range(count)])


def unflat(read, rows, columns, write):
    at = 0
    for i in range(columns // FLAT):
        write(0, i * FLAT, read(at, rows, 0, FLAT))
        at += rows
    left = columns % FLAT
    if left:
        step = rows * left // FLAT
        for i in range(FLAT // left):
            write(i * step, columns - left, read(at, step, i * left, left))
        at += step
    return at


def join_kernel(masks, parts, cores, slot_ref, *refs):
    pieces, outs = refs[: len(masks)], refs[-sum(len(w) if k == "columns" else 1 for k, _, w in parts) :]
    for mask, piece in zip(masks, pieces):
        slot = lax.bitwise_xor(slot_ref[0], mask)
        base, at = 0, 0
        for kind, rows, widths in parts:
            columns = sum(widths)

            def read(row, count, column, width, base=base):
                return piece[0, base + row : base + row + count, column : column + width]

            def write(row, column, values, kind=kind, rows=rows, widths=widths, at=at):
                if kind == "columns":
                    one = rows // cores
                    left, which = column, 0
                    while left >= widths[which]:
                        left, which = left - widths[which], which + 1
                    took, offset = 0, column
                    while took < values.shape[1]:
                        size = min(widths[which] - left, values.shape[1] - took)
                        count = values.shape[0]
                        for done in range(0, count, min(one, count)):
                            core, inside = divmod(row + done, one)
                            size_rows = min(one, count)
                            outs[at + which][0, core, slot, inside : inside + size_rows, left : left + size] = (
                                values[done : done + size_rows, took : took + size]
                            )
                        took, left, which = took + size, 0, which + 1
                else:
                    there = pl.ds(pl.multiple_of(slot * columns, columns) + column, values.shape[1])
                    outs[at][0, row : row + values.shape[0], there] = values

            base += unflat(read, rows, columns, write)
            at += len(widths) if kind == "columns" else 1


def join(pieces, masks, slot, sizes, parts, start=None, after=()):
    groups, cores = sizes
    count, rows = len(masks), pieces[0].shape[0] // groups
    read = rows if start is None else sum(h * sum(w) for _, h, w in parts) // FLAT
    at = 0 if start is None else start // read
    shapes = []
    for kind, height, widths in parts:
        if kind == "columns":
            shapes += [(groups, cores, count, height // cores, w) for w in widths]
        else:
            shapes.append((groups, height, count * widths[0]))
    outs = pl.pallas_call(
        functools.partial(join_kernel, masks, parts, cores),
        out_shape=[jax.ShapeDtypeStruct(s, jnp.bfloat16) for s in shapes],
        grid_spec=pltpu.PrefetchScalarGridSpec(
            num_scalar_prefetch=1,
            grid=(groups,),
            in_specs=[pl.BlockSpec((1, read, FLAT), lambda g, s: (g, at, 0))] * count
            + [pl.BlockSpec(memory_space=pl.ANY)] * len(after),
            out_specs=[
                pl.BlockSpec((1, *s[1:]), lambda g, t, n=len(s): (g,) + (0,) * (n - 1)) for s in shapes
            ],
        ),
        cost_estimate=pl.CostEstimate(flops=0, transcendentals=0, bytes_accessed=0),
        name="join",
    )(slot, *[p.reshape(groups, rows, FLAT) for p in pieces], *after)
    return [o.reshape(-1, o.shape[-1]) for o in outs]


def core_columns(rows, sizes, core):
    shards, cores = sizes
    width = rows.shape[1] // (shards * cores)
    even, odd = (
        jnp.concatenate(
            [rows[:, (s * cores + c) * width : (s * cores + c + 1) * width] for s in range(shards)],
            axis=1,
        )
        for c in range(cores)
    )
    return jnp.where(core == 0, even, odd), jnp.where(core == 0, odd, even)


def head_major(parts):
    pairs = parts[0].shape[1] // LANES
    return jnp.concatenate(
        [p[:, i * LANES : (i + 1) * LANES] for i in range(pairs) for p in parts], axis=1
    )


def head_minor(joined):
    pairs = joined.shape[1] // (3 * LANES)
    return [
        jnp.concatenate(
            [
                joined[:, (3 * i + j) * LANES : (3 * i + j + 1) * LANES]
                for i in range(pairs)
            ],
            axis=1,
        )
        for j in range(3)
    ]


def chip_rows(rows_of, sizes, core):
    mine, theirs = rows_of
    other = swap_cores(theirs)
    return jnp.concatenate(
        [jnp.where(core == 0, mine, other), jnp.where(core == 0, other, mine)], axis=0
    )


def gather_shard(x):
    return lax.all_gather(x, "shard", axis=0, tiled=True)


def column_parts(weights, sizes, core, interleave):
    mine, theirs = zip(*[core_columns(w.astype(jnp.bfloat16), sizes, core) for w in weights])
    if interleave:
        return head_major(mine), head_major(theirs)
    return jnp.concatenate(mine, axis=1), jnp.concatenate(theirs, axis=1)


def gather_plain(masters, sizes, core):
    _, w_query, w_key, w_value, w_proj, _, w_gate, w_upward, w_down = masters
    w_qkv = gather_shard(chip_rows(column_parts((w_query, w_key, w_value), sizes, core, True), sizes, core))
    w_wide = gather_shard(chip_rows(column_parts((w_gate, w_upward), sizes, core, False), sizes, core))
    w_proj, w_down = (gather_shard(w.astype(jnp.bfloat16)) for w in (w_proj, w_down))
    width = w_wide.shape[1] // 2
    return w_qkv, w_proj, w_wide[:, :width], w_wide[:, width:], w_down


def call(kernel, outs, grid, in_specs, out_specs, name, scratch=(), scalars=1):
    return pl.pallas_call(
        kernel,
        out_shape=outs,
        grid_spec=pltpu.PrefetchScalarGridSpec(
            num_scalar_prefetch=scalars,
            grid=grid,
            in_specs=in_specs,
            out_specs=out_specs,
            scratch_shapes=scratch,
        ),
        compiler_params=pltpu.CompilerParams(
            dimension_semantics=("arbitrary",) * len(grid), vmem_limit_bytes=56 << 20
        ),
        cost_estimate=pl.CostEstimate(flops=0, transcendentals=0, bytes_accessed=0),
        name=name,
    )


def fixed(shape):
    return pl.BlockSpec(shape, lambda *ids: (0,) * len(shape))


def low(values):
    return values.astype(jnp.bfloat16)


def near_split_kernel(shards, place_ref, *refs):
    weights, gains, (mine, theirs) = refs[:3], refs[3:-2], refs[-2:]
    core = place_ref[1]
    for out, which in ((mine, core), (theirs, 1 - core)):
        for s in range(shards):
            there = pl.ds(pl.multiple_of((2 * s + which) * LANES, LANES), LANES)
            for j, weight in enumerate(weights):
                out[:, (3 * s + j) * LANES : (3 * s + j + 1) * LANES] = low(weight[:, there])
        if gains:
            rows = jnp.concatenate([g[...] for g in gains] + [jnp.zeros((16 - len(gains), LANES), jnp.float32)], axis=0)
            out[0:16, 3 * shards * LANES :] = low(rows)


def near_merge_kernel(place_ref, mine, theirs, proj, out):
    core = place_ref[1]
    rows = mine.shape[0]
    for j in range(3):
        for part, which in ((mine, core), (theirs, 1 - core)):
            there = pl.ds(pl.multiple_of((2 * j + which) * rows, rows), rows)
            out[there, :] = part[:, j * FLAT : (j + 1) * FLAT]
    half = proj.shape[0] // 2
    start = 6 * rows
    out[start : start + half, 0 : FLAT // 2] = low(proj[0:half, :])
    out[start : start + half, FLAT // 2 :] = low(proj[half:, :])
    if out.shape[0] > start + half:
        out[start + half :, :] = jnp.zeros((16, FLAT), jnp.bfloat16)
        for part, which in ((mine, core), (theirs, 1 - core)):
            there = pl.ds(pl.multiple_of(which * LANES, LANES), LANES)
            out[start + half :, there] = part[0:16, 3 * FLAT : 3 * FLAT + LANES]


def far_split_kernel(shards, place_ref, gate, upward, mine, theirs):
    core = place_ref[1]
    width = gate.shape[1] // (2 * shards)
    for at, weight in enumerate((gate, upward)):
        even, odd = (
            low(jnp.concatenate([weight[:, (2 * s + c) * width : (2 * s + c + 1) * width] for s in range(shards)], axis=1))
            for c in range(2)
        )
        there = slice(at * shards * width, (at + 1) * shards * width)
        mine[:, there] = jnp.where(core == 0, even, odd)
        theirs[:, there] = jnp.where(core == 0, odd, even)


def far_merge_kernel(place_ref, mine, theirs, down, out):
    core = place_ref[1]
    rows, columns = mine.shape
    blocks = columns // FLAT
    for part, which in ((mine, core), (theirs, 1 - core)):
        for j in range(blocks):
            there = pl.ds(pl.multiple_of((2 * j + which) * rows, rows), rows)
            out[there, :] = part[:, j * FLAT : (j + 1) * FLAT]
        there = pl.ds(pl.multiple_of(which * (FLAT // 2), FLAT // 2), FLAT // 2)
        out[2 * blocks * rows : (2 * blocks + 1) * rows, there] = part[:, blocks * FLAT :]
    half, start = down.shape[0] // 2, (2 * blocks + 1) * rows
    out[start:, 0 : FLAT // 2] = low(down[0:half, :])
    out[start:, FLAT // 2 :] = low(down[half:, :])


def shape_of(*shape, dtype=jnp.bfloat16):
    return jax.ShapeDtypeStruct(shape, dtype)


def quarter_of_rows(weight):
    return pl.BlockSpec((weight.shape[0] // 4, weight.shape[1]), lambda i, s: (s[0], 0))


def quarter_of_columns(weight):
    return pl.BlockSpec((weight.shape[0], weight.shape[1] // 4), lambda i, s: (0, s[0]))


def gather_near(weights, proj, gains, shards, place):
    rows = weights[0].shape[0] // 4
    width = 3 * shards * LANES + (LANES if gains else 0)
    gains = [g.reshape(1, LANES) for g in gains]
    mine, theirs = call(
        functools.partial(near_split_kernel, shards),
        [shape_of(rows, width)] * 2,
        (1,),
        [quarter_of_rows(w) for w in weights] + [fixed((1, LANES))] * len(gains),
        [fixed((rows, width))] * 2,
        "near_split",
    )(place, *weights, *gains)
    total = 6 * rows + proj.shape[0] // 2 + (16 if gains else 0)
    merged = call(
        near_merge_kernel,
        shape_of(total, FLAT),
        (1,),
        [fixed((rows, width))] * 2 + [quarter_of_columns(proj)],
        fixed((total, FLAT)),
        "near_merge",
    )(place, mine, swap_cores(theirs), proj)
    return gather_shard(merged)


def gather_far(weights, down, shards, place):
    rows, width = weights[0].shape[0] // 4, weights[0].shape[1]
    mine, theirs = call(
        functools.partial(far_split_kernel, shards),
        [shape_of(rows, width)] * 2,
        (1,),
        [quarter_of_rows(w) for w in weights],
        [fixed((rows, width))] * 2,
        "far_split",
    )(place, *weights)
    total = rows * width // (FLAT // 2) + down.shape[0] // 2
    merged = call(
        far_merge_kernel,
        shape_of(total, FLAT),
        (1,),
        [fixed((rows, width))] * 2 + [quarter_of_columns(down)],
        fixed((total, FLAT)),
        "far_merge",
    )(place, mine, swap_cores(theirs), down)
    return gather_shard(merged)


def gated_kernel(none_ref, tokens, gate, upward, gate_out, upward_out, inner_out):
    one = jnp.dot(tokens[...], gate[...], preferred_element_type=jnp.float32)
    two = jnp.dot(tokens[...], upward[...], preferred_element_type=jnp.float32)
    inner_out[...] = low(one * jax.nn.sigmoid(one) * two)
    gate_out[...] = low(one)
    upward_out[...] = low(two)


def gated(tokens, gate, upward, place):
    length, width, tile = tokens.shape[0], gate.shape[1], 256
    rows = pl.BlockSpec((tile, width), lambda i, s: (i, 0))
    return call(
        gated_kernel,
        [shape_of(length, width)] * 3,
        (length // tile,),
        [pl.BlockSpec((tile, tokens.shape[1]), lambda i, s: (i, 0)), fixed(gate.shape), fixed(upward.shape)],
        [rows] * 3,
        "gated",
    )(place, tokens, gate, upward)


def bit_of(rep, mask):
    return (rep // mask) % 2


def halve_rows(grad, groups, bit, mask):
    shaped = grad.reshape(groups, 2, -1, grad.shape[1])
    sent = lax.dynamic_index_in_dim(shaped, 1 - bit, 1, keepdims=False)
    kept = lax.dynamic_index_in_dim(shaped, bit, 1, keepdims=False)
    got = exchange(sent, mask)
    total = kept.astype(jnp.float32) + got.astype(jnp.float32)
    return total.astype(jnp.bfloat16).reshape(-1, grad.shape[1])


def halve_columns(grad, bit, mask):
    width = grad.shape[1] // 2
    sent = lax.dynamic_slice_in_dim(grad, (1 - bit) * width, width, 1)
    kept = lax.dynamic_slice_in_dim(grad, bit * width, width, 1)
    got = exchange(sent, mask)
    return (kept.astype(jnp.float32) + got.astype(jnp.float32)).astype(jnp.bfloat16)


def scatter_shard(x):
    return lax.psum_scatter(x, "shard", scatter_dimension=0, tiled=True)


def columns_back(grad, sizes, rep, plan):
    if plan is None:
        return lax.psum(scatter_shard(grad), "rep")
    first, second = plan
    groups = sizes[0] * sizes[1]
    half = halve_rows(grad, groups, bit_of(rep, first), first)
    return scatter_shard(halve_rows(half, groups, bit_of(rep, second), second))


def rows_back(grad, rep, plan):
    if plan is None:
        return lax.psum(scatter_shard(grad), "rep")
    first, second = plan
    half = halve_columns(grad, bit_of(rep, first), first)
    return scatter_shard(halve_columns(half, bit_of(rep, second), second))


def in_order(pieces, slot_high, slot_low):
    p0, p1, p2, p3 = pieces
    low = slot_low == 1
    q0, q1 = jnp.where(low, p1, p0), jnp.where(low, p0, p1)
    q2, q3 = jnp.where(low, p3, p2), jnp.where(low, p2, p3)
    high = slot_high == 1
    return [
        jnp.where(high, q2, q0),
        jnp.where(high, q3, q1),
        jnp.where(high, q0, q2),
        jnp.where(high, q1, q3),
    ]


def share_slots(piece, plan):
    first, second = plan
    return [piece, exchange(piece, second), exchange(piece, first), exchange(piece, first ^ second)]


def spread_columns(even, odd, sizes):
    shards, cores = sizes
    width = even.shape[1] // shards
    return jnp.concatenate(
        [p[:, s * width : (s + 1) * width] for s in range(shards) for p in (even, odd)], axis=1
    )


def finish_columns(reduced, sizes, core, rep, plan):
    rows = reduced.shape[0] // 2
    shaped = reduced.reshape(2, rows, reduced.shape[1])
    mine = lax.dynamic_index_in_dim(shaped, core, 0, keepdims=False)
    other = swap_cores(lax.dynamic_index_in_dim(shaped, 1 - core, 0, keepdims=False))
    even, odd = jnp.where(core == 0, mine, other), jnp.where(core == 0, other, mine)
    if plan is None:
        return even.astype(jnp.float32), odd.astype(jnp.float32)
    both = jnp.concatenate([even, odd], axis=1)
    first, second = plan
    ordered = in_order(share_slots(both, plan), bit_of(rep, first), bit_of(rep, second))
    full = jnp.concatenate(ordered, axis=0).astype(jnp.float32)
    return full[:, : even.shape[1]], full[:, even.shape[1] :]


def finish_rows(reduced, rep, plan):
    if plan is None:
        return reduced.astype(jnp.float32)
    first, second = plan
    ordered = in_order(share_slots(reduced, plan), bit_of(rep, first), bit_of(rep, second))
    return jnp.concatenate(ordered, axis=1).astype(jnp.float32)


def norm_ahead(values, gain_row):
    factor = lax.rsqrt(jnp.mean(values * values, axis=-1, keepdims=True) + eps_norm)
    return ((values * factor * gain_row).astype(jnp.bfloat16), factor)


def norm_back(values, factor, gain_row, upstream):
    scaled = upstream * gain_row
    gain_grad = jnp.sum(upstream * values * factor, axis=0)
    inner_mean = jnp.mean(scaled * values, axis=-1, keepdims=True)
    return (factor * scaled - values * (factor * factor * factor) * inner_mean, gain_grad)


def both_halves(mine):
    return jnp.concatenate([mine, swap_cores(mine)], axis=0)


def dot(a, b):
    return jnp.dot(a, b, preferred_element_type=jnp.float32)


def dot_nt(a, b):
    return lax.dot_general(a, b, (((1,), (1,)), ((), ())), preferred_element_type=jnp.float32)


def dot_tn(a, b):
    return lax.dot_general(a, b, (((0,), (0,)), ((), ())), preferred_element_type=jnp.float32)


def sum_halves(product, rows):
    theirs = swap_cores(product(slice(rows, 2 * rows)).astype(jnp.bfloat16))
    return product(slice(0, rows)) + theirs.astype(jnp.float32)


def tie(value, *others):
    return lax.optimization_barrier((value, *others))[0]


def layer_ahead(flat, gains, weights, first_kept, tables, place):
    gain_attn, gain_ffn = gains
    rows = flat.shape[0]
    normed, factor_attn = norm_ahead(flat, gain_attn)
    normed_all = both_halves(normed)
    w_qkv, w_proj = weights.near()
    kept, attended, lse = attend_ahead(normed_all, w_qkv, first_kept, tables, place[1:])
    attended = weights.after_attention(attended)
    theirs = dot(attended[rows:], w_proj).astype(jnp.bfloat16)
    middle = flat + dot(attended[:rows], w_proj) + swap_cores(theirs).astype(jnp.float32)
    normed_ffn, factor_ffn = norm_ahead(middle, gain_ffn)
    ffn_all = both_halves(normed_ffn)
    w_gate, w_upward = weights.wide()
    ffn_all = weights.before_wide(ffn_all)
    gate_pre, upward_pre, inner = gated(ffn_all, w_gate, w_upward, place)
    inner = weights.after_wide(inner)
    (w_down,) = weights.down(inner)
    theirs = dot(inner[rows:], w_down).astype(jnp.bfloat16)
    result = middle + dot(inner[:rows], w_down) + swap_cores(theirs).astype(jnp.float32)
    result = weights.at_end(result)
    saved = (
        flat,
        factor_attn,
        normed_all,
        kept,
        lse,
        attended,
        middle,
        factor_ffn,
        ffn_all,
        gate_pre,
        upward_pre,
        inner,
    )
    return result, kept, saved, (w_qkv, w_proj, w_gate, w_upward, w_down)


class Plain:
    def __init__(self, weights):
        self.weights = weights

    def near(self):
        return self.weights[:2]

    def wide(self):
        return self.weights[2:4]

    def down(self, inner):
        return self.weights[4:]

    def same(self, value):
        return value

    after_attention = before_wide = after_wide = at_end = same


class Quarters:
    def __init__(self, place, piece, first, second, before_first=(), before_second=()):
        self.slot, self.starts = place[:1], {}
        self.masks = (0, first, second, first ^ second)
        self.one = exchange(tie(piece, *before_first), first)
        self.two = exchange(tie(piece, *before_second), second)
        self.three = exchange(tie(self.one, *before_second), second)
        self.pieces = [piece, self.one, self.two, self.three]


class Tuned(Plain):
    def __init__(self, shapes, sizes, place):
        (qkv_rows, qkv_width), proj_rows, (wide_rows, wide_width), down_rows = shapes
        self.cut, self.shards = wide_rows * wide_width // FLAT, sizes[0]
        self.near_parts = (("columns", qkv_rows, (qkv_width,)), ("rows", proj_rows, (FLAT // 2,)))
        self.wide_parts = (("columns", wide_rows, (wide_width // 2,) * 2),)
        self.down_parts = (("rows", down_rows, (FLAT // 2,)),)
        self.join = lambda q, parts, after=(): join(
            q.pieces, q.masks, q.slot, sizes, parts, q.starts.get(parts[0][0]), after
        )

    def split(self, far):
        far = far.reshape(self.shards, -1, FLAT)
        return (f.reshape(-1, FLAT) for f in (far[:, : self.cut], far[:, self.cut :]))

    def near(self):
        return self.join(self.near_way, self.near_parts)

    def wide(self):
        return self.join(self.wide_way, self.wide_parts)

    def down(self, inner):
        return self.join(self.down_way, self.down_parts, (inner,))


class Halves:
    def __init__(self, place, pieces, before):
        self.slot, self.starts = 2 * half_of(place[:1]), {}
        self.masks = (0, 1, 2, 3)
        self.one, self.two = exchange(tie(pieces[0], *before), 1), exchange(pieces[1], 2)
        self.pieces = [*pieces, self.one, self.two]


def half_of(rep):
    return lax.bitwise_xor(rep, rep // 2) % 2


def first_ways(layer, near, far, place):
    near = Quarters(place, near, 1, 2)
    wide, down = layer.split(tie(far, near.one, near.two, near.three))
    return near, Quarters(place, wide, 2, 1), Quarters(place, down, 1, 2)


def second_ways(layer, near, far, wide_one, down_one, place):
    near = Quarters(place, near, 2, 1, (down_one.two,), (wide_one.one,))
    wide, down = zip(*[layer.split(f) for f in far])
    wide = Halves(place, wide, (near.two, near.three))
    return near, wide, Halves(place, down, (near.two, near.three))


def layer_back(upstream, gains, weights, saved, extra, tables, half, send):
    gain_attn, gain_ffn = gains
    w_qkv, w_proj, w_gate, w_upward, w_down = weights
    (
        flat,
        factor_attn,
        normed_all,
        kept,
        lse,
        attended,
        middle,
        factor_ffn,
        ffn_all,
        gate_pre,
        upward_pre,
        inner,
    ) = saved
    rows = flat.shape[0]
    grad_down_all = both_halves(upstream.astype(jnp.bfloat16))
    grad_inner = dot_nt(grad_down_all, w_down)
    gate_pre, upward_pre = gate_pre.astype(jnp.float32), upward_pre.astype(jnp.float32)
    sigmoid_gate = jax.nn.sigmoid(gate_pre)
    grad_gate = (
        grad_inner * upward_pre * sigmoid_gate * (1.0 + gate_pre * (1.0 - sigmoid_gate))
    ).astype(jnp.bfloat16)
    grad_upward = (grad_inner * gate_pre * sigmoid_gate).astype(jnp.bfloat16)
    sent_down = send.down(dot_tn(inner, grad_down_all).astype(jnp.bfloat16))
    sent_gate = send.gate(
        jnp.concatenate(
            [
                dot_tn(ffn_all, grad_gate).astype(jnp.bfloat16),
                dot_tn(ffn_all, grad_upward).astype(jnp.bfloat16),
            ],
            axis=1,
        )
    )
    grad_normed_ffn = sum_halves(
        lambda part: dot_nt(grad_gate[part], w_gate) + dot_nt(grad_upward[part], w_upward), rows
    )
    grad_part_ffn, grad_gain_ffn = norm_back(middle, factor_ffn, gain_ffn, grad_normed_ffn)
    grad_middle = upstream + grad_part_ffn
    grad_branch_all = both_halves(grad_middle.astype(jnp.bfloat16))
    grad_attended = dot_nt(grad_branch_all, w_proj).astype(jnp.bfloat16)
    sent_proj = send.proj(dot_tn(attended, grad_branch_all).astype(jnp.bfloat16))
    grad_qkv, passed = attend_back(kept, grad_attended, lse, extra, tables, half)
    sent_qkv = send.qkv(dot_tn(normed_all, grad_qkv).astype(jnp.bfloat16))
    grad_normed = sum_halves(lambda part: dot_nt(grad_qkv[part], w_qkv), rows)
    grad_part_attn, grad_gain_attn = norm_back(flat, factor_attn, gain_attn, grad_normed)
    grad_flat = grad_middle + grad_part_attn
    grads = send.finish(sent_qkv, sent_proj, sent_gate, sent_down)
    return grad_flat, (grad_gain_attn, grad_gain_ffn), grads, passed


class Sender:
    def __init__(self, sizes, core, rep, tuned):
        self.sizes, self.core, self.rep = sizes, core, rep
        self.near = (1, 2) if tuned else None
        self.far = (2, 1) if tuned else None

    def down(self, grad):
        return rows_back(grad, self.rep, self.near)

    def proj(self, grad):
        return rows_back(grad, self.rep, self.near)

    def gate(self, grad):
        return columns_back(grad, self.sizes, self.rep, self.far)

    def qkv(self, grad):
        return columns_back(grad, self.sizes, self.rep, self.near)

    def finish(self, qkv, proj, gate, down):
        q_even, q_odd = finish_columns(qkv, self.sizes, self.core, self.rep, self.near)
        g_even, g_odd = finish_columns(gate, self.sizes, self.core, self.rep, self.far)
        grad_qkv = [
            spread_columns(e, o, self.sizes) for e, o in zip(head_minor(q_even), head_minor(q_odd))
        ]
        width = g_even.shape[1] // 2
        grad_gate = spread_columns(g_even[:, :width], g_odd[:, :width], self.sizes)
        grad_upward = spread_columns(g_even[:, width:], g_odd[:, width:], self.sizes)
        joined = finish_rows(jnp.concatenate([proj, down], axis=0), self.rep, self.near)
        return (*grad_qkv, joined[: proj.shape[0]], grad_gate, grad_upward, joined[proj.shape[0] :])


def shards(inputs, documents, *rest):
    masters_one, masters_two, cotangent = rest[:9], rest[9:18], rest[18]
    batch, rows, features = inputs.shape
    reps, sizes = lax.axis_size("rep"), (lax.axis_size("shard"), lax.axis_size("seq"))
    assert batch == 1 and sizes[1] == 2
    core, rep = lax.axis_index("seq"), lax.axis_index("rep")
    rows_owned = masters_one[1].shape[0]
    tuned = reps == 4 and rows_owned == LANES
    length = sizes[1] * rows
    half = core.astype(jnp.int32).reshape(1)
    frequencies = rope_base ** (-(jnp.arange(HD // 2, dtype=jnp.float32) * 2.0 / HD))
    angles = jnp.arange(length, dtype=jnp.float32)[:, None] * frequencies[None, :]
    cosine, sine = jnp.cos(angles), jnp.sin(angles)
    tables = (
        jnp.tile(cosine, (1, LANES * 2 // HD)),
        jnp.tile(jnp.concatenate([-sine, sine], axis=1), (1, LANES // HD)),
        documents.reshape(length, 1),
        documents.reshape(1, length),
    )
    gain_rows = jnp.stack([masters_one[0], masters_one[5], masters_two[0], masters_two[5]]).astype(
        jnp.bfloat16
    )
    flat = inputs.reshape(rows, features).astype(jnp.float32)
    place = jnp.stack([rep, core]).astype(jnp.int32)
    if tuned:
        gain_list = [masters_one[0], masters_one[5], masters_two[0], masters_two[5]]
        near_one = gather_near(masters_one[1:4], masters_one[4], gain_list, sizes[0], place)
        far_one = gather_far(masters_one[6:8], masters_one[8], sizes[0], place)
        near_two = gather_near(masters_two[1:4], masters_two[4], [], sizes[0], place)
        quarter_of = 2 * half_of(rep)
        far_two = [
            gather_far(
                masters_two[6:8], masters_two[8], sizes[0], jnp.stack([quarter_of + u, core]).astype(jnp.int32)
            )
            for u in range(2)
        ]
        gains = near_one.reshape(sizes[0], -1, FLAT)[:, -16:-12, : 2 * LANES]
        gains = gains.transpose(1, 0, 2).reshape(4, features).astype(jnp.float32)
        quarter, columns = rows_owned // 4 * 2, sizes[0] * LANES
        shapes = (
            (quarter, 3 * columns),
            rows_owned,
            (quarter, 2 * sizes[0] * masters_one[8].shape[0]),
            masters_one[8].shape[0],
        )
        first, second = Tuned(shapes, sizes, place), Tuned(shapes, sizes, place)
        near, wide, down = ways_one = first_ways(first, near_one, far_one, place)
        first.near_way, first.wide_way, first.down_way = ways_one
        ways = second_ways(second, near_two, far_two, wide, down, place)
        second.near_way, second.wide_way, second.down_way = ways
        first.after_attention = lambda value: tie(value, near_two, wide.one, wide.two, down.one, down.two)
        first.before_wide = lambda value: tie(value, far_two[0])
        first.after_wide = lambda value: tie(value, far_two[1], ways[0].one, ways[0].two)
        first.at_end = lambda value: tie(value, ways[0].three)
        second.after_attention = lambda value: tie(value, ways[1].one, ways[1].two)
    else:
        gains = lax.all_gather(gain_rows, ("shard", "seq"), axis=1, tiled=True).astype(jnp.float32)
        first, second = (Plain(gather_plain(m, sizes, core)) for m in (masters_one, masters_two))
    middle_one, first_kept, saved_one, weights_one = layer_ahead(
        flat, (gains[0:1], gains[1:2]), first, None, tables, place
    )
    final, _, saved_two, weights_two = layer_ahead(
        middle_one, (gains[2:3], gains[3:4]), second, first_kept, tables, place
    )
    outputs = final.astype(jnp.bfloat16).reshape(batch, rows, features)
    upstream = cotangent.reshape(rows, features).astype(jnp.float32)
    send = Sender(sizes, core, rep, tuned)
    grad_middle, gains_two, grads_two, extra = layer_back(
        upstream, (gains[2:3], gains[3:4]), weights_two, saved_two, None, tables, half, send
    )
    grad_flat, gains_one, grads_one, _ = layer_back(
        grad_middle, (gains[0:1], gains[1:2]), weights_one, saved_one, extra, tables, half, send
    )
    grad_input = grad_flat.reshape(batch, rows, features)
    gain_total = lax.psum(jnp.stack([*gains_one, *gains_two]), ("rep", "shard", "seq"))
    block = features // (sizes[0] * sizes[1])
    mine = lax.axis_index("shard") * sizes[1] + core
    own = lax.dynamic_slice_in_dim(gain_total, mine * block, block, 1)

    def ordered(gain_attn, gain_ffn, grads):
        query, key, value, proj, gate, upward, down = grads
        return (gain_attn, query, key, value, proj, gain_ffn, gate, upward, down)

    return (
        (outputs, grad_input)
        + ordered(own[0], own[1], grads_one)
        + ordered(own[2], own[3], grads_two)
    )


def solution(mesh):
    tokens = P(("rep", "shard"), "seq", None)
    vector, matrix = P(("shard", "seq")), P(("shard", "seq"), None)
    layer = (vector, matrix, matrix, matrix, matrix, vector, matrix, matrix, matrix)
    return jax.shard_map(
        shards,
        mesh=mesh,
        in_specs=(tokens, P(("rep", "shard"), None), *layer, *layer, tokens),
        out_specs=(tokens, tokens, *layer, *layer),
        check_vma=False,
    )
```

time: 1880 us -> 916 us (0.49)
  waiting for transfers between devices: 912 us -> 317 us
  matrix products: 690 us -> 130 us
  Pallas kernels: 0 us -> 174 us
  starting transfers between devices: 20 us -> 64.2 us
    dot_general x98 -> x34, matrix products: 690 us -> 130 us  [the longest x16 63 us: dot_nt(): lax.dot_general(a, b, (((1,), (1,)), ((), ())), preferred_element_type=jn...]
    reduce_scatter x14 -> x8, waiting for transfers between devices: 437 us -> 39.3 us  [scatter_shard(): return lax.psum_scatter(x, 'shard', scatter_dimension=0, tiled=True)]
    all_gather x14 -> x5, waiting for transfers between devices: 363 us -> 31.1 us  [gather_shard(): return lax.all_gather(x, 'shard', axis=0, tiled=True)]
    ppermute x8 -> x75, waiting for transfers between devices: 7.43 us -> 247 us  [the longest x50 237 us: exchange(): return lax.ppermute(x, 'rep', [(i, i ^ mask) for i in range(count)])]
    pallas_call x0 -> x22, Pallas kernels: none -> 174 us  [the longest x2 49.8 us: attend_ahead(): pl.pallas_call(functools.partial(ahead_kernel, blocks, mixed), out_shape=...]
    psum x1 -> x0, waiting for transfers between devices: 105 us -> none  [reduce_grads(): lax.psum(owned_rows[1].astype(jnp.bfloat16), 'rep').astype(jnp.float32)]
    ppermute x8 -> x75, starting transfers between devices: 18.6 us -> 62.9 us  [the longest x50 58.6 us: exchange(): return lax.ppermute(x, 'rep', [(i, i ^ mask) for i in range(count)])]
    psum x1, blocking collectives: 9.94 us -> 51.6 us  [shards(): lax.psum(jnp.stack([*gains_one, *gains_two]), ('rep', 'shard', 'seq'))]
  transfers between devices with their start and end apart: 37 -> 88, of which waited for: 21 -> 32; matrix products, arithmetic and copies ran while one was open for 30% -> 28% of each run, Pallas kernels for 0% -> 19%
where the time goes in v1:
time: 916 us; the launch traced here: 909 us
  waiting for transfers between devices  317 us (35%)
  Pallas kernels  174 us (19%)
  matrix products  130 us (14%)
  other arithmetic  82.5 us (9%)
  local copies, waits for them, and re-layouts  73.7 us (8%)
  starting transfers between devices  64.2 us (7%)
  blocking collectives  51.6 us (6%)
  between operations  15.8 us (2%)
    ppermute x50, waiting for transfers between devices, exchange(): return lax.ppermute(x, 'rep', [(i, i ^ mask) for i in range(count)])  237 us
    dot_general x16, matrix products, dot_nt(): lax.dot_general(a, b, (((1,), (1,)), ((), ())), preferred_element_type=jn...  63 us
    ppermute x50, starting transfers between devices, exchange(): return lax.ppermute(x, 'rep', [(i, i ^ mask) for i in range(count)])  58.6 us
    psum x1, blocking collectives, shards(): lax.psum(jnp.stack([*gains_one, *gains_two]), ('rep', 'shard', 'seq'))  51.6 us
    pallas_call x2, Pallas kernels, attend_ahead(): pl.pallas_call(functools.partial(ahead_kernel, blocks, mixed), out_shape=...  49.8 us
    dot_general x10, matrix products, dot_tn(): lax.dot_general(a, b, (((0,), (0,)), ((), ())), preferred_element_type=jn...  46.9 us
    pallas_call x2, Pallas kernels, attend_back(): pl.pallas_call(functools.partial(back_kernel, blocks, mixed), out_shape=t...  44.3 us
    reduce_scatter x8, waiting for transfers between devices, scatter_shard(): return lax.psum_scatter(x, 'shard', scatter_dimension=0, tiled=True)  39.3 us
  transfers between devices with their start and end apart: 88, of which 32 were waited for; matrix products, arithmetic and copies ran while one was open for 28% of the time, Pallas kernels for 19%

profile of v1, /device:TPU:0, one launch (start us, length us, event | category | flops | bytes accessed | tf_op | source)
XLA Modules:
  0.0 909.4 jit_solution(18119349534264441137)
XLA Ops:
  29.8 17.0 %all-gather.6.cloned.1.call-done = bf16[1088,512]{1,0:T(8,128)(2,1)} async-done(((bf16[272,512]{1,0:T(8,128)(2,1)}), bf16[1088,512]{1,0:T(8,128)(2,1)}) %all-gather.6.cloned.1.call-update) | async-done | bytes 1114128 | tf_op jit(solution)/shard_map/all_gather | solution.py:389
  58.1 14.9 %collective-permute-done.2 = bf16[1088,512]{1,0:T(8,128)(2,1)S(1)} collective-permute-done((bf16[1088,512]{1,0:T(8,128)(2,1)}, bf16[1088,512]{1,0:T(8,128)(2,1)S(1)}, u32[]{:S(2)}, u32[]{:S(2)}) %collective-permute-start.2) | collective-permute-done | bytes 1114144 | tf_op jit(solution)/shard_map/ppermute | solution.py:264
  75.5 8.7 collective-permute-done.3
  84.2 11.5 %all-gather.10.cloned.1.call-done = bf16[2112,512]{1,0:T(8,128)(2,1)} async-done(((bf16[528,512]{1,0:T(8,128)(2,1)}), bf16[2112,512]{1,0:T(8,128)(2,1)}) %all-gather.10.cloned.1.call-update) | async-done | bytes 2162704 | tf_op jit(solution)/shard_map/all_gather | solution.py:389
  95.6 11.6 %collective-permute-done.4 = bf16[1088,512]{1,0:T(8,128)(2,1)} collective-permute-done((bf16[1088,512]{1,0:T(8,128)(2,1)S(1)}, bf16[1088,512]{1,0:T(8,128)(2,1)}, u32[]{:S(2)}, u32[]{:S(2)}) %collective-permute-start.4) | collective-permute-done | bytes 1114144 | tf_op jit(solution)/shard_map/ppermute | solution.py:264
  128.1 4.7 join.6
  134.5 24.8 %attend_ahead.2 = (bf16[1024,1536]{1,0:T(8,128)(2,1)}, bf16[1024,512]{1,0:T(8,128)(2,1)S(1)}, f32[4,2,1024]{2,1,0:T(2,128)S(1)}) custom-call(s32[1]{0:T(128)} %bitcast.1.half_ref, bf16[1024,1024]{1,0:T(8,128)(2,1)S(1)} %copy-done, bf16[1024,1536]{1,0:T(8,128)(2,1)} %bitcast.210, f32[1024,128]{1,0:T(8,128)S(1)} %copy.41.rest_0_.rest_1_, ...), custom_call_target="tpu_custom_call" | custom-call | tf_op jit(solution)/shard_map/attend_ahead/pallas_call | solution.py:201
  169.6 18.5 %collective-permute-done.16 = bf16[1024,512]{1,0:T(8,128)(2,1)} collective-permute-done((bf16[1024,512]{1,0:T(8,128)(2,1)}, bf16[1024,512]{1,0:T(8,128)(2,1)}, u32[]{:S(2)}, u32[]{:S(2)}) %collective-permute-start.16) | collective-permute-done | bytes 1048608 | tf_op jit(solution)/shard_map/ppermute | solution.py:264
  189.0 9.2 %collective-permute-done.14 = bf16[1408,512]{1,0:T(8,128)(2,1)} collective-permute-done((bf16[1408,512]{1,0:T(8,128)(2,1)}, bf16[1408,512]{1,0:T(8,128)(2,1)}, u32[]{:S(2)}, u32[]{:S(2)}) %collective-permute-start.14) | collective-permute-done | bytes 1441824 | tf_op jit(solution)/shard_map/ppermute | solution.py:264
  198.2 5.6 join.7
  206.5 12.0 %gated.2 = (bf16[1024,1408]{1,0:T(8,128)(2,1)}, bf16[1024,1408]{1,0:T(8,128)(2,1)}, bf16[1024,1408]{1,0:T(8,128)(2,1)}) custom-call(s32[2]{0:T(128)} %pad_add_fusion.place_ref.none_ref, bf16[1024,1024]{1,0:T(8,128)(2,1)} %pad_maximum_fusion.3.tokens, bf16[1024,1408]{1,0:T(8,128)(2,1)} %bitcast.229, bf16[1024,1408]{1,0:T(8,128)(2,1)} %bitcast.232), custom_call_target="tpu_custom_call" | custom-call | tf_op jit(solution)/shard_map/gated/pallas_call | solution.py:563
  222.1 4.5 join.8
  226.6 4.2 convolution_convert_fusion.13
  234.8 7.5 collective-permute-done.20
  246.4 5.1 join.9
  252.9 25.1 %attend_ahead.3 = (bf16[1024,1536]{1,0:T(8,128)(2,1)}, bf16[1024,512]{1,0:T(8,128)(2,1)S(1)}, f32[4,2,1024]{2,1,0:T(2,128)S(1)}) custom-call(s32[1]{0:T(128)} %bitcast.1.half_ref, bf16[1024,1024]{1,0:T(8,128)(2,1)S(1)} %pad_maximum_fusion.4.tokens_ref, bf16[1024,1536]{1,0:T(8,128)(2,1)} %bitcast.217, bf16[1024,1536]{1,0:T(8,128)(2,1)} %get-tuple-element.88.rest_0_.kept_ref, ...), custom_call_target="tpu_custom_call" | custom-call | tf_op jit(solution)/shard_map/attend_ahead/pallas_call | solution.py:201
  289.0 5.6 join.10
  294.6 3.0 pad_maximum_fusion.5.tokens
  297.6 12.5 %gated.3 = (bf16[1024,1408]{1,0:T(8,128)(2,1)}, bf16[1024,1408]{1,0:T(8,128)(2,1)}, bf16[1024,1408]{1,0:T(8,128)(2,1)}) custom-call(s32[2]{0:T(128)} %pad_add_fusion.place_ref.none_ref, bf16[1024,1024]{1,0:T(8,128)(2,1)} %pad_maximum_fusion.5.tokens, bf16[1024,1408]{1,0:T(8,128)(2,1)} %bitcast.235, bf16[1024,1408]{1,0:T(8,128)(2,1)} %bitcast.238), custom_call_target="tpu_custom_call" | custom-call | tf_op jit(solution)/shard_map/gated/pallas_call | solution.py:563
  310.1 4.3 join.11
  314.4 5.2 convolution_convert_fusion.12
  320.0 4.8 convolution_convert_fusion.2
  328.2 5.7 fusion.73
  334.0 3.1 fusion.5
  343.8 6.5 convolution_convert_fusion
  350.3 6.7 convolution_convert_fusion.1
  357.0 3.1 pad_maximum_fusion.1
  370.5 3.2 fusion.93
  374.2 4.3 fusion.69
  386.6 22.2 %attend_back.2 = (bf16[1024,1536]{1,0:T(8,128)(2,1)}, f32[1024,512]{1,0:T(8,128)S(1)}) custom-call(s32[1]{0:T(128)} %bitcast.1.half_ref, bf16[1024,1536]{1,0:T(8,128)(2,1)} %get-tuple-element.99.kept_ref, bf16[1024,512]{1,0:T(8,128)(2,1)S(1)} %convolution_convert_fusion.11.grad_ref, f32[4,2,1024]{2,1,0:T(2,128)S(1)} %get-tuple-element.100.lse_ref, ...), custom_call_target="tpu_custom_call" | custom-call | tf_op jit(solution)/shard_map/attend_back/pallas_call | solution.py:235
  408.8 5.0 fusion.47
  415.1 6.2 convolution_convert_fusion.3
  421.3 29.3 %collective-permute-done.63 = bf16[512,256]{1,0:T(8,128)(2,1)S(1)} collective-permute-done((bf16[512,256]{1,0:T(8,128)(2,1)S(1)}, bf16[512,256]{1,0:T(8,128)(2,1)S(1)}, u32[]{:S(2)}, u32[]{:S(2)}) %collective-permute-start.63) | collective-permute-done | bytes 262176 | tf_op jit(solution)/shard_map/ppermute | solution.py:264
  457.3 3.5 fusion.16
  463.5 3.4 multiply_reduce_fusion.1
  473.0 21.1 %reduce-scatter.21.cloned.1.call-done = bf16[352,256]{1,0:T(8,128)(2,1)} async-done(((bf16[1408,256]{1,0:T(8,128)(2,1)}), bf16[352,256]{1,0:T(8,128)(2,1)}) %reduce-scatter.21.cloned.1.call-update) | async-done | bytes 180240 | tf_op jit(solution)/shard_map/reduce_scatter | solution.py:595
  502.4 8.9 fusion.13
  513.9 3.8 convolution_convert_fusion.4
  517.7 4.8 convolution_convert_fusion.6
  525.9 4.8 convolution_convert_fusion.5
  533.5 4.7 pad_maximum_fusion
  540.9 5.4 fusion.56
  546.3 3.7 dynamic-slice_bitcast_fusion.1
  551.6 6.2 multiply_reduce_fusion.2
  569.5 3.1 convolution_convert_fusion.10.grad_ref
  572.6 22.1 %attend_back.3 = bf16[1024,1536]{1,0:T(8,128)(2,1)} custom-call(s32[1]{0:T(128)} %bitcast.1.half_ref, bf16[1024,1536]{1,0:T(8,128)(2,1)} %get-tuple-element.88.rest_0_.kept_ref, bf16[1024,512]{1,0:T(8,128)(2,1)S(1)} %convolution_convert_fusion.10.grad_ref, f32[4,2,1024]{2,1,0:T(2,128)S(1)} %get-tuple-element.104.lse_ref, f32[1024,512]{1,0:T(8,128)S(1)} %copy-done.2, ...), custom_call_target="tpu_custom_call" | custom-call | tf_op jit(solution)/shard_map/attend_back/pallas_call | solution.py:235
  594.7 4.3 fusion.50
  599.0 3.0 convolution_convert_fusion.9
  602.0 5.0 convolution_convert_fusion.7
  612.5 11.2 %collective-permute-done.43 = bf16[512,512]{1,0:T(8,128)(2,1)S(1)} collective-permute-done((bf16[512,512]{1,0:T(8,128)(2,1)S(1)}, bf16[512,512]{1,0:T(8,128)(2,1)S(1)}, u32[]{:S(2)}, u32[]{:S(2)}) %collective-permute-start.43) | collective-permute-done | bytes 524320 | tf_op jit(solution)/shard_map/ppermute | solution.py:264
  625.4 68.6 %collective-permute-done.44 = bf16[512,256]{1,0:T(8,128)(2,1)S(1)} collective-permute-done((bf16[512,256]{1,0:T(8,128)(2,1)S(1)}, bf16[512,256]{1,0:T(8,128)(2,1)S(1)}, u32[]{:S(2)}, u32[]{:S(2)}) %collective-permute-start.44) | collective-permute-done | bytes 262176 | tf_op jit(solution)/shard_map/ppermute | solution.py:264
  699.1 3.4 fusion.17
  707.2 6.3 fusion.32
  713.5 51.6 %psum.7 = f32[4,1024]{1,0:T(4,128)S(1)} all-reduce(f32[4,1024]{1,0:T(4,128)S(1)} %pad_maximum_fusion.29), channel_id=1, replica_groups=mesh['rep'=4,'shard'=4,'seq'=2] {'rep','shard','seq'}, use_global_device_ids=true, to_apply=%region_12.13 | all-reduce | flops 4096 | bytes 32768 | tf_op jit(solution)/shard_map/psum | solution.py:976
  765.0 3.5 fusion.29
  777.8 3.9 collective-permute-done.74
  783.7 9.0 collective-permute-done.73
  797.2 13.1 %collective-permute-done.38 = bf16[8,32,1536]{2,1,0:T(8,128)(2,1)S(1)} collective-permute-done((bf16[8,32,1536]{2,1,0:T(8,128)(2,1)S(1)}, bf16[8,32,1536]{2,1,0:T(8,128)(2,1)S(1)}, u32[]{:S(2)}, u32[]{:S(2)}) %collective-permute-start.38) | collective-permute-done | bytes 786464 | tf_op jit(solution)/shard_map/ppermute | solution.py:264
  824.4 7.1 collective-permute-done.48
  831.5 3.3 collective-permute-done.47
  852.8 4.2 collective-permute-done.40
  857.4 18.2 %reduce-scatter.15.cloned.1.call-done = bf16[64,2816]{1,0:T(8,128)(2,1)} async-done(((bf16[256,2816]{1,0:T(8,128)(2,1)}), bf16[64,2816]{1,0:T(8,128)(2,1)}) %reduce-scatter.15.cloned.1.call-update) | async-done | bytes 360464 | tf_op jit(solution)/shard_map/reduce_scatter | solution.py:595
  884.2 6.1 collective-permute-done.55
  890.3 8.1 collective-permute-done.54
  (525 shorter events, 253.0 us)
Async XLA Ops:
  7.2 39.6 %all-gather.6.cloned.1.call-start = ((), (), s32[]{:S(2)}) async-start(), calls=%async_computation.8 | async-start | bytes 1392640 | tf_op jit(solution)/shard_map/all_gather | solution.py:389
  15.0 80.7 %all-gather.10.cloned.1.call-start = ((), (), s32[]{:S(2)}) async-start(), calls=%async_computation.10 | async-start | bytes 2703360 | tf_op jit(solution)/shard_map/all_gather | solution.py:389
  22.7 136.6 %all-gather.8.cloned.1.call-start = ((), (), s32[]{:S(2)}) async-start(), calls=%async_computation.9 | async-start | bytes 1310720 | tf_op jit(solution)/shard_map/all_gather | solution.py:389
  29.7 176.8 %all-gather.12.cloned.1.call-start = ((), (), s32[]{:S(2)}) async-start(), calls=%async_computation.11 | async-start | bytes 2703360 | tf_op jit(solution)/shard_map/all_gather | solution.py:389
  46.8 26.3 %collective-permute-start.2 = (bf16[1088,512]{1,0:T(8,128)(2,1)}, bf16[1088,512]{1,0:T(8,128)(2,1)S(1)}, u32[]{:S(2)}, u32[]{:S(2)}) collective-permute-start(bf16[1088,512]{1,0:T(8,128)(2,1)} %all-gather.6.cloned.1.call-done), channel_id=1, source_target_pairs={{0,8},{8,0},{16,24},{24,16},{1,9},{9,1},{17,25},{25,17},{2,10},{10... | collective-permute-start | bytes 3342344 | tf_op jit(solution)/shard_map/ppermute | solution.py:264
  56.5 164.7 %all-gather.14.cloned.1.call-start = ((), (), s32[]{:S(2)}) async-start(), calls=%async_computation.12 | async-start | bytes 2703360 | tf_op jit(solution)/shard_map/all_gather | solution.py:389
  56.6 27.6 %collective-permute-start.3 = (bf16[1088,512]{1,0:T(8,128)(2,1)S(1)}, bf16[1088,512]{1,0:T(8,128)(2,1)}, u32[]{:S(2)}, u32[]{:S(2)}) collective-permute-start(bf16[1088,512]{1,0:T(8,128)(2,1)S(1)} %copy-done.66), channel_id=1, source_target_pairs={{0,16},{8,24},{16,0},{24,8},{1,17},{9,25},{17,1},{25,9},{2,18},{10... | collective-permute-start | bytes 3342344 | tf_op jit(solution)/shard_map/ppermute | solution.py:264
  73.1 34.1 %collective-permute-start.4 = (bf16[1088,512]{1,0:T(8,128)(2,1)S(1)}, bf16[1088,512]{1,0:T(8,128)(2,1)}, u32[]{:S(2)}, u32[]{:S(2)}) collective-permute-start(bf16[1088,512]{1,0:T(8,128)(2,1)S(1)} %collective-permute-done.2), channel_id=1, source_target_pairs={{0,16},{8,24},{16,0},{24,8},{1,17},{9,25},{17,1},{25,9},{2,18},{10... | collective-permute-start | bytes 3342344 | tf_op jit(solution)/shard_map/ppermute | solution.py:264
  109.8 49.5 %collective-permute-start.8 = (bf16[1408,512]{1,0:T(8,128)(2,1)}, bf16[1408,512]{1,0:T(8,128)(2,1)}, u32[]{:S(2)}, u32[]{:S(2)}) collective-permute-start(bf16[1408,512]{1,0:T(8,128)(2,1)} %bitcast.19), channel_id=1, source_target_pairs={{0,8},{8,0},{16,24},{24,16},{1,9},{9,1},{17,25},{25,17},{2,10},{10... | collective-permute-start | bytes 4325384 | tf_op jit(solution)/shard_map/ppermute | solution.py:264
  110.3 49.0 %collective-permute-start.7 = (bf16[1408,512]{1,0:T(8,128)(2,1)}, bf16[1408,512]{1,0:T(8,128)(2,1)}, u32[]{:S(2)}, u32[]{:S(2)}) collective-permute-start(bf16[1408,512]{1,0:T(8,128)(2,1)} %bitcast.19), channel_id=1, source_target_pairs={{0,16},{8,24},{16,0},{24,8},{1,17},{9,25},{17,1},{25,9},{2,18},{10... | collective-permute-start | bytes 4325384 | tf_op jit(solution)/shard_map/ppermute | solution.py:264
  117.1 42.2 %collective-permute-start.10 = (bf16[704,512]{1,0:T(8,128)(2,1)S(1)}, bf16[704,512]{1,0:T(8,128)(2,1)}, u32[]{:S(2)}, u32[]{:S(2)}) collective-permute-start(bf16[704,512]{1,0:T(8,128)(2,1)S(1)} %bitcast.227), channel_id=1, source_target_pairs={{0,16},{8,24},{16,0},{24,8},{1,17},{9,25},{17,1},{25,9},{2,18},{10... | collective-permute-start | bytes 2162696 | tf_op jit(solution)/shard_map/ppermute | solution.py:264
  117.7 41.6 %collective-permute-start.9 = (bf16[704,512]{1,0:T(8,128)(2,1)S(1)}, bf16[704,512]{1,0:T(8,128)(2,1)}, u32[]{:S(2)}, u32[]{:S(2)}) collective-permute-start(bf16[704,512]{1,0:T(8,128)(2,1)S(1)} %bitcast.228), channel_id=1, source_target_pairs={{0,8},{8,0},{16,24},{24,16},{1,9},{9,1},{17,25},{25,17},{2,10},{10... | collective-permute-start | bytes 2162696 | tf_op jit(solution)/shard_map/ppermute | solution.py:264
  125.1 346.4 %reduce-scatter.19.cloned.1.call-start = ((), (), s32[]{:S(2)}) async-start(), calls=%async_computation.18 | async-start | bytes 327680 | tf_op jit(solution)/shard_map/reduce_scatter | solution.py:595
  161.8 26.3 %collective-permute-start.16 = (bf16[1024,512]{1,0:T(8,128)(2,1)}, bf16[1024,512]{1,0:T(8,128)(2,1)}, u32[]{:S(2)}, u32[]{:S(2)}) collective-permute-start(bf16[1024,512]{1,0:T(8,128)(2,1)} %all-gather.8.cloned.1.call-done), channel_id=1, source_target_pairs={{0,16},{8,24},{16,0},{24,8},{1,17},{9,25},{17,1},{25,9},{2,18},{10... | collective-permute-start | bytes 3145736 | tf_op jit(solution)/shard_map/ppermute | solution.py:264
  163.4 34.7 %collective-permute-start.14 = (bf16[1408,512]{1,0:T(8,128)(2,1)}, bf16[1408,512]{1,0:T(8,128)(2,1)}, u32[]{:S(2)}, u32[]{:S(2)}) collective-permute-start(bf16[1408,512]{1,0:T(8,128)(2,1)} %collective-permute-done.7), channel_id=1, source_target_pairs={{0,8},{8,0},{16,24},{24,16},{1,9},{9,1},{17,25},{25,17},{2,10},{10... | collective-permute-start | bytes 4325384 | tf_op jit(solution)/shard_map/ppermute | solution.py:264
  167.0 36.8 %collective-permute-start.12 = (bf16[512,1024]{1,0:T(8,128)(2,1)S(1)}, bf16[512,1024]{1,0:T(8,128)(2,1)}, u32[]{:S(2)}, u32[]{:S(2)}) collective-permute-start(bf16[512,1024]{1,0:T(8,128)(2,1)S(1)} %multiply_convert_fusion.2), channel_id=1, source_target_pairs={{0,1},{1,0},{2,3},{3,2},{4,5},{5,4},{6,7},{7,6},{8,9},{9,8},{10,11... | collective-permute-start | bytes 3145736 | tf_op jit(solution)/shard_map/ppermute | solution.py:259
  167.2 54.0 %collective-permute-start.17 = (bf16[1024,512]{1,0:T(8,128)(2,1)}, bf16[1024,512]{1,0:T(8,128)(2,1)}, u32[]{:S(2)}, u32[]{:S(2)}) collective-permute-start(bf16[1024,512]{1,0:T(8,128)(2,1)} %all-gather.8.cloned.1.call-done), channel_id=1, source_target_pairs={{0,8},{8,0},{16,24},{24,16},{1,9},{9,1},{17,25},{25,17},{2,10},{10... | collective-permute-start | bytes 3145736 | tf_op jit(solution)/shard_map/ppermute | solution.py:264
  168.2 53.1 %collective-permute-start.18 = (bf16[704,512]{1,0:T(8,128)(2,1)}, bf16[704,512]{1,0:T(8,128)(2,1)S(1)}, u32[]{:S(2)}, u32[]{:S(2)}) collective-permute-start(bf16[704,512]{1,0:T(8,128)(2,1)} %collective-permute-done.9), channel_id=1, source_target_pairs={{0,16},{8,24},{16,0},{24,8},{1,17},{9,25},{17,1},{25,9},{2,18},{10... | collective-permute-start | bytes 2162696 | tf_op jit(solution)/shard_map/ppermute | solution.py:264
  188.1 54.2 %collective-permute-start.20 = (bf16[1024,512]{1,0:T(8,128)(2,1)}, bf16[1024,512]{1,0:T(8,128)(2,1)}, u32[]{:S(2)}, u32[]{:S(2)}) collective-permute-start(bf16[1024,512]{1,0:T(8,128)(2,1)} %collective-permute-done.16), channel_id=1, source_target_pairs={{0,8},{8,0},{16,24},{24,16},{1,9},{9,1},{17,25},{25,17},{2,10},{10... | collective-permute-start | bytes 3145736 | tf_op jit(solution)/shard_map/ppermute | solution.py:264
  233.4 44.6 %collective-permute-start.23 = (bf16[1408,512]{1,0:T(8,128)(2,1)}, bf16[1408,512]{1,0:T(8,128)(2,1)}, u32[]{:S(2)}, u32[]{:S(2)}) collective-permute-start(bf16[1408,512]{1,0:T(8,128)(2,1)} %bitcast.43), channel_id=1, source_target_pairs={{0,16},{8,24},{16,0},{24,8},{1,17},{9,25},{17,1},{25,9},{2,18},{10... | collective-permute-start | bytes 4325384 | tf_op jit(solution)/shard_map/ppermute | solution.py:264
  242.4 35.6 %collective-permute-start.22 = (bf16[1408,512]{1,0:T(8,128)(2,1)}, bf16[1408,512]{1,0:T(8,128)(2,1)}, u32[]{:S(2)}, u32[]{:S(2)}) collective-permute-start(bf16[1408,512]{1,0:T(8,128)(2,1)} %bitcast.41), channel_id=1, source_target_pairs={{0,8},{8,0},{16,24},{24,16},{1,9},{9,1},{17,25},{25,17},{2,10},{10... | collective-permute-start | bytes 4325384 | tf_op jit(solution)/shard_map/ppermute | solution.py:264
  287.4 22.7 %collective-permute-start.27 = (bf16[704,512]{1,0:T(8,128)(2,1)}, bf16[704,512]{1,0:T(8,128)(2,1)}, u32[]{:S(2)}, u32[]{:S(2)}) collective-permute-start(bf16[704,512]{1,0:T(8,128)(2,1)} %bitcast.52), channel_id=1, source_target_pairs={{0,16},{8,24},{16,0},{24,8},{1,17},{9,25},{17,1},{25,9},{2,18},{10... | collective-permute-start | bytes 2162696 | tf_op jit(solution)/shard_map/ppermute | solution.py:264
  287.9 22.2 %collective-permute-start.26 = (bf16[704,512]{1,0:T(8,128)(2,1)S(1)}, bf16[704,512]{1,0:T(8,128)(2,1)}, u32[]{:S(2)}, u32[]{:S(2)}) collective-permute-start(bf16[704,512]{1,0:T(8,128)(2,1)S(1)} %bitcast.226), channel_id=1, source_target_pairs={{0,8},{8,0},{16,24},{24,16},{1,9},{9,1},{17,25},{25,17},{2,10},{10... | collective-permute-start | bytes 2162696 | tf_op jit(solution)/shard_map/ppermute | solution.py:264
  289.0 31.0 %collective-permute-start.29 = (bf16[512,1024]{1,0:T(8,128)(2,1)}, bf16[512,1024]{1,0:T(8,128)(2,1)}, u32[]{:S(2)}, u32[]{:S(2)}) collective-permute-start(bf16[512,1024]{1,0:T(8,128)(2,1)} %bitcast.56), channel_id=1, source_target_pairs={{0,1},{1,0},{2,3},{3,2},{4,5},{5,4},{6,7},{7,6},{8,9},{9,8},{10,11... | collective-permute-start | bytes 3145736 | tf_op jit(solution)/shard_map/ppermute | solution.py:259
  319.5 54.7 %collective-permute-start.28 = (bf16[512,1024]{1,0:T(8,128)(2,1)}, bf16[512,1024]{1,0:T(8,128)(2,1)}, u32[]{:S(2)}, u32[]{:S(2)}) collective-permute-start(bf16[512,1024]{1,0:T(8,128)(2,1)} %convolution_convert_fusion.12), channel_id=1, source_target_pairs={{0,1},{1,0},{2,3},{3,2},{4,5},{5,4},{6,7},{7,6},{8,9},{9,8},{10,11... | collective-permute-start | bytes 3145736 | tf_op jit(solution)/shard_map/ppermute | solution.py:259
  327.0 51.5 %collective-permute-start.64 = (bf16[1408,512]{1,0:T(8,128)(2,1)}, bf16[1408,512]{1,0:T(8,128)(2,1)}, u32[]{:S(2)}, u32[]{:S(2)}) collective-permute-start(bf16[1408,512]{1,0:T(8,128)(2,1)} %constant_dynamic-slice_fusion.1), channel_id=1, source_target_pairs={{0,8},{8,0},{16,24},{24,16},{1,9},{9,1},{17,25},{25,17},{2,10},{10... | collective-permute-start | bytes 4325384 | tf_op jit(solution)/shard_map/ppermute | solution.py:264
  343.8 24.0 %collective-permute-start.30 = (bf16[512,1024]{1,0:T(8,128)(2,1)}, bf16[512,1024]{1,0:T(8,128)(2,1)S(1)}, u32[]{:S(2)}, u32[]{:S(2)}) collective-permute-start(bf16[512,1024]{1,0:T(8,128)(2,1)} %add_convert_fusion.3), channel_id=1, source_target_pairs={{0,1},{1,0},{2,3},{3,2},{4,5},{5,4},{6,7},{7,6},{8,9},{9,8},{10,11... | collective-permute-start | bytes 3145736 | tf_op jit(solution)/shard_map/ppermute | solution.py:259
  364.4 92.9 %collective-permute-start.69 = (bf16[8,64,2816]{2,1,0:T(8,128)(2,1)}, bf16[8,64,2816]{2,1,0:T(8,128)(2,1)}, u32[]{:S(2)}, u32[]{:S(2)}) collective-permute-start(bf16[8,64,2816]{2,1,0:T(8,128)(2,1)} %dynamic-slice_bitcast_fusion), channel_id=1, source_target_pairs={{0,16},{8,24},{16,0},{24,8},{1,17},{9,25},{17,1},{25,9},{2,18},{10... | collective-permute-start | bytes 8650760 | tf_op jit(solution)/shard_map/ppermute | solution.py:264
  381.5 73.6 %collective-permute-start.65 = (bf16[1408,256]{1,0:T(8,128)(2,1)}, bf16[1408,256]{1,0:T(8,128)(2,1)}, u32[]{:S(2)}, u32[]{:S(2)}) collective-permute-start(bf16[1408,256]{1,0:T(8,128)(2,1)} %constant_dynamic-slice_fusion), channel_id=1, source_target_pairs={{0,16},{8,24},{16,0},{24,8},{1,17},{9,25},{17,1},{25,9},{2,18},{10... | collective-permute-start | bytes 2162696 | tf_op jit(solution)/shard_map/ppermute | solution.py:264
  384.4 29.5 %collective-permute-start.62 = (bf16[512,512]{1,0:T(8,128)(2,1)S(1)}, bf16[512,512]{1,0:T(8,128)(2,1)S(1)}, u32[]{:S(2)}, u32[]{:S(2)}) collective-permute-start(bf16[512,512]{1,0:T(8,128)(2,1)S(1)} %constant_dynamic-slice_fusion.3), channel_id=1, source_target_pairs={{0,8},{8,0},{16,24},{24,16},{1,9},{9,1},{17,25},{25,17},{2,10},{10... | collective-permute-start | bytes 1572872 | tf_op jit(solution)/shard_map/ppermute | solution.py:264
  413.9 47.0 %collective-permute-start.32 = (bf16[512,1024]{1,0:T(8,128)(2,1)}, bf16[512,1024]{1,0:T(8,128)(2,1)}, u32[]{:S(2)}, u32[]{:S(2)}) collective-permute-start(bf16[512,1024]{1,0:T(8,128)(2,1)} %fusion.47), channel_id=1, source_target_pairs={{0,1},{1,0},{2,3},{3,2},{4,5},{5,4},{6,7},{7,6},{8,9},{9,8},{10,11... | collective-permute-start | bytes 3145736 | tf_op jit(solution)/shard_map/ppermute | solution.py:259
  414.1 36.5 %collective-permute-start.63 = (bf16[512,256]{1,0:T(8,128)(2,1)S(1)}, bf16[512,256]{1,0:T(8,128)(2,1)S(1)}, u32[]{:S(2)}, u32[]{:S(2)}) collective-permute-start(bf16[512,256]{1,0:T(8,128)(2,1)S(1)} %constant_dynamic-slice_fusion.2), channel_id=1, source_target_pairs={{0,16},{8,24},{16,0},{24,8},{1,17},{9,25},{17,1},{25,9},{2,18},{10... | collective-permute-start | bytes 786440 | tf_op jit(solution)/shard_map/ppermute | solution.py:264
  451.4 42.7 %reduce-scatter.21.cloned.1.call-start = ((), (), s32[]{:S(2)}) async-start(), calls=%async_computation.19 | async-start | bytes 901120 | tf_op jit(solution)/shard_map/reduce_scatter | solution.py:595
  454.1 44.4 %collective-permute-start.56 = (bf16[8,64,1536]{2,1,0:T(8,128)(2,1)}, bf16[8,64,1536]{2,1,0:T(8,128)(2,1)}, u32[]{:S(2)}, u32[]{:S(2)}) collective-permute-start(bf16[8,64,1536]{2,1,0:T(8,128)(2,1)} %dynamic-slice_bitcast_fusion.2), channel_id=1, source_target_pairs={{0,8},{8,0},{16,24},{24,16},{1,9},{9,1},{17,25},{25,17},{2,10},{10... | collective-permute-start | bytes 4718600 | tf_op jit(solution)/shard_map/ppermute | solution.py:264
  457.2 105.4 %reduce-scatter.17.cloned.1.call-start = ((), (), s32[]{:S(2)}) async-start(), calls=%async_computation.17 | async-start | bytes 983040 | tf_op jit(solution)/shard_map/reduce_scatter | solution.py:595
  469.2 33.1 %collective-permute-start.33 = (bf16[512,1024]{1,0:T(8,128)(2,1)}, bf16[512,1024]{1,0:T(8,128)(2,1)}, u32[]{:S(2)}, u32[]{:S(2)}) collective-permute-start(bf16[512,1024]{1,0:T(8,128)(2,1)} %get-tuple-element.116), channel_id=1, source_target_pairs={{0,1},{1,0},{2,3},{3,2},{4,5},{5,4},{6,7},{7,6},{8,9},{9,8},{10,11... | collective-permute-start | bytes 3145736 | tf_op jit(solution)/shard_map/ppermute | solution.py:259
  470.4 79.6 %collective-permute-start.70 = (bf16[8,32,2816]{2,1,0:T(8,128)(2,1)}, bf16[8,32,2816]{2,1,0:T(8,128)(2,1)S(1)}, u32[]{:S(2)}, u32[]{:S(2)}) collective-permute-start(bf16[8,32,2816]{2,1,0:T(8,128)(2,1)} %dynamic-slice_bitcast_fusion.4), channel_id=1, source_target_pairs={{0,8},{8,0},{16,24},{24,16},{1,9},{9,1},{17,25},{25,17},{2,10},{10... | collective-permute-start | bytes 4325384 | tf_op jit(solution)/shard_map/ppermute | solution.py:264
  495.7 320.5 %collective-permute-start.68 = (bf16[480,256]{1,0:T(8,128)(2,1)}, bf16[480,256]{1,0:T(8,128)(2,1)S(1)}, u32[]{:S(2)}, u32[]{:S(2)}) collective-permute-start(bf16[480,256]{1,0:T(8,128)(2,1)} %constant_dynamic-update-slice_fusion.50), channel_id=1, source_target_pairs={{0,16},{8,24},{16,0},{24,8},{1,17},{9,25},{17,1},{25,9},{2,18},{10... | collective-permute-start | bytes 737288 | tf_op jit(solution)/shard_map/ppermute | solution.py:264
  497.1 319.6 %collective-permute-start.67 = (bf16[480,256]{1,0:T(8,128)(2,1)}, bf16[480,256]{1,0:T(8,128)(2,1)}, u32[]{:S(2)}, u32[]{:S(2)}) collective-permute-start(bf16[480,256]{1,0:T(8,128)(2,1)} %constant_dynamic-update-slice_fusion.50), channel_id=1, source_target_pairs={{0,8},{8,0},{16,24},{24,16},{1,9},{9,1},{17,25},{25,17},{2,10},{10... | collective-permute-start | bytes 737288 | tf_op jit(solution)/shard_map/ppermute | solution.py:264
  501.7 36.5 %collective-permute-start.57 = (bf16[8,32,1536]{2,1,0:T(8,128)(2,1)}, bf16[8,32,1536]{2,1,0:T(8,128)(2,1)}, u32[]{:S(2)}, u32[]{:S(2)}) collective-permute-start(bf16[8,32,1536]{2,1,0:T(8,128)(2,1)} %dynamic-slice_bitcast_fusion.6), channel_id=1, source_target_pairs={{0,16},{8,24},{16,0},{24,8},{1,17},{9,25},{17,1},{25,9},{2,18},{10... | collective-permute-start | bytes 2359304 | tf_op jit(solution)/shard_map/ppermute | solution.py:264
  523.8 36.9 %collective-permute-start.45 = (bf16[1408,512]{1,0:T(8,128)(2,1)}, bf16[1408,512]{1,0:T(8,128)(2,1)}, u32[]{:S(2)}, u32[]{:S(2)}) collective-permute-start(bf16[1408,512]{1,0:T(8,128)(2,1)} %constant_dynamic-slice_fusion.5), channel_id=1, source_target_pairs={{0,8},{8,0},{16,24},{24,16},{1,9},{9,1},{17,25},{25,17},{2,10},{10... | collective-permute-start | bytes 4325384 | tf_op jit(solution)/shard_map/ppermute | solution.py:264
  538.2 13.4 %collective-permute-start.34 = (bf16[512,1024]{1,0:T(8,128)(2,1)}, bf16[512,1024]{1,0:T(8,128)(2,1)}, u32[]{:S(2)}, u32[]{:S(2)}) collective-permute-start(bf16[512,1024]{1,0:T(8,128)(2,1)} %add_convert_fusion.2), channel_id=1, source_target_pairs={{0,1},{1,0},{2,3},{3,2},{4,5},{5,4},{6,7},{7,6},{8,9},{9,8},{10,11... | collective-permute-start | bytes 3145736 | tf_op jit(solution)/shard_map/ppermute | solution.py:259
  540.5 164.9 %reduce-scatter.23.cloned.1.call-start = ((), (), s32[]{:S(2)}) async-start(), calls=%async_computation.20 | async-start | bytes 1802240 | tf_op jit(solution)/shard_map/reduce_scatter | solution.py:595
  551.5 221.4 %reduce-scatter.11.cloned.1.call-start = ((), (), s32[]{:S(2)}) async-start(), calls=%async_computation.14 | async-start | bytes 327680 | tf_op jit(solution)/shard_map/reduce_scatter | solution.py:595
  565.9 43.2 %collective-permute-start.61 = (bf16[32,3072]{1,0:T(8,128)(2,1)S(1)}, bf16[32,3072]{1,0:T(8,128)(2,1)S(1)}, u32[]{:S(2)}, u32[]{:S(2)}) collective-permute-start(bf16[32,3072]{1,0:T(8,128)(2,1)S(1)} %pad_maximum_fusion.28), channel_id=1, source_target_pairs={{0,16},{8,24},{16,0},{24,8},{1,17},{9,25},{17,1},{25,9},{2,18},{10... | collective-permute-start | bytes 589832 | tf_op jit(solution)/shard_map/ppermute | solution.py:264
  567.4 43.0 %collective-permute-start.60 = (bf16[32,3072]{1,0:T(8,128)(2,1)S(1)}, bf16[32,3072]{1,0:T(8,128)(2,1)S(1)}, u32[]{:S(2)}, u32[]{:S(2)}) collective-permute-start(bf16[32,3072]{1,0:T(8,128)(2,1)S(1)} %pad_maximum_fusion.28), channel_id=1, source_target_pairs={{0,8},{8,0},{16,24},{24,16},{1,9},{9,1},{17,25},{25,17},{2,10},{10... | collective-permute-start | bytes 589832 | tf_op jit(solution)/shard_map/ppermute | solution.py:264
  568.4 42.7 %collective-permute-start.59 = (bf16[32,3072]{1,0:T(8,128)(2,1)S(1)}, bf16[32,3072]{1,0:T(8,128)(2,1)S(1)}, u32[]{:S(2)}, u32[]{:S(2)}) collective-permute-start(bf16[32,3072]{1,0:T(8,128)(2,1)S(1)} %pad_maximum_fusion.28), channel_id=1, source_target_pairs={{0,24},{8,16},{16,8},{24,0},{1,25},{9,17},{17,9},{25,1},{2,26},{10... | collective-permute-start | bytes 589832 | tf_op jit(solution)/shard_map/ppermute | solution.py:264
  609.2 90.0 %collective-permute-start.50 = (bf16[8,64,2816]{2,1,0:T(8,128)(2,1)}, bf16[8,64,2816]{2,1,0:T(8,128)(2,1)}, u32[]{:S(2)}, u32[]{:S(2)}) collective-permute-start(bf16[8,64,2816]{2,1,0:T(8,128)(2,1)} %dynamic-slice_bitcast_fusion.1), channel_id=1, source_target_pairs={{0,16},{8,24},{16,0},{24,8},{1,17},{9,25},{17,1},{25,9},{2,18},{10... | collective-permute-start | bytes 8650760 | tf_op jit(solution)/shard_map/ppermute | solution.py:264
  610.4 85.2 %collective-permute-start.46 = (bf16[1408,256]{1,0:T(8,128)(2,1)}, bf16[1408,256]{1,0:T(8,128)(2,1)}, u32[]{:S(2)}, u32[]{:S(2)}) collective-permute-start(bf16[1408,256]{1,0:T(8,128)(2,1)} %constant_dynamic-slice_fusion.4), channel_id=1, source_target_pairs={{0,16},{8,24},{16,0},{24,8},{1,17},{9,25},{17,1},{25,9},{2,18},{10... | collective-permute-start | bytes 2162696 | tf_op jit(solution)/shard_map/ppermute | solution.py:264
  623.8 70.1 %collective-permute-start.44 = (bf16[512,256]{1,0:T(8,128)(2,1)S(1)}, bf16[512,256]{1,0:T(8,128)(2,1)S(1)}, u32[]{:S(2)}, u32[]{:S(2)}) collective-permute-start(bf16[512,256]{1,0:T(8,128)(2,1)S(1)} %constant_dynamic-slice_fusion.6), channel_id=1, source_target_pairs={{0,16},{8,24},{16,0},{24,8},{1,17},{9,25},{17,1},{25,9},{2,18},{10... | collective-permute-start | bytes 786440 | tf_op jit(solution)/shard_map/ppermute | solution.py:264
  694.8 118.2 %reduce-scatter.13.cloned.1.call-start = ((), (), s32[]{:S(2)}) async-start(), calls=%async_computation.15 | async-start | bytes 901120 | tf_op jit(solution)/shard_map/reduce_scatter | solution.py:595
  695.6 78.8 %collective-permute-start.37 = (bf16[8,64,1536]{2,1,0:T(8,128)(2,1)}, bf16[8,64,1536]{2,1,0:T(8,128)(2,1)}, u32[]{:S(2)}, u32[]{:S(2)}) collective-permute-start(bf16[8,64,1536]{2,1,0:T(8,128)(2,1)} %dynamic-slice_bitcast_fusion.3), channel_id=1, source_target_pairs={{0,8},{8,0},{16,24},{24,16},{1,9},{9,1},{17,25},{25,17},{2,10},{10... | collective-permute-start | bytes 4718600 | tf_op jit(solution)/shard_map/ppermute | solution.py:264
  698.9 140.5 %reduce-scatter.9.cloned.1.call-start = ((), (), s32[]{:S(2)}) async-start(), calls=%async_computation.13 | async-start | bytes 983040 | tf_op jit(solution)/shard_map/reduce_scatter | solution.py:595
  706.9 62.1 %collective-permute-start.71 = (bf16[32,2816]{1,0:T(8,128)(2,1)}, bf16[32,2816]{1,0:T(8,128)(2,1)}, u32[]{:S(2)}, u32[]{:S(2)}) collective-permute-start(bf16[32,2816]{1,0:T(8,128)(2,1)} %dynamic-slice_bitcast_fusion.8), channel_id=1, source_target_pairs={{0,1},{1,0},{2,3},{3,2},{4,5},{5,4},{6,7},{7,6},{8,9},{9,8},{10,11... | collective-permute-start | bytes 540680 | tf_op jit(solution)/shard_map/ppermute | solution.py:259
  772.4 20.3 %collective-permute-start.73 = (bf16[32,5632]{1,0:T(8,128)(2,1)S(1)}, bf16[32,5632]{1,0:T(8,128)(2,1)S(1)}, u32[]{:S(2)}, u32[]{:S(2)}) collective-permute-start(bf16[32,5632]{1,0:T(8,128)(2,1)S(1)} %pad_maximum_fusion.25), channel_id=1, source_target_pairs={{0,16},{8,24},{16,0},{24,8},{1,17},{9,25},{17,1},{25,9},{2,18},{10... | collective-permute-start | bytes 1081352 | tf_op jit(solution)/shard_map/ppermute | solution.py:264
  774.4 18.3 %collective-permute-start.72 = (bf16[32,5632]{1,0:T(8,128)(2,1)S(1)}, bf16[32,5632]{1,0:T(8,128)(2,1)S(1)}, u32[]{:S(2)}, u32[]{:S(2)}) collective-permute-start(bf16[32,5632]{1,0:T(8,128)(2,1)S(1)} %pad_maximum_fusion.25), channel_id=1, source_target_pairs={{0,24},{8,16},{16,8},{24,0},{1,25},{9,17},{17,9},{25,1},{2,26},{10... | collective-permute-start | bytes 1081352 | tf_op jit(solution)/shard_map/ppermute | solution.py:264
  781.8 42.6 %collective-permute-start.66 = (bf16[480,256]{1,0:T(8,128)(2,1)}, bf16[480,256]{1,0:T(8,128)(2,1)}, u32[]{:S(2)}, u32[]{:S(2)}) collective-permute-start(bf16[480,256]{1,0:T(8,128)(2,1)} %constant_dynamic-update-slice_fusion.50), channel_id=1, source_target_pairs={{0,24},{8,16},{16,8},{24,0},{1,25},{9,17},{17,9},{25,1},{2,26},{10... | collective-permute-start | bytes 737288 | tf_op jit(solution)/shard_map/ppermute | solution.py:264
  792.7 47.6 %collective-permute-start.51 = (bf16[8,32,2816]{2,1,0:T(8,128)(2,1)}, bf16[8,32,2816]{2,1,0:T(8,128)(2,1)}, u32[]{:S(2)}, u32[]{:S(2)}) collective-permute-start(bf16[8,32,2816]{2,1,0:T(8,128)(2,1)} %dynamic-slice_bitcast_fusion.5), channel_id=1, source_target_pairs={{0,8},{8,0},{16,24},{24,16},{1,9},{9,1},{17,25},{25,17},{2,10},{10... | collective-permute-start | bytes 4325384 | tf_op jit(solution)/shard_map/ppermute | solution.py:264
  792.7 17.6 %collective-permute-start.38 = (bf16[8,32,1536]{2,1,0:T(8,128)(2,1)S(1)}, bf16[8,32,1536]{2,1,0:T(8,128)(2,1)S(1)}, u32[]{:S(2)}, u32[]{:S(2)}) collective-permute-start(bf16[8,32,1536]{2,1,0:T(8,128)(2,1)S(1)} %dynamic-slice_bitcast_fusion.7), channel_id=1, source_target_pairs={{0,16},{8,24},{16,0},{24,8},{1,17},{9,25},{17,1},{25,9},{2,18},{10... | collective-permute-start | bytes 2359304 | tf_op jit(solution)/shard_map/ppermute | solution.py:264
  811.4 64.1 %reduce-scatter.15.cloned.1.call-start = ((), (), s32[]{:S(2)}) async-start(), calls=%async_computation.16 | async-start | bytes 1802240 | tf_op jit(solution)/shard_map/reduce_scatter | solution.py:595
  816.2 15.2 %collective-permute-start.48 = (bf16[480,256]{1,0:T(8,128)(2,1)}, bf16[480,256]{1,0:T(8,128)(2,1)}, u32[]{:S(2)}, u32[]{:S(2)}) collective-permute-start(bf16[480,256]{1,0:T(8,128)(2,1)} %constant_dynamic-update-slice_fusion.24), channel_id=1, source_target_pairs={{0,8},{8,0},{16,24},{24,16},{1,9},{9,1},{17,25},{25,17},{2,10},{10... | collective-permute-start | bytes 737288 | tf_op jit(solution)/shard_map/ppermute | solution.py:264
  816.9 17.9 %collective-permute-start.47 = (bf16[480,256]{1,0:T(8,128)(2,1)}, bf16[480,256]{1,0:T(8,128)(2,1)}, u32[]{:S(2)}, u32[]{:S(2)}) collective-permute-start(bf16[480,256]{1,0:T(8,128)(2,1)} %constant_dynamic-update-slice_fusion.24), channel_id=1, source_target_pairs={{0,24},{8,16},{16,8},{24,0},{1,25},{9,17},{17,9},{25,1},{2,26},{10... | collective-permute-start | bytes 737288 | tf_op jit(solution)/shard_map/ppermute | solution.py:264
  880.5 17.9 %collective-permute-start.54 = (bf16[32,5632]{1,0:T(8,128)(2,1)S(1)}, bf16[32,5632]{1,0:T(8,128)(2,1)S(1)}, u32[]{:S(2)}, u32[]{:S(2)}) collective-permute-start(bf16[32,5632]{1,0:T(8,128)(2,1)S(1)} %pad_maximum_fusion.24), channel_id=1, source_target_pairs={{0,16},{8,24},{16,0},{24,8},{1,17},{9,25},{17,1},{25,9},{2,18},{10... | collective-permute-start | bytes 1081352 | tf_op jit(solution)/shard_map/ppermute | solution.py:264
  882.0 16.4 %collective-permute-start.53 = (bf16[32,5632]{1,0:T(8,128)(2,1)S(1)}, bf16[32,5632]{1,0:T(8,128)(2,1)S(1)}, u32[]{:S(2)}, u32[]{:S(2)}) collective-permute-start(bf16[32,5632]{1,0:T(8,128)(2,1)S(1)} %pad_maximum_fusion.24), channel_id=1, source_target_pairs={{0,24},{8,16},{16,8},{24,0},{1,25},{9,17},{17,9},{25,1},{2,26},{10... | collective-permute-start | bytes 1081352 | tf_op jit(solution)/shard_map/ppermute | solution.py:264
  (131 other events, 1394.3 us)
Sparse Core Ops, SparseCore 0:
  15.1 31.6 all-gather.5
  48.9 46.7 all-gather.9
  97.8 26.6 all-gather.7
  126.5 46.7 all-gather.11
  175.2 45.9 all-gather.13
  451.5 18.4 reduce-scatter.18
  472.9 21.0 reduce-scatter.20
  540.6 21.5 reduce-scatter.16
  565.2 32.5 reduce-scatter.22
  694.9 18.3 reduce-scatter.10
  716.2 21.1 reduce-scatter.12
  811.6 22.2 reduce-scatter.8
  843.3 32.2 reduce-scatter.14

commit v2 on v1

--- a/solution.py
+++ b/solution.py
@@ -39,7 +39,12 @@
         at += rows
 
 
-def ahead_kernel(blocks, mixed, half_ref, tokens_ref, weight_ref, *rest):
+def block_of(mine_ref, other_ref, block, blocks, half):
+    own, rows = block // (blocks // 2), pl.ds(block % (blocks // 2) * BLOCK, BLOCK)
+    return jnp.where(half == own, mine_ref[rows, :], other_ref[rows, :])
+
+
+def ahead_kernel(blocks, mixed, half_ref, mine_ref, other_ref, weight_ref, *rest):
     if mixed:
         first_ref, rest = rest[0], rest[1:]
     cos_ref, sin_ref, column_ref, row_ref, kept_ref, out_ref, lse_ref, bias = rest
@@ -55,9 +60,8 @@
     for b in range(blocks):
         rows = pl.ds(b * BLOCK, BLOCK)
         cosine, sine = cos_ref[rows, :], sin_ref[rows, :]
-        raw = jnp.dot(
-            tokens_ref[pl.ds(place(b), BLOCK), :], weight_ref[...], preferred_element_type=jnp.float32
-        )
+        tokens = block_of(mine_ref, other_ref, b, blocks, half_ref[0])
+        raw = jnp.dot(tokens, weight_ref[...], preferred_element_type=jnp.float32)
         for part in range(2):
             one = raw[:, part * LANES : (part + 1) * LANES]
             turned = one * cosine + swap_halves(one) * sine
@@ -101,7 +105,7 @@
         out_ref[pl.ds(place(i), BLOCK), :] = merged.T.astype(jnp.bfloat16)
 
 
-def back_kernel(blocks, mixed, half_ref, kept_ref, grad_ref, lse_ref, *rest):
+def back_kernel(blocks, mixed, half_ref, kept_ref, mine_ref, other_ref, lse_ref, *rest):
     if not mixed:
         extra_ref, rest = rest[0], rest[1:]
     cos_ref, sin_ref, column_ref, row_ref, out_ref, *rest = rest
@@ -129,7 +133,7 @@
         rows = pl.ds(i * BLOCK, BLOCK)
         span = pl.ds(first * BLOCK, count)
         query = kept_ref[rows, 0:LANES] * jnp.bfloat16(HD**-0.5)
-        grad = grad_ref[pl.ds(place(i), BLOCK), :]
+        grad = block_of(mine_ref, other_ref, i, blocks, half_ref[0])
         keys = kept_ref[span, LANES : 2 * LANES]
         values = kept_ref[span, 2 * LANES :]
         fill = bias[pl.ds(at, count), :]
@@ -193,7 +197,7 @@
 
 def attend_ahead(tokens, weight, first_kept, tables, half):
     cosine, sine, column, row = tables
-    length, width = tokens.shape[0], weight.shape[1]
+    length, width = 2 * tokens[0].shape[0], weight.shape[1]
     pairs, blocks = width // (3 * LANES), length // BLOCK
     mixed = first_kept is not None
     wide = pl.BlockSpec((length, 3 * LANES), lambda h, s: (0, h))
@@ -208,7 +212,8 @@
         grid_spec=pltpu.PrefetchScalarGridSpec(
             num_scalar_prefetch=1,
             grid=(pairs,),
-            in_specs=[whole(tokens.shape), pl.BlockSpec((weight.shape[0], 3 * LANES), lambda h, s: (0, h))]
+            in_specs=[whole(tokens[0].shape)] * 2
+            + [pl.BlockSpec((weight.shape[0], 3 * LANES), lambda h, s: (0, h))]
             + ([wide] if mixed else [])
             + [whole(cosine.shape), whole(sine.shape), whole(column.shape), whole(row.shape)],
             out_specs=(wide, slim, pl.BlockSpec((1, LANES // HD, length), lambda h, s: (h, 0, 0))),
@@ -217,7 +222,7 @@
         compiler_params=pltpu.CompilerParams(dimension_semantics=("arbitrary",), vmem_limit_bytes=48 << 20),
         cost_estimate=pl.CostEstimate(flops=0, transcendentals=0, bytes_accessed=0),
         name="attend_ahead",
-    )(half, tokens, weight, *((first_kept,) if mixed else ()), cosine, sine, column, row)
+    )(half, *tokens, weight, *((first_kept,) if mixed else ()), cosine, sine, column, row)
 
 
 def attend_back(kept, grad, lse, extra, tables, half):
@@ -238,7 +243,9 @@
         grid_spec=pltpu.PrefetchScalarGridSpec(
             num_scalar_prefetch=1,
             grid=(pairs,),
-            in_specs=[wide, slim, pl.BlockSpec((1, LANES // HD, length), lambda h, s: (h, 0, 0))]
+            in_specs=[wide]
+            + [pl.BlockSpec((length // 2, LANES), lambda h, s: (0, h))] * 2
+            + [pl.BlockSpec((1, LANES // HD, length), lambda h, s: (h, 0, 0))]
             + ([] if mixed else [slim])
             + [whole(cosine.shape), whole(sine.shape), whole(column.shape), whole(row.shape)],
             out_specs=tuple(out_specs),
@@ -251,7 +258,7 @@
         compiler_params=pltpu.CompilerParams(dimension_semantics=("arbitrary",), vmem_limit_bytes=48 << 20),
         cost_estimate=pl.CostEstimate(flops=0, transcendentals=0, bytes_accessed=0),
         name="attend_back",
-    )(half, kept, grad, lse, *(() if mixed else (extra,)), cosine, sine, column, row)
+    )(half, kept, *grad, lse, *(() if mixed else (extra,)), cosine, sine, column, row)
     return result if mixed else (result[0], None)
 
 
@@ -401,8 +408,7 @@
     w_qkv = gather_shard(chip_rows(column_parts((w_query, w_key, w_value), sizes, core, True), sizes, core))
     w_wide = gather_shard(chip_rows(column_parts((w_gate, w_upward), sizes, core, False), sizes, core))
     w_proj, w_down = (gather_shard(w.astype(jnp.bfloat16)) for w in (w_proj, w_down))
-    width = w_wide.shape[1] // 2
-    return w_qkv, w_proj, w_wide[:, :width], w_wide[:, width:], w_down
+    return w_qkv, w_proj, w_wide, w_down
 
 
 def call(kernel, outs, grid, in_specs, out_specs, name, scratch=(), scalars=1):
@@ -524,7 +530,7 @@
         fixed((total, FLAT)),
         "near_merge",
     )(place, mine, swap_cores(theirs), proj)
-    return gather_shard(merged)
+    return merged
 
 
 def gather_far(weights, down, shards, place):
@@ -546,89 +552,509 @@
         fixed((total, FLAT)),
         "far_merge",
     )(place, mine, swap_cores(theirs), down)
-    return gather_shard(merged)
-
-
-def gated_kernel(none_ref, tokens, gate, upward, gate_out, upward_out, inner_out):
-    one = jnp.dot(tokens[...], gate[...], preferred_element_type=jnp.float32)
-    two = jnp.dot(tokens[...], upward[...], preferred_element_type=jnp.float32)
+    return merged
+
+
+def dot_nn(a, b):
+    return jnp.dot(a, b, preferred_element_type=jnp.float32)
+
+
+def halves_of_rows(tile, per_half):
+    return [
+        lambda i, s: (jnp.minimum(i, per_half - 1), 0),
+        lambda i, s: (jnp.maximum(i - per_half, 0), 0),
+    ]
+
+
+def gated_kernel(per_half, none_ref, mine, other, weight, gate_out, upward_out, inner_out):
+    tokens = jnp.where(pl.program_id(0) < per_half, mine[...], other[...])
+    width = gate_out.shape[1]
+    one, two = dot_nn(tokens, weight[:, :width]), dot_nn(tokens, weight[:, width:])
     inner_out[...] = low(one * jax.nn.sigmoid(one) * two)
     gate_out[...] = low(one)
     upward_out[...] = low(two)
 
 
-def gated(tokens, gate, upward, place):
-    length, width, tile = tokens.shape[0], gate.shape[1], 256
+def gated(tokens, weight, place):
+    length, width, tile = 2 * tokens[0].shape[0], weight.shape[1] // 2, 256
     rows = pl.BlockSpec((tile, width), lambda i, s: (i, 0))
+    maps = halves_of_rows(tile, length // tile // 2)
     return call(
-        gated_kernel,
+        functools.partial(gated_kernel, length // tile // 2),
         [shape_of(length, width)] * 3,
         (length // tile,),
-        [pl.BlockSpec((tile, tokens.shape[1]), lambda i, s: (i, 0)), fixed(gate.shape), fixed(upward.shape)],
+        [pl.BlockSpec((tile, tokens[0].shape[1]), m) for m in maps] + [fixed(weight.shape)],
         [rows] * 3,
         "gated",
-    )(place, tokens, gate, upward)
+    )(place, *tokens, weight)
+
+
+def gated_back_kernel(per_half, none_ref, mine, other, weight, gate, upward, out):
+    grad = jnp.where(pl.program_id(0) < per_half, mine[...], other[...])
+    width = gate.shape[1]
+    inner = lax.dot_general(grad, weight[...], (((1,), (1,)), ((), ())), preferred_element_type=jnp.float32)
+    one, two = gate[...].astype(jnp.float32), upward[...].astype(jnp.float32)
+    part = jax.nn.sigmoid(one)
+    out[:, :width] = low(inner * two * part * (1.0 + one * (1.0 - part)))
+    out[:, width:] = low(inner * one * part)
+
+
+def gated_back(grad, weight, gate, upward, place):
+    (length, width), tile = gate.shape, 256
+    rows = pl.BlockSpec((tile, width), lambda i, s: (i, 0))
+    maps = halves_of_rows(tile, length // tile // 2)
+    return call(
+        functools.partial(gated_back_kernel, length // tile // 2),
+        shape_of(length, 2 * width),
+        (length // tile,),
+        [pl.BlockSpec((tile, grad[0].shape[1]), m) for m in maps] + [fixed(weight.shape), rows, rows],
+        pl.BlockSpec((tile, 2 * width), lambda i, s: (i, 0)),
+        "gated_back",
+    )(place, *grad, weight, gate, upward)
+
+
+def turned(a, b):
+    return lax.dot_general(a, b, (((0,), (0,)), ((), ())), preferred_element_type=jnp.float32)
+
+
+def grad_rows_kernel(bits_ref, mine, other, right, *outs):
+    half, parts = mine.shape[0], len(outs) // 2
+    product = turned(mine[...], right[0:half, :]) + turned(other[...], right[half:, :])
+    groups, rows, width = outs[0].shape
+    for part in range(parts):
+        sent, kept = outs[2 * part : 2 * part + 2]
+        upper, columns = bits_ref[part] == 0, slice(part * width, (part + 1) * width)
+        for g in range(groups):
+            one, two = (low(product[(2 * g + h) * rows : (2 * g + h + 1) * rows, columns]) for h in range(2))
+            kept[g] = jnp.where(upper, one, two)
+            sent[g] = jnp.where(upper, two, one)
+
+
+def grad_rows(left, right, groups, bits, parts=1, tile=256):
+    half, features = left[0].shape
+    length, width = right.shape
+    per, rows = groups * tile // features, features // groups // 2
+    out = pl.BlockSpec((per, rows, width // parts), lambda i, s: (i, 0, 0))
+    return call(
+        grad_rows_kernel,
+        [shape_of(groups, rows, width // parts)] * (2 * parts),
+        (features // tile,),
+        [pl.BlockSpec((half, tile), lambda i, s: (0, i))] * 2 + [fixed((length, width))],
+        [out] * (2 * parts),
+        "grad_rows",
+    )(bits, *left, right)
+
+
+def grad_whole_kernel(none_ref, left, mine, other, out):
+    half = mine.shape[0]
+    out[...] = low(turned(left[0:half, :], mine[...]) + turned(left[half:, :], other[...]))
+
+
+def grad_whole(left, right, place, steps=2):
+    length, rows = left.shape
+    half, width = right[0].shape
+    side = pl.BlockSpec((half, width // steps), lambda i, s: (0, i))
+    return call(
+        grad_whole_kernel,
+        shape_of(rows, width),
+        (steps,),
+        [fixed((length, rows)), side, side],
+        pl.BlockSpec((rows, width // steps), lambda i, s: (0, i)),
+        "grad_whole",
+    )(place, left, *right)
+
+
+def grad_columns_kernel(bits_ref, left, mine, other, sent, kept):
+    half = mine.shape[0]
+    product = low(turned(left[0:half, :], mine[...]) + turned(left[half:, :], other[...]))
+
+    @pl.when(pl.program_id(0) == 0)
+    def _():
+        sent[...] = product
+
+    @pl.when(pl.program_id(0) == 1)
+    def _():
+        kept[...] = product
+
+
+def grad_columns(left, right, bits):
+    length, rows = left.shape
+    half, width = right[0].shape
+    side = pl.BlockSpec((half, width // 2), lambda i, s: (0, jnp.where(i == 0, 1 - s[0], s[0])))
+    return call(
+        grad_columns_kernel,
+        [shape_of(rows, width // 2)] * 2,
+        (2,),
+        [fixed((length, rows)), side, side],
+        [fixed((rows, width // 2))] * 2,
+        "grad_columns",
+    )(bits, left, *right)
+
+
+def add(a, b):
+    return a + b
+
+
+def halve_kernel(parts, bits_ref, *refs):
+    ins, outs = refs[: 2 * parts], refs[2 * parts :]
+    for part in range(parts):
+        kept, got = ins[2 * part : 2 * part + 2]
+        sent_out, kept_out = outs[2 * part : 2 * part + 2]
+        total = add(kept[...], got[...])
+        upper = bits_ref[1 - part] == 0
+        middle = kept.shape[1] // 2
+        one, two = total[:, :middle], total[:, middle:]
+        kept_out[...] = jnp.where(upper, one, two)
+        sent_out[...] = jnp.where(upper, two, one)
+
+
+def halve(ins, bits, steps):
+    shape, parts = ins[0].shape, len(ins) // 2
+    block = (shape[0] // steps, *shape[1:])
+    small = (*shape[:1], shape[1] // 2, *shape[2:])
+    index = lambda i, s: (i,) + (0,) * (len(shape) - 1)
+    return call(
+        functools.partial(halve_kernel, parts),
+        [shape_of(*small)] * (2 * parts),
+        (steps,),
+        [pl.BlockSpec(block, index)] * (2 * parts),
+        [pl.BlockSpec((block[0], *small[1:]), index)] * (2 * parts),
+        "halve",
+    )(bits, *ins)
+
+
+def flatten_kernel(parts, none_ref, *refs):
+    bodies, tails, out = refs[: 2 * parts], refs[2 * parts : -1], refs[-1]
+    sums = [add(bodies[2 * p][...], bodies[2 * p + 1][...]) for p in range(parts)]
+    total = jnp.concatenate(sums, axis=2) if parts > 1 else sums[0]
+    cores, rows, columns = total.shape
+    blocks, left = columns // FLAT, columns % FLAT
+    for j in range(blocks):
+        for c in range(cores):
+            there = slice((j * cores + c) * rows, (j * cores + c + 1) * rows)
+            out[0, there, :] = total[c, :, j * FLAT : (j + 1) * FLAT]
+    at = blocks * cores * rows
+    if left:
+        for c in range(cores):
+            out[0, at : at + rows, c * left : (c + 1) * left] = total[c, :, columns - left :]
+        at += rows
+    if tails:
+        tail = add(tails[0][...], tails[1][...])
+        half = tail.shape[0] // 2
+        out[0, at:, 0 : FLAT // 2] = tail[:half]
+        out[0, at:, FLAT // 2 :] = tail[half:]
+
+
+def flatten(bodies, tails, shards, bits):
+    groups, rows, columns = bodies[0].shape
+    height, width = tails[0].shape if tails else (0, 0)
+    cores, parts = groups // shards, len(bodies) // 2
+    total = (parts * cores * rows * columns + height // shards * width) // FLAT
+    return call(
+        functools.partial(flatten_kernel, parts),
+        shape_of(shards, total, FLAT),
+        (shards,),
+        [pl.BlockSpec((cores, rows, columns), lambda i, s: (i, 0, 0))] * len(bodies)
+        + [pl.BlockSpec((height // shards, width), lambda i, s: (i, 0))] * len(tails),
+        pl.BlockSpec((1, total, FLAT), lambda i, s: (i, 0, 0)),
+        "flatten",
+    )(bits, *bodies, *tails).reshape(-1, FLAT)
+
+
+def append_kernel(none_ref, *refs):
+    bodies, (kept, got, out) = refs[:-3], refs[-3:]
+    at = 0
+    for body in bodies:
+        out[at : at + body.shape[0], :] = body[...]
+        at += body.shape[0]
+    tail, half = add(kept[...], got[...]), kept.shape[0] // 2
+    out[at:, 0 : FLAT // 2] = tail[:half]
+    out[at:, FLAT // 2 :] = tail[half:]
+
+
+def append(bodies, kept, got, bits):
+    rows = sum(b.shape[0] for b in bodies) + kept.shape[0] // 2
+    return call(
+        append_kernel,
+        shape_of(rows, FLAT),
+        (1,),
+        [fixed(x.shape) for x in (*bodies, kept, got)],
+        fixed((rows, FLAT)),
+        "append",
+    )(bits, *bodies, kept, got)
+
+
+def from_row(pieces, start):
+    return [p.at[pl.ds(start, p.shape[0] - start)] for p in pieces] if start else pieces
+
+
+def pick_kernel(blocks, rows, left, start, count, place_ref, *refs):
+    pieces, out = from_row(refs[:count], start), refs[-1]
+    which = 1 - place_ref[1]
+    for k, piece in enumerate(pieces):
+        for j in range(blocks):
+            there = pl.ds(pl.multiple_of((2 * j + which) * rows, rows), rows)
+            out[k, j * rows : (j + 1) * rows, :] = piece[there, :]
+        if left:
+            there = pl.ds(pl.multiple_of(which * left, left), left)
+            out[k, blocks * rows :, 0:left] = piece[2 * blocks * rows : (2 * blocks + 1) * rows, there]
+            out[k, blocks * rows :, left:] = jnp.zeros((rows, FLAT - left), jnp.bfloat16)
+
+
+def pick(pieces, rows, columns, place, start, after):
+    blocks, left = columns // FLAT, columns % FLAT
+    total = (blocks + (left > 0)) * rows
+    return call(
+        functools.partial(pick_kernel, blocks, rows, left, start, len(pieces)),
+        shape_of(len(pieces), total, FLAT),
+        (1,),
+        [fixed(pieces[0].shape)] * len(pieces) + [pl.BlockSpec(memory_space=pl.ANY)] * len(after),
+        fixed((len(pieces), total, FLAT)),
+        "pick",
+    )(place, *pieces, *after)
+
+
+def slots_of(bits_ref):
+    places = []
+    for one, two in ((0, 0), (1, 0), (0, 1), (1, 1)):
+        first, second = lax.bitwise_xor(bits_ref[0], one), lax.bitwise_xor(bits_ref[1], two)
+        places.append((2 * first + second, 2 * second + first))
+    return places
+
+
+def tail_out(piece, start, out, slot):
+    half, columns = out.shape[0] // 2, FLAT // 2
+    there = pl.ds(pl.multiple_of(slot * columns, columns), columns)
+    out[0:half, there] = piece[start : start + half, 0:columns].astype(jnp.float32)
+    out[half:, there] = piece[start : start + half, columns:].astype(jnp.float32)
+
+
+def finish_near_kernel(shards, rows, start, bits_ref, place_ref, *refs):
+    pieces, other, outs, tail = from_row(refs[:4], start), refs[4], refs[5:8], refs[8]
+    core = place_ref[1]
+    for k, slots in enumerate(slots_of(bits_ref)):
+        for s in range(shards):
+            there = pl.ds(pl.multiple_of(slots[2 * s // shards] * rows, rows), rows)
+            for j, out in enumerate(outs):
+                block, lane = divmod((3 * s + j) * LANES, FLAT)
+                mine_rows = pl.ds(pl.multiple_of((2 * block + core) * rows, rows), rows)
+                mine = pieces[k][mine_rows, lane : lane + LANES]
+                theirs = other[k, block * rows : (block + 1) * rows, lane : lane + LANES]
+                for part, which in ((mine, core), (theirs, 1 - core)):
+                    lanes = pl.ds(pl.multiple_of((2 * s + which) * LANES, LANES), LANES)
+                    out[there, lanes] = part.astype(jnp.float32)
+        tail_out(pieces[k], 6 * rows, tail, slots[0])
+
+
+def finish_far_kernel(shards, rows, start, bits_ref, place_ref, *refs):
+    pieces, other, outs, tail = from_row(refs[:4], start), refs[4], refs[5:7], refs[7]
+    core = place_ref[1]
+    width = outs[0].shape[1] // (2 * shards)
+    columns = 2 * shards * width
+    blocks, left = columns // FLAT, columns % FLAT
+    for k, slots in enumerate(slots_of(bits_ref)):
+        mine = [
+            pieces[k][pl.ds(pl.multiple_of((2 * j + core) * rows, rows), rows), :] for j in range(blocks)
+        ]
+        lanes = pl.ds(pl.multiple_of(core * left, left), left)
+        mine.append(pieces[k][2 * blocks * rows : (2 * blocks + 1) * rows, lanes])
+        theirs = [other[k, j * rows : (j + 1) * rows, :] for j in range(blocks)]
+        theirs.append(other[k, blocks * rows :, 0:left])
+        mine, theirs = (jnp.concatenate(p, axis=1).astype(jnp.float32) for p in (mine, theirs))
+        even, odd = jnp.where(core == 0, mine, theirs), jnp.where(core == 0, theirs, mine)
+        for at, out in enumerate(outs):
+            there = pl.ds(pl.multiple_of(slots[at] * rows, rows), rows)
+            parts = [
+                p[:, (at * shards + s) * width : (at * shards + s + 1) * width]
+                for s in range(shards)
+                for p in (even, odd)
+            ]
+            out[there, :] = jnp.concatenate(parts, axis=1)
+        tail_out(pieces[k], (2 * blocks + 1) * rows, tail, slots[0])
+
+
+class Way:
+    def __init__(self, halves, plan, bits):
+        self.sent, self.kept = halves[::2], halves[1::2]
+        self.plan, self.bits = plan, bits
+        self.got = [exchange(x, plan[p]) for p, x in enumerate(self.sent)]
+
+    def last(self, value):
+        return [x for pair in zip(self.kept, self.got) for x in (tie(pair[0], value), pair[1])]
+
+    def half(self, value, steps=2):
+        outs = halve(self.last(value), self.bits, steps)
+        self.sent, self.kept = outs[::2], outs[1::2]
+        self.got = [exchange(x, self.plan[1 - p]) for p, x in enumerate(self.sent)]
+        return tuple(self.sent)
+
+
+class TunedSender:
+    def __init__(self, sizes, place, near, far):
+        self.sizes, self.place, self.near_plan, self.far_plan = sizes, place, near, far
+        self.near_bits, self.far_bits = (
+            jnp.stack([bit_of(place[0], m) for m in plan]).astype(jnp.int32) for plan in (near, far)
+        )
+        self.groups = sizes[0] * sizes[1]
+
+    def down(self, left, right):
+        grad = grad_whole(left, right, self.place)
+        self.down_sum = scatter_shard(grad)
+        return grad
+
+    def down_way(self, value):
+        reduced, bit = tie(self.down_sum, value), self.far_bits[0]
+        width = reduced.shape[1] // 2
+        halves = [lax.dynamic_slice_in_dim(reduced, b * width, width, 1) for b in (1 - bit, bit)]
+        self.way_down = Way(halves, self.far_plan, self.far_bits)
+        return halves[0]
+
+    def wide(self, left, right):
+        self.way_wide = Way(grad_rows(left, right, self.groups, self.far_bits, 2), self.far_plan, self.far_bits)
+        return self.way_wide.sent[0]
+
+    def proj(self, left, right):
+        self.way_proj = Way(grad_columns(left, right, self.near_bits), self.near_plan, self.near_bits)
+        return self.way_proj.sent[0]
+
+    def qkv(self, left, right):
+        self.way_qkv = Way(grad_rows(left, right, self.groups, self.near_bits, 2), self.near_plan, self.near_bits)
+        return self.way_qkv.sent[0]
+
+    def half(self, name, steps=2):
+        return lambda value: getattr(self, name).half(value, steps)
+
+    def got(self, name):
+        return lambda value: tuple(getattr(self, name).got)
+
+    def scatter_wide(self, value):
+        self.wide_shape = self.way_wide.kept[0].shape
+        flat = flatten(self.way_wide.last(value), (), self.sizes[0], self.far_bits)
+        self.wide_sum = scatter_shard(flat)
+        return flat
+
+    def scatter_near(self, value):
+        self.near_shape, self.proj_height = self.way_qkv.kept[0].shape, self.way_proj.kept[0].shape[0] // self.sizes[0]
+        flat = flatten(self.way_qkv.last(value), self.way_proj.last(value), self.sizes[0], self.near_bits)
+        self.near_sum = scatter_shard(flat)
+        return flat
+
+    def shared(self, piece, plan):
+        return [piece] + [exchange(piece, m) for m in (*plan, plan[0] ^ plan[1])]
+
+    def share_near(self, value):
+        self.near_at, self.near_pieces = 0, self.shared(tie(self.near_sum, value), self.near_plan)
+        return self.near_pieces[0]
+
+    def share_far(self, value):
+        piece = append([tie(self.wide_sum, value)], self.way_down.kept[0], self.way_down.got[0], self.far_bits)
+        self.far_at, self.far_pieces = 0, self.shared(piece, self.far_plan)
+        return piece
+
+    def share_all(self, value):
+        bodies = [tie(self.near_sum, value), self.wide_sum]
+        piece = append(bodies, self.way_down.kept[0], self.way_down.got[0], self.far_bits)
+        self.near_at, self.far_at = 0, self.near_sum.shape[0]
+        own, one, two, both = self.near_pieces = self.shared(piece, self.near_plan)
+        self.far_pieces = [own, one, two, both] if self.near_plan == self.far_plan else [own, two, one, both]
+        return piece
+
+    def far_got(self, value):
+        return tuple(self.far_pieces[1:])
+
+    def near_got(self, value):
+        return tuple(self.near_pieces[1:])
+
+    def pick_near(self, value, *after):
+        _, rows, columns = self.near_shape
+        pieces = [tie(self.near_pieces[0], value), *self.near_pieces[1:]]
+        picked = pick(pieces, rows, 2 * columns, self.place, self.near_at, after)
+        self.near_other = swap_cores(picked)
+        return picked
+
+    def pick_far(self, value, *after):
+        _, rows, columns = self.wide_shape
+        pieces = [tie(self.far_pieces[0], value), *self.far_pieces[1:]]
+        picked = pick(pieces, rows, 2 * columns, self.place, self.far_at, after)
+        self.far_other = swap_cores(picked)
+        return picked
+
+    def finish_near(self, value):
+        rows, features = self.near_shape[1], self.groups * LANES
+        self.near = self.finish(
+            functools.partial(finish_near_kernel, self.sizes[0], rows, self.near_at),
+            [(4 * rows, features)] * 3 + [(self.proj_height, 2 * FLAT)],
+            (self.near_bits, tie(self.place, value), *self.near_pieces, self.near_other),
+            "finish_near",
+        )
+        return self.near[0]
+
+    def finish_far(self, value):
+        _, rows, columns = self.wide_shape
+        self.far = self.finish(
+            functools.partial(finish_far_kernel, self.sizes[0], rows, self.far_at),
+            [(4 * rows, 2 * columns)] * 2 + [(self.way_down.kept[0].shape[0], 2 * FLAT)],
+            (self.far_bits, tie(self.place, value), *self.far_pieces, self.far_other),
+            "finish_far",
+        )
+        return self.far[0]
+
+    def finish(self, kernel, shapes, operands, name):
+        return call(
+            kernel,
+            [shape_of(*s, dtype=jnp.float32) for s in shapes],
+            (1,),
+            [fixed(x.shape) for x in operands[2:]],
+            [fixed(s) for s in shapes],
+            name,
+            scalars=2,
+        )(*operands)
+
+
+class PlainSender:
+    def __init__(self, sizes, core):
+        self.sizes, self.core = sizes, core
+
+    def total(self, grad):
+        return lax.psum(scatter_shard(low(grad)), "rep")
+
+    def down(self, left, right):
+        self.down_sum = self.total(dot_tn(left, jnp.concatenate(right, axis=0)))
+
+    def proj(self, left, right):
+        self.proj_sum = self.total(dot_tn(left, jnp.concatenate(right, axis=0)))
+
+    def wide(self, left, right):
+        self.wide_sum = self.total(dot_tn(jnp.concatenate(left, axis=0), right))
+
+    def qkv(self, left, right):
+        self.qkv_sum = self.total(dot_tn(jnp.concatenate(left, axis=0), right))
+
+    def columns(self, reduced):
+        shaped = reduced.reshape(2, -1, reduced.shape[1])
+        mine = lax.dynamic_index_in_dim(shaped, self.core, 0, keepdims=False)
+        other = swap_cores(lax.dynamic_index_in_dim(shaped, 1 - self.core, 0, keepdims=False))
+        even, odd = jnp.where(self.core == 0, mine, other), jnp.where(self.core == 0, other, mine)
+        return even.astype(jnp.float32), odd.astype(jnp.float32)
+
+    def near(self):
+        even, odd = self.columns(self.qkv_sum)
+        parts = [spread_columns(e, o, self.sizes) for e, o in zip(head_minor(even), head_minor(odd))]
+        return (*parts, self.proj_sum.astype(jnp.float32))
+
+    def far(self):
+        even, odd = self.columns(self.wide_sum)
+        width = even.shape[1] // 2
+        parts = [spread_columns(even[:, at], odd[:, at], self.sizes) for at in (slice(0, width), slice(width, None))]
+        return (*parts, self.down_sum.astype(jnp.float32))
 
 
 def bit_of(rep, mask):
     return (rep // mask) % 2
 
 
-def halve_rows(grad, groups, bit, mask):
-    shaped = grad.reshape(groups, 2, -1, grad.shape[1])
-    sent = lax.dynamic_index_in_dim(shaped, 1 - bit, 1, keepdims=False)
-    kept = lax.dynamic_index_in_dim(shaped, bit, 1, keepdims=False)
-    got = exchange(sent, mask)
-    total = kept.astype(jnp.float32) + got.astype(jnp.float32)
-    return total.astype(jnp.bfloat16).reshape(-1, grad.shape[1])
-
-
-def halve_columns(grad, bit, mask):
-    width = grad.shape[1] // 2
-    sent = lax.dynamic_slice_in_dim(grad, (1 - bit) * width, width, 1)
-    kept = lax.dynamic_slice_in_dim(grad, bit * width, width, 1)
-    got = exchange(sent, mask)
-    return (kept.astype(jnp.float32) + got.astype(jnp.float32)).astype(jnp.bfloat16)
-
-
 def scatter_shard(x):
     return lax.psum_scatter(x, "shard", scatter_dimension=0, tiled=True)
-
-
-def columns_back(grad, sizes, rep, plan):
-    if plan is None:
-        return lax.psum(scatter_shard(grad), "rep")
-    first, second = plan
-    groups = sizes[0] * sizes[1]
-    half = halve_rows(grad, groups, bit_of(rep, first), first)
-    return scatter_shard(halve_rows(half, groups, bit_of(rep, second), second))
-
-
-def rows_back(grad, rep, plan):
-    if plan is None:
-        return lax.psum(scatter_shard(grad), "rep")
-    first, second = plan
-    half = halve_columns(grad, bit_of(rep, first), first)
-    return scatter_shard(halve_columns(half, bit_of(rep, second), second))
-
-
-def in_order(pieces, slot_high, slot_low):
-    p0, p1, p2, p3 = pieces
-    low = slot_low == 1
-    q0, q1 = jnp.where(low, p1, p0), jnp.where(low, p0, p1)
-    q2, q3 = jnp.where(low, p3, p2), jnp.where(low, p2, p3)
-    high = slot_high == 1
-    return [
-        jnp.where(high, q2, q0),
-        jnp.where(high, q3, q1),
-        jnp.where(high, q0, q2),
-        jnp.where(high, q1, q3),
-    ]
-
-
-def share_slots(piece, plan):
-    first, second = plan
-    return [piece, exchange(piece, second), exchange(piece, first), exchange(piece, first ^ second)]
 
 
 def spread_columns(even, odd, sizes):
@@ -639,29 +1065,6 @@
     )
 
 
-def finish_columns(reduced, sizes, core, rep, plan):
-    rows = reduced.shape[0] // 2
-    shaped = reduced.reshape(2, rows, reduced.shape[1])
-    mine = lax.dynamic_index_in_dim(shaped, core, 0, keepdims=False)
-    other = swap_cores(lax.dynamic_index_in_dim(shaped, 1 - core, 0, keepdims=False))
-    even, odd = jnp.where(core == 0, mine, other), jnp.where(core == 0, other, mine)
-    if plan is None:
-        return even.astype(jnp.float32), odd.astype(jnp.float32)
-    both = jnp.concatenate([even, odd], axis=1)
-    first, second = plan
-    ordered = in_order(share_slots(both, plan), bit_of(rep, first), bit_of(rep, second))
-    full = jnp.concatenate(ordered, axis=0).astype(jnp.float32)
-    return full[:, : even.shape[1]], full[:, even.shape[1] :]
-
-
-def finish_rows(reduced, rep, plan):
-    if plan is None:
-        return reduced.astype(jnp.float32)
-    first, second = plan
-    ordered = in_order(share_slots(reduced, plan), bit_of(rep, first), bit_of(rep, second))
-    return jnp.concatenate(ordered, axis=1).astype(jnp.float32)
-
-
 def norm_ahead(values, gain_row):
     factor = lax.rsqrt(jnp.mean(values * values, axis=-1, keepdims=True) + eps_norm)
     return ((values * factor * gain_row).astype(jnp.bfloat16), factor)
@@ -675,7 +1078,7 @@
 
 
 def both_halves(mine):
-    return jnp.concatenate([mine, swap_cores(mine)], axis=0)
+    return mine, swap_cores(mine)
 
 
 def dot(a, b):
@@ -690,8 +1093,8 @@
     return lax.dot_general(a, b, (((0,), (0,)), ((), ())), preferred_element_type=jnp.float32)
 
 
-def sum_halves(product, rows):
-    theirs = swap_cores(product(slice(rows, 2 * rows)).astype(jnp.bfloat16))
+def sum_halves(product, rows, hook=lambda value: value):
+    theirs = hook(swap_cores(product(slice(rows, 2 * rows)).astype(jnp.bfloat16)))
     return product(slice(0, rows)) + theirs.astype(jnp.float32)
 
 
@@ -703,37 +1106,37 @@
     gain_attn, gain_ffn = gains
     rows = flat.shape[0]
     normed, factor_attn = norm_ahead(flat, gain_attn)
-    normed_all = both_halves(normed)
+    normed = both_halves(normed)
     w_qkv, w_proj = weights.near()
-    kept, attended, lse = attend_ahead(normed_all, w_qkv, first_kept, tables, place[1:])
+    kept, attended, lse = attend_ahead(normed, w_qkv, first_kept, tables, place[1:])
     attended = weights.after_attention(attended)
-    theirs = dot(attended[rows:], w_proj).astype(jnp.bfloat16)
+    theirs = low(dot(attended[rows:], w_proj))
     middle = flat + dot(attended[:rows], w_proj) + swap_cores(theirs).astype(jnp.float32)
     normed_ffn, factor_ffn = norm_ahead(middle, gain_ffn)
-    ffn_all = both_halves(normed_ffn)
-    w_gate, w_upward = weights.wide()
-    ffn_all = weights.before_wide(ffn_all)
-    gate_pre, upward_pre, inner = gated(ffn_all, w_gate, w_upward, place)
+    normed_ffn = both_halves(normed_ffn)
+    (w_wide,) = weights.wide()
+    normed_ffn = (weights.before_wide(normed_ffn[0]), normed_ffn[1])
+    gate_pre, upward_pre, inner = gated(normed_ffn, w_wide, place)
     inner = weights.after_wide(inner)
     (w_down,) = weights.down(inner)
-    theirs = dot(inner[rows:], w_down).astype(jnp.bfloat16)
+    theirs = low(dot(inner[rows:], w_down))
     result = middle + dot(inner[:rows], w_down) + swap_cores(theirs).astype(jnp.float32)
     result = weights.at_end(result)
     saved = (
         flat,
         factor_attn,
-        normed_all,
+        normed,
         kept,
         lse,
         attended,
         middle,
         factor_ffn,
-        ffn_all,
+        normed_ffn,
         gate_pre,
         upward_pre,
         inner,
     )
-    return result, kept, saved, (w_qkv, w_proj, w_gate, w_upward, w_down)
+    return result, kept, saved, (w_qkv, w_proj, w_wide, w_down)
 
 
 class Plain:
@@ -744,10 +1147,10 @@
         return self.weights[:2]
 
     def wide(self):
-        return self.weights[2:4]
+        return self.weights[2:3]
 
     def down(self, inner):
-        return self.weights[4:]
+        return self.weights[3:]
 
     def same(self, value):
         return value
@@ -770,7 +1173,7 @@
         (qkv_rows, qkv_width), proj_rows, (wide_rows, wide_width), down_rows = shapes
         self.cut, self.shards = wide_rows * wide_width // FLAT, sizes[0]
         self.near_parts = (("columns", qkv_rows, (qkv_width,)), ("rows", proj_rows, (FLAT // 2,)))
-        self.wide_parts = (("columns", wide_rows, (wide_width // 2,) * 2),)
+        self.wide_parts = (("columns", wide_rows, (wide_width,)),)
         self.down_parts = (("rows", down_rows, (FLAT // 2,)),)
         self.join = lambda q, parts, after=(): join(
             q.pieces, q.masks, q.slot, sizes, parts, q.starts.get(parts[0][0]), after
@@ -815,88 +1218,62 @@
     return near, wide, Halves(place, down, (near.two, near.three))
 
 
-def layer_back(upstream, gains, weights, saved, extra, tables, half, send):
+def layer_back(upstream, gains, weights, saved, extra, tables, place, send, hooks):
     gain_attn, gain_ffn = gains
-    w_qkv, w_proj, w_gate, w_upward, w_down = weights
+    w_qkv, w_proj, w_wide, w_down = weights
     (
         flat,
         factor_attn,
-        normed_all,
+        normed,
         kept,
         lse,
         attended,
         middle,
         factor_ffn,
-        ffn_all,
+        normed_ffn,
         gate_pre,
         upward_pre,
         inner,
     ) = saved
     rows = flat.shape[0]
-    grad_down_all = both_halves(upstream.astype(jnp.bfloat16))
-    grad_inner = dot_nt(grad_down_all, w_down)
-    gate_pre, upward_pre = gate_pre.astype(jnp.float32), upward_pre.astype(jnp.float32)
-    sigmoid_gate = jax.nn.sigmoid(gate_pre)
-    grad_gate = (
-        grad_inner * upward_pre * sigmoid_gate * (1.0 + gate_pre * (1.0 - sigmoid_gate))
-    ).astype(jnp.bfloat16)
-    grad_upward = (grad_inner * gate_pre * sigmoid_gate).astype(jnp.bfloat16)
-    sent_down = send.down(dot_tn(inner, grad_down_all).astype(jnp.bfloat16))
-    sent_gate = send.gate(
-        jnp.concatenate(
-            [
-                dot_tn(ffn_all, grad_gate).astype(jnp.bfloat16),
-                dot_tn(ffn_all, grad_upward).astype(jnp.bfloat16),
-            ],
-            axis=1,
-        )
-    )
-    grad_normed_ffn = sum_halves(
-        lambda part: dot_nt(grad_gate[part], w_gate) + dot_nt(grad_upward[part], w_upward), rows
-    )
+    mine, other = both_halves(low(upstream))
+    grad_down = hooks.start(mine), other
+    grad_down = hooks.after_down(hooks.after(grad_down[0], send.down(inner, grad_down))), grad_down[1]
+    grad_wide = hooks.before_wide(gated_back(grad_down, w_down, gate_pre, upward_pre, place))
+    grad_wide = hooks.after_wide(hooks.after(grad_wide, send.wide(normed_ffn, grad_wide)))
+    grad_normed_ffn = sum_halves(lambda part: dot_nt(grad_wide[part], w_wide), rows)
     grad_part_ffn, grad_gain_ffn = norm_back(middle, factor_ffn, gain_ffn, grad_normed_ffn)
     grad_middle = upstream + grad_part_ffn
-    grad_branch_all = both_halves(grad_middle.astype(jnp.bfloat16))
-    grad_attended = dot_nt(grad_branch_all, w_proj).astype(jnp.bfloat16)
-    sent_proj = send.proj(dot_tn(attended, grad_branch_all).astype(jnp.bfloat16))
-    grad_qkv, passed = attend_back(kept, grad_attended, lse, extra, tables, half)
-    sent_qkv = send.qkv(dot_tn(normed_all, grad_qkv).astype(jnp.bfloat16))
-    grad_normed = sum_halves(lambda part: dot_nt(grad_qkv[part], w_qkv), rows)
+    mine, other = both_halves(low(grad_middle))
+    grad_branch = hooks.before_branch(mine), other
+    mine, other = (low(dot_nt(g, w_proj)) for g in grad_branch)
+    mine = hooks.before_attention(hooks.after(mine, send.proj(attended, grad_branch)))
+    grad_qkv, passed = attend_back(kept, (mine, other), lse, extra, tables, place[1:])
+    grad_qkv = hooks.before_qkv(grad_qkv)
+    grad_qkv = hooks.after_qkv(hooks.after(grad_qkv, send.qkv(normed, grad_qkv)))
+    grad_normed = sum_halves(lambda part: dot_nt(grad_qkv[part], w_qkv), rows, hooks.before_norm)
     grad_part_attn, grad_gain_attn = norm_back(flat, factor_attn, gain_attn, grad_normed)
-    grad_flat = grad_middle + grad_part_attn
-    grads = send.finish(sent_qkv, sent_proj, sent_gate, sent_down)
-    return grad_flat, (grad_gain_attn, grad_gain_ffn), grads, passed
-
-
-class Sender:
-    def __init__(self, sizes, core, rep, tuned):
-        self.sizes, self.core, self.rep = sizes, core, rep
-        self.near = (1, 2) if tuned else None
-        self.far = (2, 1) if tuned else None
-
-    def down(self, grad):
-        return rows_back(grad, self.rep, self.near)
-
-    def proj(self, grad):
-        return rows_back(grad, self.rep, self.near)
-
-    def gate(self, grad):
-        return columns_back(grad, self.sizes, self.rep, self.far)
-
-    def qkv(self, grad):
-        return columns_back(grad, self.sizes, self.rep, self.near)
-
-    def finish(self, qkv, proj, gate, down):
-        q_even, q_odd = finish_columns(qkv, self.sizes, self.core, self.rep, self.near)
-        g_even, g_odd = finish_columns(gate, self.sizes, self.core, self.rep, self.far)
-        grad_qkv = [
-            spread_columns(e, o, self.sizes) for e, o in zip(head_minor(q_even), head_minor(q_odd))
-        ]
-        width = g_even.shape[1] // 2
-        grad_gate = spread_columns(g_even[:, :width], g_odd[:, :width], self.sizes)
-        grad_upward = spread_columns(g_even[:, width:], g_odd[:, width:], self.sizes)
-        joined = finish_rows(jnp.concatenate([proj, down], axis=0), self.rep, self.near)
-        return (*grad_qkv, joined[: proj.shape[0]], grad_gate, grad_upward, joined[proj.shape[0] :])
+    grad_flat = hooks.at_end(grad_middle + grad_part_attn)
+    return grad_flat, (grad_gain_attn, grad_gain_ffn), passed
+
+
+class Hooks:
+    def same(self, value):
+        return value
+
+    start = before_norm = before_branch = after_down = before_wide = after_wide = before_attention = before_qkv = after_qkv = at_end = same
+
+    def after(self, value, other):
+        return value if other is None else tie(value, other)
+
+
+def sum_over(x, axes):
+    for axis in axes:
+        count, mask = lax.axis_size(axis), 1
+        while mask < count:
+            x = x + lax.ppermute(x, axis, [(i, i ^ mask) for i in range(count)])
+            mask *= 2
+    return x
 
 
 def shards(inputs, documents, *rest):
@@ -908,7 +1285,6 @@
     rows_owned = masters_one[1].shape[0]
     tuned = reps == 4 and rows_owned == LANES
     length = sizes[1] * rows
-    half = core.astype(jnp.int32).reshape(1)
     frequencies = rope_base ** (-(jnp.arange(HD // 2, dtype=jnp.float32) * 2.0 / HD))
     angles = jnp.arange(length, dtype=jnp.float32)[:, None] * frequencies[None, :]
     cosine, sine = jnp.cos(angles), jnp.sin(angles)
@@ -935,6 +1311,10 @@
             )
             for u in range(2)
         ]
+        ready = (far_one, near_two, *far_two)
+        near_one, far_one, near_two = gather_shard(near_one), gather_shard(far_one), gather_shard(near_two)
+        far_two = [gather_shard(f) for f in far_two]
+        near_one = tie(near_one, *ready)
         gains = near_one.reshape(sizes[0], -1, FLAT)[:, -16:-12, : 2 * LANES]
         gains = gains.transpose(1, 0, 2).reshape(4, features).astype(jnp.float32)
         quarter, columns = rows_owned // 4 * 2, sizes[0] * LANES
@@ -965,27 +1345,71 @@
     )
     outputs = final.astype(jnp.bfloat16).reshape(batch, rows, features)
     upstream = cotangent.reshape(rows, features).astype(jnp.float32)
-    send = Sender(sizes, core, rep, tuned)
-    grad_middle, gains_two, grads_two, extra = layer_back(
-        upstream, (gains[2:3], gains[3:4]), weights_two, saved_two, None, tables, half, send
+    hooks_two, hooks_one = Hooks(), Hooks()
+    if tuned:
+        two, one = TunedSender(sizes, place, (1, 2), (2, 1)), TunedSender(sizes, place, (1, 2), (2, 1))
+
+        def at(*steps):
+            def hook(value):
+                for step in steps:
+                    done = step(value)
+                    value = tie(value, *(done if isinstance(done, tuple) else (done,)))
+                return value
+
+            return hook
+
+        hooks_two.before_attention = at(two.got("way_wide"))
+        hooks_two.before_qkv = at(two.half("way_wide"), two.half("way_proj", 1))
+        hooks_two.after_qkv = at(two.got("way_wide"), two.got("way_proj"))
+        hooks_one.start = at(two.scatter_wide, two.down_way)
+        hooks_one.after_down = at(two.half("way_qkv"), two.half("way_down", 1))
+        hooks_one.before_wide = at(two.got("way_qkv"), two.got("way_down"))
+        hooks_one.after_wide = at(two.scatter_near)
+        hooks_one.before_attention = at(one.half("way_wide"), one.down_way)
+        hooks_one.before_qkv = at(
+            lambda value: two.near_sum,
+            two.share_far,
+            one.half("way_proj", 1),
+            one.scatter_wide,
+            one.half("way_down", 1),
+        )
+        hooks_one.after_qkv = at(two.far_got, one.got("way_down"))
+        hooks_one.before_norm = at(one.half("way_qkv"))
+    else:
+        two, one = PlainSender(sizes, core), PlainSender(sizes, core)
+    grad_middle, gains_two, extra = layer_back(
+        upstream, (gains[2:3], gains[3:4]), weights_two, saved_two, None, tables, place, two, hooks_two
     )
-    grad_flat, gains_one, grads_one, _ = layer_back(
-        grad_middle, (gains[0:1], gains[1:2]), weights_one, saved_one, extra, tables, half, send
+    grad_flat, gains_one, _ = layer_back(
+        grad_middle, (gains[0:1], gains[1:2]), weights_one, saved_one, extra, tables, place, one, hooks_one
     )
+    gain_grads = jnp.stack([*gains_one, *gains_two])
+    if tuned:
+        gain_total = sum_over(gain_grads, ("shard", "seq", "rep"))
+        value = at(one.got("way_qkv"), one.got("way_proj"), one.share_far, one.scatter_near)(tie(grad_flat, outputs))
+        at(two.pick_far, two.finish_far, two.share_near)(value)
+        one.pick_far(value, two.far[0])
+        two.pick_near(value, two.far[0])
+        at(one.finish_far, two.finish_near, one.share_near)(value)
+        one.pick_near(value, two.near[0], one.far[0], gain_total)
+        one.finish_near(value)
+        near_two, far_two, near_one, far_one = two.near, two.far, one.near, one.far
+    else:
+        gain_total = sum_over(gain_grads, ("shard", "seq", "rep"))
+        near_two, far_two, near_one, far_one = two.near(), two.far(), one.near(), one.far()
     grad_input = grad_flat.reshape(batch, rows, features)
-    gain_total = lax.psum(jnp.stack([*gains_one, *gains_two]), ("rep", "shard", "seq"))
     block = features // (sizes[0] * sizes[1])
     mine = lax.axis_index("shard") * sizes[1] + core
     own = lax.dynamic_slice_in_dim(gain_total, mine * block, block, 1)
 
-    def ordered(gain_attn, gain_ffn, grads):
-        query, key, value, proj, gate, upward, down = grads
+    def ordered(gain_attn, gain_ffn, near, far):
+        (query, key, value, proj), (gate, upward, down) = near, far
         return (gain_attn, query, key, value, proj, gain_ffn, gate, upward, down)
 
     return (
         (outputs, grad_input)
-        + ordered(own[0], own[1], grads_one)
-        + ordered(own[2], own[3], grads_two)
+        + ordered(own[0], own[1], near_one, far_one)
+        + ordered(own[2], own[3], near_two, far_two)
     )
 
 

time: 916 us -> 758 us (0.83)
  Pallas kernels: 174 us -> 339 us
  waiting for transfers between devices: 317 us -> 213 us
  other arithmetic: 82.5 us -> 16.1 us
  matrix products: 130 us -> 66.7 us
  blocking collectives: 51.6 us -> 0 us
  local copies, waits for them, and re-layouts: 73.7 us -> 35.9 us
    pallas_call x2 -> x34, Pallas kernels: 24.5 us -> 188 us  [the longest x4 38.5 us: grad_rows(): call(grad_rows_kernel, [shape_of(groups, rows, width // parts)] * (2 * pa...]
    ppermute x50 -> x52, waiting for transfers between devices: 237 us -> 157 us  [exchange(): return lax.ppermute(x, 'rep', [(i, i ^ mask) for i in range(count)])]
    psum x1 -> x0, blocking collectives: 51.6 us -> none  [shards(): lax.psum(jnp.stack([*gains_one, *gains_two]), ('rep', 'shard', 'seq'))]
    dot_general x10 -> x0, matrix products: 46.9 us -> none  [dot_tn(): lax.dot_general(a, b, (((0,), (0,)), ((), ())), preferred_element_type=jn...]
    reduce_scatter x8 -> x6, waiting for transfers between devices: 39.3 us -> 0.01 us  [scatter_shard(): return lax.psum_scatter(x, 'shard', scatter_dimension=0, tiled=True)]
    convert_element_type x26 -> x3, other arithmetic: 44.6 us -> 7.06 us  [low(): return values.astype(jnp.bfloat16)]
    concatenate x10 -> x0, other arithmetic: 17.7 us -> none  [the longest x4 9.86 us: both_halves(): return jnp.concatenate([mine, swap_cores(mine)], axis=0)]
    squeeze x12 -> x0, local copies, waits for them, and re-layouts: 17.5 us -> none  [the longest x8 13 us: halve_rows(): sent = lax.dynamic_index_in_dim(shaped, 1 - bit, 1, keepdims=False)]
  transfers between devices with their start and end apart: 88 -> 93, of which waited for: 32 -> 43; matrix products, arithmetic and copies ran while one was open for 28% -> 12% of each run, Pallas kernels for 19% -> 38%
where the time goes in v2:
time: 758 us; the launch traced here: 751 us
  Pallas kernels  339 us (45%)
  waiting for transfers between devices  213 us (28%)
  matrix products  66.7 us (9%)
  starting transfers between devices  64.8 us (9%)
  local copies, waits for them, and re-layouts  35.9 us (5%)
  other arithmetic  16.1 us (2%)
  between operations  15.2 us (2%)
    ppermute x52, waiting for transfers between devices, exchange(): return lax.ppermute(x, 'rep', [(i, i ^ mask) for i in range(count)])  157 us
    ppermute x52, starting transfers between devices, exchange(): return lax.ppermute(x, 'rep', [(i, i ^ mask) for i in range(count)])  57.3 us
    pallas_call x2, Pallas kernels, attend_ahead(): pl.pallas_call(functools.partial(ahead_kernel, blocks, mixed), out_shape=...  51.7 us
    dot_general x12, matrix products, dot_nt(): lax.dot_general(a, b, (((1,), (1,)), ((), ())), preferred_element_type=jn...  46.6 us
    pallas_call x2, Pallas kernels, attend_back(): pl.pallas_call(functools.partial(back_kernel, blocks, mixed), out_shape=t...  43.6 us
    all_gather x5, waiting for transfers between devices, gather_shard(): return lax.all_gather(x, 'shard', axis=0, tiled=True)  38.8 us
    pallas_call x4, Pallas kernels, grad_rows(): call(grad_rows_kernel, [shape_of(groups, rows, width // parts)] * (2 * pa...  38.5 us
    pallas_call x6, Pallas kernels, join(): pl.pallas_call(functools.partial(join_kernel, masks, parts, cores), out_s...  29.7 us
  transfers between devices with their start and end apart: 93, of which 43 were waited for; matrix products, arithmetic and copies ran while one was open for 12% of the time, Pallas kernels for 38%

profile of v2, /device:TPU:0, one launch (start us, length us, event | category | flops | bytes accessed | tf_op | source)
XLA Modules:
  0.0 751.1 jit_solution(5455988882683099590)
XLA Ops:
  43.6 3.1 all-gather.6.cloned.1.call-done
  49.8 23.2 %collective-permute-done.6 = bf16[1088,512]{1,0:T(8,128)(2,1)S(1)} collective-permute-done((bf16[1088,512]{1,0:T(8,128)(2,1)}, bf16[1088,512]{1,0:T(8,128)(2,1)S(1)}, u32[]{:S(2)}, u32[]{:S(2)}) %collective-permute-start.6) | collective-permute-done | bytes 1114144 | tf_op jit(solution)/shard_map/ppermute | solution.py:271
  76.1 19.5 %all-gather.10.cloned.1.call-done = bf16[2112,512]{1,0:T(8,128)(2,1)} async-done(((bf16[528,512]{1,0:T(8,128)(2,1)}), bf16[2112,512]{1,0:T(8,128)(2,1)}) %all-gather.10.cloned.1.call-update) | async-done | bytes 2162704 | tf_op jit(solution)/shard_map/all_gather | solution.py:396
  95.6 2.9 collective-permute-done.8
  109.2 4.7 join.6
  114.0 25.6 %attend_ahead.2 = (bf16[1024,1536]{1,0:T(8,128)(2,1)}, bf16[1024,512]{1,0:T(8,128)(2,1)S(1)}, f32[4,2,1024]{2,1,0:T(2,128)S(1)}) custom-call(s32[1]{0:T(128)} %bitcast.1.half_ref, bf16[512,1024]{1,0:T(8,128)(2,1)S(1)} %fusion.10.mine_ref.mine, bf16[512,1024]{1,0:T(8,128)(2,1)} %collective-permute-done.5.other_ref.other, bf16[1024,1536]{1,0:T(8,128)(2,1)} %bitcast.127, ...), custom_call_target="tpu_custom_call" | custom-call | tf_op jit(solution)/shard_map/attend_ahead/pallas_call | solution.py:205
  140.5 7.7 %collective-permute-done.12 = bf16[704,512]{1,0:T(8,128)(2,1)} collective-permute-done((bf16[704,512]{1,0:T(8,128)(2,1)S(1)}, bf16[704,512]{1,0:T(8,128)(2,1)}, u32[]{:S(2)}, u32[]{:S(2)}) %collective-permute-start.12) | collective-permute-done | bytes 720928 | tf_op jit(solution)/shard_map/ppermute | solution.py:271
  160.3 17.7 %collective-permute-done.16 = bf16[1024,512]{1,0:T(8,128)(2,1)} collective-permute-done((bf16[1024,512]{1,0:T(8,128)(2,1)}, bf16[1024,512]{1,0:T(8,128)(2,1)}, u32[]{:S(2)}, u32[]{:S(2)}) %collective-permute-start.16) | collective-permute-done | bytes 1048608 | tf_op jit(solution)/shard_map/ppermute | solution.py:271
  179.4 7.6 %collective-permute-done.15 = bf16[1408,512]{1,0:T(8,128)(2,1)} collective-permute-done((bf16[1408,512]{1,0:T(8,128)(2,1)}, bf16[1408,512]{1,0:T(8,128)(2,1)}, u32[]{:S(2)}, u32[]{:S(2)}) %collective-permute-start.15) | collective-permute-done | bytes 1441824 | tf_op jit(solution)/shard_map/ppermute | solution.py:271
  187.0 5.6 join.7
  192.6 12.1 %gated.2 = (bf16[1024,1408]{1,0:T(8,128)(2,1)}, bf16[1024,1408]{1,0:T(8,128)(2,1)}, bf16[1024,1408]{1,0:T(8,128)(2,1)}) custom-call(s32[2]{0:T(128)} %pad_add_fusion.place_ref.none_ref, bf16[512,1024]{1,0:T(8,128)(2,1)} %copy-done.27, bf16[512,1024]{1,0:T(8,128)(2,1)} %collective-permute-done.14.other, bf16[1024,2816]{1,0:T(8,128)(2,1)} %bitcast.109), custom_call_target="tpu_custom_call" | custom-call | tf_op jit(solution)/shard_map/gated/pallas_call | solution.py:582
  204.7 16.2 %all-gather.14.cloned.1.call-done = bf16[2112,512]{1,0:T(8,128)(2,1)} async-done(((bf16[528,512]{1,0:T(8,128)(2,1)}), bf16[2112,512]{1,0:T(8,128)(2,1)}) %all-gather.14.cloned.1.call-update) | async-done | bytes 2162704 | tf_op jit(solution)/shard_map/all_gather | solution.py:396
  221.8 4.4 join.8
  226.2 4.2 convolution_convert_fusion.1
  239.1 5.1 join.9
  244.2 26.1 %attend_ahead.3 = (bf16[1024,1536]{1,0:T(8,128)(2,1)}, bf16[1024,512]{1,0:T(8,128)(2,1)S(1)}, f32[4,2,1024]{2,1,0:T(2,128)S(1)}) custom-call(s32[1]{0:T(128)} %bitcast.1.half_ref, bf16[512,1024]{1,0:T(8,128)(2,1)S(1)} %multiply_convert_fusion.1.mine_ref.mine, bf16[512,1024]{1,0:T(8,128)(2,1)} %collective-permute-done.21.other_ref.other, ...), custom_call_target="tpu_custom_call" | custom-call | tf_op jit(solution)/shard_map/attend_ahead/pallas_call | solution.py:205
  281.1 5.6 join.10
  286.7 12.2 %gated.3 = (bf16[1024,1408]{1,0:T(8,128)(2,1)}, bf16[1024,1408]{1,0:T(8,128)(2,1)}, bf16[1024,1408]{1,0:T(8,128)(2,1)}) custom-call(s32[2]{0:T(128)} %pad_add_fusion.place_ref.none_ref, bf16[512,1024]{1,0:T(8,128)(2,1)} %copy-done.28, bf16[512,1024]{1,0:T(8,128)(2,1)} %collective-permute-done.25.other, bf16[1024,2816]{1,0:T(8,128)(2,1)} %bitcast.112), custom_call_target="tpu_custom_call" | custom-call | tf_op jit(solution)/shard_map/gated/pallas_call | solution.py:582
  298.9 7.6 %grad_whole.2 = bf16[1408,1024]{1,0:T(8,128)(2,1)} custom-call(s32[2]{0:T(128)} %pad_add_fusion.place_ref.none_ref, bf16[1024,1408]{1,0:T(8,128)(2,1)} %get-tuple-element.213.refs_4_.left, bf16[512,1024]{1,0:T(8,128)(2,1)} %bitcast.54.mine, bf16[512,1024]{1,0:T(8,128)(2,1)} %collective-permute-done.29.other), custom_call_target="tpu_custom_call" | custom-call | tf_op jit(solution)/shard_map/grad_whole/pallas_call | solution.py:657
  306.5 4.3 join.11
  310.7 10.8 %gated_back.2.right = bf16[1024,2816]{1,0:T(8,128)(2,1)} custom-call(s32[2]{0:T(128)} %pad_add_fusion.place_ref.none_ref, bf16[512,1024]{1,0:T(8,128)(2,1)} %bitcast.54.mine, bf16[512,1024]{1,0:T(8,128)(2,1)} %collective-permute-done.29.other, bf16[1408,1024]{1,0:T(8,128)(2,1)} %bitcast.117, bf16[1024,1408]{1,0:T(8,128)(2,1)} %get-tuple-element.216.gate, ...), custom_call_target="tpu_custom_call" | custom-call | tf_op jit(solution)/shard_map/gated_back/pallas_call | solution.py:606
  321.6 11.4 %grad_rows.4 = (bf16[8,64,1408]{2,1,0:T(8,128)(2,1)}, bf16[8,64,1408]{2,1,0:T(8,128)(2,1)}, bf16[8,64,1408]{2,1,0:T(8,128)(2,1)}, bf16[8,64,1408]{2,1,0:T(8,128)(2,1)}) custom-call(s32[2]{0:T(128)} %pad_add_fusion.3.bits_ref.none_ref, bf16[512,1024]{1,0:T(8,128)(2,1)} %copy-done.28, bf16[512,1024]{1,0:T(8,128)(2,1)} %collective-permute-done.25.other, ...), custom_call_target="tpu_custom_call" | custom-call | tf_op jit(solution)/shard_map/grad_rows/pallas_call | solution.py:638
  332.9 6.8 fusion.34
  342.7 3.5 multiply_reduce_fusion
  346.2 3.2 fusion.63
  352.3 5.7 grad_columns.2
  361.0 13.2 %collective-permute-done.32.refs_1_ = bf16[8,64,1408]{2,1,0:T(8,128)(2,1)} collective-permute-done((bf16[8,64,1408]{2,1,0:T(8,128)(2,1)}, bf16[8,64,1408]{2,1,0:T(8,128)(2,1)}, u32[]{:S(2)}, u32[]{:S(2)}) %collective-permute-start.32) | collective-permute-done | bytes 1441824 | tf_op jit(solution)/shard_map/ppermute | solution.py:271
  375.9 21.6 %attend_back.2 = (bf16[1024,1536]{1,0:T(8,128)(2,1)}, f32[1024,512]{1,0:T(8,128)S(1)}) custom-call(s32[1]{0:T(128)} %bitcast.1.half_ref, bf16[1024,1536]{1,0:T(8,128)(2,1)} %get-tuple-element.220.kept_ref, bf16[512,512]{1,0:T(8,128)(2,1)S(1)} %convolution_convert_fusion.7.mine_ref, bf16[512,512]{1,0:T(8,128)(2,1)S(1)} %convolution_convert_fusion.6.other_ref, ...), custom_call_target="tpu_custom_call" | custom-call | tf_op jit(solution)/shard_map/attend_back/pallas_call | solution.py:240
  398.9 4.6 halve.8
  410.5 7.8 %grad_rows.5 = (bf16[8,64,768]{2,1,0:T(8,128)(2,1)}, bf16[8,64,768]{2,1,0:T(8,128)(2,1)}, bf16[8,64,768]{2,1,0:T(8,128)(2,1)}, bf16[8,64,768]{2,1,0:T(8,128)(2,1)}) custom-call(s32[2]{0:T(128)} %pad_add_fusion.4.bits_ref.none_ref, bf16[512,1024]{1,0:T(8,128)(2,1)} %copy-done.1, bf16[512,1024]{1,0:T(8,128)(2,1)} %collective-permute-done.21.other_ref.other, ...), custom_call_target="tpu_custom_call" | custom-call | tf_op jit(solution)/shard_map/grad_rows/pallas_call | solution.py:638
  420.4 3.9 collective-permute-done.36.refs_3_
  424.3 2.9 collective-permute-done.37.refs_5_
  427.2 3.3 fusion.40
  437.5 4.6 flatten.4
  444.0 7.5 %grad_whole.3 = bf16[1408,1024]{1,0:T(8,128)(2,1)} custom-call(s32[2]{0:T(128)} %pad_add_fusion.place_ref.none_ref, bf16[1024,1408]{1,0:T(8,128)(2,1)} %get-tuple-element.204.refs_4_.left, bf16[512,1024]{1,0:T(8,128)(2,1)} %copy-done.26, bf16[512,1024]{1,0:T(8,128)(2,1)} %collective-permute-done.39.other), custom_call_target="tpu_custom_call" | custom-call | tf_op jit(solution)/shard_map/grad_whole/pallas_call | solution.py:657
  454.7 17.0 %collective-permute-done.40.refs_1_ = bf16[8,64,768]{2,1,0:T(8,128)(2,1)S(1)} collective-permute-done((bf16[8,64,768]{2,1,0:T(8,128)(2,1)}, bf16[8,64,768]{2,1,0:T(8,128)(2,1)S(1)}, u32[]{:S(2)}, u32[]{:S(2)}) %collective-permute-start.40) | collective-permute-done | bytes 786464 | tf_op jit(solution)/shard_map/ppermute | solution.py:271
  473.9 3.5 halve.10
  485.1 10.8 %gated_back.3.right = bf16[1024,2816]{1,0:T(8,128)(2,1)} custom-call(s32[2]{0:T(128)} %pad_add_fusion.place_ref.none_ref, bf16[512,1024]{1,0:T(8,128)(2,1)} %copy-done.26, bf16[512,1024]{1,0:T(8,128)(2,1)} %collective-permute-done.39.other, bf16[1408,1024]{1,0:T(8,128)(2,1)} %bitcast.121, bf16[1024,1408]{1,0:T(8,128)(2,1)} %get-tuple-element.261.gate, ...), custom_call_target="tpu_custom_call" | custom-call | tf_op jit(solution)/shard_map/gated_back/pallas_call | solution.py:606
  496.0 11.3 %grad_rows.6 = (bf16[8,64,1408]{2,1,0:T(8,128)(2,1)}, bf16[8,64,1408]{2,1,0:T(8,128)(2,1)}, bf16[8,64,1408]{2,1,0:T(8,128)(2,1)}, bf16[8,64,1408]{2,1,0:T(8,128)(2,1)}) custom-call(s32[2]{0:T(128)} %pad_add_fusion.3.bits_ref.none_ref, bf16[512,1024]{1,0:T(8,128)(2,1)} %copy-done.27, bf16[512,1024]{1,0:T(8,128)(2,1)} %collective-permute-done.14.other, ...), custom_call_target="tpu_custom_call" | custom-call | tf_op jit(solution)/shard_map/grad_rows/pallas_call | solution.py:638
  507.3 4.2 flatten.5
  511.6 7.7 %fusion.37 = bf16[512,1024]{1,0:T(8,128)(2,1)} fusion(bf16[1024,2816]{1,0:T(8,128)(2,1)} %bitcast.110, bf16[1024,2816]{1,0:T(8,128)(2,1)} %gated_back.3.right), kind=kOutput, calls=%fused_computation.55 | convolution fusion | flops 2953314304 | bytes 9699328 | tf_op jit(solution)/shard_map/dot_general | solution.py:1089
  522.2 8.3 %multiply_reduce_fusion.2 = (f32[1024]{0:T(1024)}, f32[512]{0:T(512)S(1)}, f32[512,1024]{1,0:T(8,128)S(1)}) fusion(f32[512,1024]{1,0:T(8,128)} %copy-done.15, f32[512]{0:T(512)S(1)} %get-tuple-element.377, f32[1024]{0:T(1024)S(1)} %bitcast.161, bf16[512,1024]{1,0:T(8,128)(2,1)S(1)} %collective-permute-done.46, bf16[1024,2816]{1,0:T(8,128)(2,1)} %bitcast.111, ...), kind=kOutput, calls=%fused_computation.26 | convolution fusion | flops 2956982784 | bytes 13905920 | tf_op jit(solution)/shard_map/dot_general | solution.py:1089
  536.0 5.0 grad_columns.3
  541.0 12.7 %collective-permute-done.48.refs_1_ = bf16[8,64,1408]{2,1,0:T(8,128)(2,1)S(1)} collective-permute-done((bf16[8,64,1408]{2,1,0:T(8,128)(2,1)}, bf16[8,64,1408]{2,1,0:T(8,128)(2,1)S(1)}, u32[]{:S(2)}, u32[]{:S(2)}) %collective-permute-start.48) | collective-permute-done | bytes 1441824 | tf_op jit(solution)/shard_map/ppermute | solution.py:271
  554.7 4.6 halve.12
  567.4 22.0 %attend_back.3.right = bf16[1024,1536]{1,0:T(8,128)(2,1)} custom-call(s32[1]{0:T(128)} %bitcast.1.half_ref, bf16[1024,1536]{1,0:T(8,128)(2,1)} %get-tuple-element.208.rest_0_.kept_ref, bf16[512,512]{1,0:T(8,128)(2,1)S(1)} %convolution_convert_fusion.5.mine_ref, bf16[512,512]{1,0:T(8,128)(2,1)S(1)} %convolution_convert_fusion.4.other_ref, ...), custom_call_target="tpu_custom_call" | custom-call | tf_op jit(solution)/shard_map/attend_back/pallas_call | solution.py:240
  598.2 4.6 flatten.6
  607.0 4.0 convolution_convert_fusion
  611.2 8.2 %grad_rows.7 = (bf16[8,64,768]{2,1,0:T(8,128)(2,1)}, bf16[8,64,768]{2,1,0:T(8,128)(2,1)}, bf16[8,64,768]{2,1,0:T(8,128)(2,1)}, bf16[8,64,768]{2,1,0:T(8,128)(2,1)}) custom-call(s32[2]{0:T(128)} %pad_add_fusion.4.bits_ref.none_ref, bf16[512,1024]{1,0:T(8,128)(2,1)} %copy-done, bf16[512,1024]{1,0:T(8,128)(2,1)} %collective-permute-done.5.other_ref.other, ...), custom_call_target="tpu_custom_call" | custom-call | tf_op jit(solution)/shard_map/grad_rows/pallas_call | solution.py:638
  620.8 4.6 fusion.43
  628.1 4.2 fusion.50
  632.9 12.7 %collective-permute-done.59.refs_1_ = bf16[8,64,768]{2,1,0:T(8,128)(2,1)} collective-permute-done((bf16[8,64,768]{2,1,0:T(8,128)(2,1)S(1)}, bf16[8,64,768]{2,1,0:T(8,128)(2,1)}, u32[]{:S(2)}, u32[]{:S(2)}) %collective-permute-start.59) | collective-permute-done | bytes 786464 | tf_op jit(solution)/shard_map/ppermute | solution.py:271
  647.1 3.5 halve.15
  653.2 3.5 fusion.17
  664.2 4.2 flatten.7
  668.4 3.3 pick.4
  676.3 10.1 %collective-permute-done.77.refs_1_ = bf16[528,512]{1,0:T(8,128)(2,1)S(1)} collective-permute-done((bf16[528,512]{1,0:T(8,128)(2,1)S(1)}, bf16[528,512]{1,0:T(8,128)(2,1)S(1)}, u32[]{:S(2)}, u32[]{:S(2)}) %collective-permute-start.77) | collective-permute-done | bytes 540704 | tf_op jit(solution)/shard_map/ppermute | solution.py:271
  690.3 5.0 finish_far.2
  695.3 4.6 collective-permute-done.79.refs_3_
  700.7 3.1 pick.6
  705.5 5.0 collective-permute-done.74.refs_3_
  725.4 3.4 finish_near.2
  729.7 5.0 finish_far.3
  740.9 3.4 finish_near.3
  (447 shorter events, 210.3 us)
Async XLA Ops:
  7.2 39.6 %all-gather.6.cloned.1.call-start = ((), (), s32[]{:S(2)}) async-start(), calls=%async_computation.6 | async-start | bytes 1392640 | tf_op jit(solution)/shard_map/all_gather | solution.py:396
  15.0 80.7 %all-gather.10.cloned.1.call-start = ((), (), s32[]{:S(2)}) async-start(), calls=%async_computation.8 | async-start | bytes 2703360 | tf_op jit(solution)/shard_map/all_gather | solution.py:396
  22.7 117.9 %all-gather.8.cloned.1.call-start = ((), (), s32[]{:S(2)}) async-start(), calls=%async_computation.7 | async-start | bytes 1310720 | tf_op jit(solution)/shard_map/all_gather | solution.py:396
  29.7 149.7 %all-gather.12.cloned.1.call-start = ((), (), s32[]{:S(2)}) async-start(), calls=%async_computation.9 | async-start | bytes 2703360 | tf_op jit(solution)/shard_map/all_gather | solution.py:396
  46.7 26.3 %collective-permute-start.6 = (bf16[1088,512]{1,0:T(8,128)(2,1)}, bf16[1088,512]{1,0:T(8,128)(2,1)S(1)}, u32[]{:S(2)}, u32[]{:S(2)}) collective-permute-start(bf16[1088,512]{1,0:T(8,128)(2,1)} %all-gather.6.cloned.1.call-done), channel_id=1, source_target_pairs={{0,8},{8,0},{16,24},{24,16},{1,9},{9,1},{17,25},{25,17},{2,10},{10... | collective-permute-start | bytes 3342344 | tf_op jit(solution)/shard_map/ppermute | solution.py:271
  48.2 172.7 %all-gather.14.cloned.1.call-start = ((), (), s32[]{:S(2)}) async-start(), calls=%async_computation.10 | async-start | bytes 2703360 | tf_op jit(solution)/shard_map/all_gather | solution.py:396
  48.3 27.9 %collective-permute-start.7 = (bf16[1088,512]{1,0:T(8,128)(2,1)}, bf16[1088,512]{1,0:T(8,128)(2,1)}, u32[]{:S(2)}, u32[]{:S(2)}) collective-permute-start(bf16[1088,512]{1,0:T(8,128)(2,1)} %all-gather.6.cloned.1.call-done), channel_id=1, source_target_pairs={{0,16},{8,24},{16,0},{24,8},{1,17},{9,25},{17,1},{25,9},{2,18},{10... | collective-permute-start | bytes 3342344 | tf_op jit(solution)/shard_map/ppermute | solution.py:271
  73.1 25.4 %collective-permute-start.8 = (bf16[1088,512]{1,0:T(8,128)(2,1)S(1)}, bf16[1088,512]{1,0:T(8,128)(2,1)}, u32[]{:S(2)}, u32[]{:S(2)}) collective-permute-start(bf16[1088,512]{1,0:T(8,128)(2,1)S(1)} %collective-permute-done.6), channel_id=1, source_target_pairs={{0,16},{8,24},{16,0},{24,8},{1,17},{9,25},{17,1},{25,9},{2,18},{10... | collective-permute-start | bytes 3342344 | tf_op jit(solution)/shard_map/ppermute | solution.py:271
  101.1 48.4 %collective-permute-start.9 = (bf16[1408,512]{1,0:T(8,128)(2,1)}, bf16[1408,512]{1,0:T(8,128)(2,1)}, u32[]{:S(2)}, u32[]{:S(2)}) collective-permute-start(bf16[1408,512]{1,0:T(8,128)(2,1)} %bitcast.21), channel_id=1, source_target_pairs={{0,16},{8,24},{16,0},{24,8},{1,17},{9,25},{17,1},{25,9},{2,18},{10... | collective-permute-start | bytes 4325384 | tf_op jit(solution)/shard_map/ppermute | solution.py:271
  102.5 46.9 %collective-permute-start.10 = (bf16[1408,512]{1,0:T(8,128)(2,1)}, bf16[1408,512]{1,0:T(8,128)(2,1)}, u32[]{:S(2)}, u32[]{:S(2)}) collective-permute-start(bf16[1408,512]{1,0:T(8,128)(2,1)} %bitcast.21), channel_id=1, source_target_pairs={{0,8},{8,0},{16,24},{24,16},{1,9},{9,1},{17,25},{25,17},{2,10},{10... | collective-permute-start | bytes 4325384 | tf_op jit(solution)/shard_map/ppermute | solution.py:271
  105.9 42.3 %collective-permute-start.12 = (bf16[704,512]{1,0:T(8,128)(2,1)S(1)}, bf16[704,512]{1,0:T(8,128)(2,1)}, u32[]{:S(2)}, u32[]{:S(2)}) collective-permute-start(bf16[704,512]{1,0:T(8,128)(2,1)S(1)} %bitcast.133), channel_id=1, source_target_pairs={{0,16},{8,24},{16,0},{24,8},{1,17},{9,25},{17,1},{25,9},{2,18},{10... | collective-permute-start | bytes 2162696 | tf_op jit(solution)/shard_map/ppermute | solution.py:271
  106.6 42.9 %collective-permute-start.11 = (bf16[704,512]{1,0:T(8,128)(2,1)S(1)}, bf16[704,512]{1,0:T(8,128)(2,1)}, u32[]{:S(2)}, u32[]{:S(2)}) collective-permute-start(bf16[704,512]{1,0:T(8,128)(2,1)S(1)} %bitcast.134), channel_id=1, source_target_pairs={{0,8},{8,0},{16,24},{24,16},{1,9},{9,1},{17,25},{25,17},{2,10},{10... | collective-permute-start | bytes 2162696 | tf_op jit(solution)/shard_map/ppermute | solution.py:271
  108.6 333.5 %reduce-scatter.7.cloned.1.call-start = ((), (), s32[]{:S(2)}) async-start(), calls=%async_computation.11 | async-start | bytes 3604480 | tf_op jit(solution)/shard_map/reduce_scatter | solution.py:1057
  151.6 26.3 %collective-permute-start.16 = (bf16[1024,512]{1,0:T(8,128)(2,1)}, bf16[1024,512]{1,0:T(8,128)(2,1)}, u32[]{:S(2)}, u32[]{:S(2)}) collective-permute-start(bf16[1024,512]{1,0:T(8,128)(2,1)} %all-gather.8.cloned.1.call-done), channel_id=1, source_target_pairs={{0,16},{8,24},{16,0},{24,8},{1,17},{9,25},{17,1},{25,9},{2,18},{10... | collective-permute-start | bytes 3145736 | tf_op jit(solution)/shard_map/ppermute | solution.py:271
  152.3 34.7 %collective-permute-start.15 = (bf16[1408,512]{1,0:T(8,128)(2,1)}, bf16[1408,512]{1,0:T(8,128)(2,1)}, u32[]{:S(2)}, u32[]{:S(2)}) collective-permute-start(bf16[1408,512]{1,0:T(8,128)(2,1)} %collective-permute-done.9), channel_id=1, source_target_pairs={{0,8},{8,0},{16,24},{24,16},{1,9},{9,1},{17,25},{25,17},{2,10},{10... | collective-permute-start | bytes 4325384 | tf_op jit(solution)/shard_map/ppermute | solution.py:271
  158.0 34.6 %collective-permute-start.14 = (bf16[512,1024]{1,0:T(8,128)(2,1)S(1)}, bf16[512,1024]{1,0:T(8,128)(2,1)}, u32[]{:S(2)}, u32[]{:S(2)}) collective-permute-start(bf16[512,1024]{1,0:T(8,128)(2,1)S(1)} %multiply_convert_fusion.2.mine), channel_id=1, source_target_pairs={{0,1},{1,0},{2,3},{3,2},{4,5},{5,4},{6,7},{7,6},{8,9},{9,8},{10,11... | collective-permute-start | bytes 3145736 | tf_op jit(solution)/shard_map/ppermute | solution.py:266
  158.2 62.7 %collective-permute-start.17 = (bf16[1024,512]{1,0:T(8,128)(2,1)}, bf16[1024,512]{1,0:T(8,128)(2,1)}, u32[]{:S(2)}, u32[]{:S(2)}) collective-permute-start(bf16[1024,512]{1,0:T(8,128)(2,1)} %all-gather.8.cloned.1.call-done), channel_id=1, source_target_pairs={{0,8},{8,0},{16,24},{24,16},{1,9},{9,1},{17,25},{25,17},{2,10},{10... | collective-permute-start | bytes 3145736 | tf_op jit(solution)/shard_map/ppermute | solution.py:271
  159.7 61.2 %collective-permute-start.18 = (bf16[704,512]{1,0:T(8,128)(2,1)}, bf16[704,512]{1,0:T(8,128)(2,1)S(1)}, u32[]{:S(2)}, u32[]{:S(2)}) collective-permute-start(bf16[704,512]{1,0:T(8,128)(2,1)} %collective-permute-done.11), channel_id=1, source_target_pairs={{0,16},{8,24},{16,0},{24,8},{1,17},{9,25},{17,1},{25,9},{2,18},{10... | collective-permute-start | bytes 2162696 | tf_op jit(solution)/shard_map/ppermute | solution.py:271
  178.0 56.5 %collective-permute-start.20 = (bf16[1024,512]{1,0:T(8,128)(2,1)}, bf16[1024,512]{1,0:T(8,128)(2,1)}, u32[]{:S(2)}, u32[]{:S(2)}) collective-permute-start(bf16[1024,512]{1,0:T(8,128)(2,1)} %collective-permute-done.16), channel_id=1, source_target_pairs={{0,8},{8,0},{16,24},{24,16},{1,9},{9,1},{17,25},{25,17},{2,10},{10... | collective-permute-start | bytes 3145736 | tf_op jit(solution)/shard_map/ppermute | solution.py:271
  233.0 37.3 %collective-permute-start.23 = (bf16[1408,512]{1,0:T(8,128)(2,1)}, bf16[1408,512]{1,0:T(8,128)(2,1)}, u32[]{:S(2)}, u32[]{:S(2)}) collective-permute-start(bf16[1408,512]{1,0:T(8,128)(2,1)} %bitcast.42), channel_id=1, source_target_pairs={{0,16},{8,24},{16,0},{24,8},{1,17},{9,25},{17,1},{25,9},{2,18},{10... | collective-permute-start | bytes 4325384 | tf_op jit(solution)/shard_map/ppermute | solution.py:271
  234.5 35.9 %collective-permute-start.22 = (bf16[1408,512]{1,0:T(8,128)(2,1)}, bf16[1408,512]{1,0:T(8,128)(2,1)}, u32[]{:S(2)}, u32[]{:S(2)}) collective-permute-start(bf16[1408,512]{1,0:T(8,128)(2,1)} %bitcast.40), channel_id=1, source_target_pairs={{0,8},{8,0},{16,24},{24,16},{1,9},{9,1},{17,25},{25,17},{2,10},{10... | collective-permute-start | bytes 4325384 | tf_op jit(solution)/shard_map/ppermute | solution.py:271
  275.2 23.7 %collective-permute-start.29 = (bf16[512,1024]{1,0:T(8,128)(2,1)}, bf16[512,1024]{1,0:T(8,128)(2,1)}, u32[]{:S(2)}, u32[]{:S(2)}) collective-permute-start(bf16[512,1024]{1,0:T(8,128)(2,1)} %bitcast.54.mine), channel_id=1, source_target_pairs={{0,1},{1,0},{2,3},{3,2},{4,5},{5,4},{6,7},{7,6},{8,9},{9,8},{10,11... | collective-permute-start | bytes 3145736 | tf_op jit(solution)/shard_map/ppermute | solution.py:266
  279.2 27.2 %collective-permute-start.27 = (bf16[704,512]{1,0:T(8,128)(2,1)}, bf16[704,512]{1,0:T(8,128)(2,1)}, u32[]{:S(2)}, u32[]{:S(2)}) collective-permute-start(bf16[704,512]{1,0:T(8,128)(2,1)} %bitcast.50), channel_id=1, source_target_pairs={{0,16},{8,24},{16,0},{24,8},{1,17},{9,25},{17,1},{25,9},{2,18},{10... | collective-permute-start | bytes 2162696 | tf_op jit(solution)/shard_map/ppermute | solution.py:271
  279.8 26.7 %collective-permute-start.26 = (bf16[704,512]{1,0:T(8,128)(2,1)S(1)}, bf16[704,512]{1,0:T(8,128)(2,1)}, u32[]{:S(2)}, u32[]{:S(2)}) collective-permute-start(bf16[704,512]{1,0:T(8,128)(2,1)S(1)} %bitcast.135), channel_id=1, source_target_pairs={{0,8},{8,0},{16,24},{24,16},{1,9},{9,1},{17,25},{25,17},{2,10},{10... | collective-permute-start | bytes 2162696 | tf_op jit(solution)/shard_map/ppermute | solution.py:271
  339.8 34.3 %collective-permute-start.32 = (bf16[8,64,1408]{2,1,0:T(8,128)(2,1)}, bf16[8,64,1408]{2,1,0:T(8,128)(2,1)}, u32[]{:S(2)}, u32[]{:S(2)}) collective-permute-start(bf16[8,64,1408]{2,1,0:T(8,128)(2,1)} %get-tuple-element.218), channel_id=1, source_target_pairs={{0,16},{8,24},{16,0},{24,8},{1,17},{9,25},{17,1},{25,9},{2,18},{10... | collective-permute-start | bytes 4325384 | tf_op jit(solution)/shard_map/ppermute | solution.py:271
  341.2 34.7 %collective-permute-start.33 = (bf16[8,64,1408]{2,1,0:T(8,128)(2,1)}, bf16[8,64,1408]{2,1,0:T(8,128)(2,1)}, u32[]{:S(2)}, u32[]{:S(2)}) collective-permute-start(bf16[8,64,1408]{2,1,0:T(8,128)(2,1)} %get-tuple-element.223), channel_id=1, source_target_pairs={{0,8},{8,0},{16,24},{24,16},{1,9},{9,1},{17,25},{25,17},{2,10},{10... | collective-permute-start | bytes 4325384 | tf_op jit(solution)/shard_map/ppermute | solution.py:271
  349.5 212.6 %reduce-scatter.9.cloned.1.call-start = ((), (), s32[]{:S(2)}) async-start(), calls=%async_computation.12 | async-start | bytes 3604480 | tf_op jit(solution)/shard_map/reduce_scatter | solution.py:1057
  358.0 47.5 %collective-permute-start.34 = (bf16[512,512]{1,0:T(8,128)(2,1)}, bf16[512,512]{1,0:T(8,128)(2,1)S(1)}, u32[]{:S(2)}, u32[]{:S(2)}) collective-permute-start(bf16[512,512]{1,0:T(8,128)(2,1)} %get-tuple-element.221), channel_id=1, source_target_pairs={{0,8},{8,0},{16,24},{24,16},{1,9},{9,1},{17,25},{25,17},{2,10},{10... | collective-permute-start | bytes 1572872 | tf_op jit(solution)/shard_map/ppermute | solution.py:271
  403.6 16.8 %collective-permute-start.35 = (bf16[8,32,1408]{2,1,0:T(8,128)(2,1)}, bf16[8,32,1408]{2,1,0:T(8,128)(2,1)S(1)}, u32[]{:S(2)}, u32[]{:S(2)}) collective-permute-start(bf16[8,32,1408]{2,1,0:T(8,128)(2,1)} %get-tuple-element.231), channel_id=1, source_target_pairs={{0,8},{8,0},{16,24},{24,16},{1,9},{9,1},{17,25},{25,17},{2,10},{10... | collective-permute-start | bytes 2162696 | tf_op jit(solution)/shard_map/ppermute | solution.py:271
  405.0 19.3 %collective-permute-start.36 = (bf16[8,32,1408]{2,1,0:T(8,128)(2,1)}, bf16[8,32,1408]{2,1,0:T(8,128)(2,1)S(1)}, u32[]{:S(2)}, u32[]{:S(2)}) collective-permute-start(bf16[8,32,1408]{2,1,0:T(8,128)(2,1)} %get-tuple-element.232), channel_id=1, source_target_pairs={{0,16},{8,24},{16,0},{24,8},{1,17},{9,25},{17,1},{25,9},{2,18},{10... | collective-permute-start | bytes 2162696 | tf_op jit(solution)/shard_map/ppermute | solution.py:271
  409.0 18.1 %collective-permute-start.37 = (bf16[512,256]{1,0:T(8,128)(2,1)}, bf16[512,256]{1,0:T(8,128)(2,1)S(1)}, u32[]{:S(2)}, u32[]{:S(2)}) collective-permute-start(bf16[512,256]{1,0:T(8,128)(2,1)} %get-tuple-element.236), channel_id=1, source_target_pairs={{0,16},{8,24},{16,0},{24,8},{1,17},{9,25},{17,1},{25,9},{2,18},{10... | collective-permute-start | bytes 786440 | tf_op jit(solution)/shard_map/ppermute | solution.py:271
  451.6 137.8 %reduce-scatter.11.cloned.1.call-start = ((), (), s32[]{:S(2)}) async-start(), calls=%async_computation.13 | async-start | bytes 1310720 | tf_op jit(solution)/shard_map/reduce_scatter | solution.py:1057
  451.6 20.1 %collective-permute-start.40 = (bf16[8,64,768]{2,1,0:T(8,128)(2,1)}, bf16[8,64,768]{2,1,0:T(8,128)(2,1)S(1)}, u32[]{:S(2)}, u32[]{:S(2)}) collective-permute-start(bf16[8,64,768]{2,1,0:T(8,128)(2,1)} %get-tuple-element.238), channel_id=1, source_target_pairs={{0,8},{8,0},{16,24},{24,16},{1,9},{9,1},{17,25},{25,17},{2,10},{10... | collective-permute-start | bytes 2359304 | tf_op jit(solution)/shard_map/ppermute | solution.py:271
  452.7 20.4 %collective-permute-start.41 = (bf16[8,64,768]{2,1,0:T(8,128)(2,1)S(1)}, bf16[8,64,768]{2,1,0:T(8,128)(2,1)S(1)}, u32[]{:S(2)}, u32[]{:S(2)}) collective-permute-start(bf16[8,64,768]{2,1,0:T(8,128)(2,1)S(1)} %copy-done.90), channel_id=1, source_target_pairs={{0,16},{8,24},{16,0},{24,8},{1,17},{9,25},{17,1},{25,9},{2,18},{10... | collective-permute-start | bytes 2359304 | tf_op jit(solution)/shard_map/ppermute | solution.py:271
  453.2 27.5 %collective-permute-start.42 = (bf16[352,512]{1,0:T(8,128)(2,1)S(1)}, bf16[352,512]{1,0:T(8,128)(2,1)S(1)}, u32[]{:S(2)}, u32[]{:S(2)}) collective-permute-start(bf16[352,512]{1,0:T(8,128)(2,1)S(1)} %get-tuple-element.365), channel_id=1, source_target_pairs={{0,16},{8,24},{16,0},{24,8},{1,17},{9,25},{17,1},{25,9},{2,18},{10... | collective-permute-start | bytes 1081352 | tf_op jit(solution)/shard_map/ppermute | solution.py:271
  477.4 18.5 %collective-permute-start.43 = (bf16[8,32,768]{2,1,0:T(8,128)(2,1)}, bf16[8,32,768]{2,1,0:T(8,128)(2,1)S(1)}, u32[]{:S(2)}, u32[]{:S(2)}) collective-permute-start(bf16[8,32,768]{2,1,0:T(8,128)(2,1)} %get-tuple-element.255), channel_id=1, source_target_pairs={{0,16},{8,24},{16,0},{24,8},{1,17},{9,25},{17,1},{25,9},{2,18},{10... | collective-permute-start | bytes 1179656 | tf_op jit(solution)/shard_map/ppermute | solution.py:271
  477.9 18.0 %collective-permute-start.44 = (bf16[8,32,768]{2,1,0:T(8,128)(2,1)}, bf16[8,32,768]{2,1,0:T(8,128)(2,1)S(1)}, u32[]{:S(2)}, u32[]{:S(2)}) collective-permute-start(bf16[8,32,768]{2,1,0:T(8,128)(2,1)} %get-tuple-element.256), channel_id=1, source_target_pairs={{0,8},{8,0},{16,24},{24,16},{1,9},{9,1},{17,25},{25,17},{2,10},{10... | collective-permute-start | bytes 1179656 | tf_op jit(solution)/shard_map/ppermute | solution.py:271
  511.5 77.8 %reduce-scatter.13.cloned.1.call-start = ((), (), s32[]{:S(2)}) async-start(), calls=%async_computation.14 | async-start | bytes 1802240 | tf_op jit(solution)/shard_map/reduce_scatter | solution.py:1057
  519.3 142.2 %reduce-scatter.15.cloned.1.call-start = ((), (), s32[]{:S(2)}) async-start(), calls=%async_computation.15 | async-start | bytes 1802240 | tf_op jit(solution)/shard_map/reduce_scatter | solution.py:1057
  519.4 34.3 %collective-permute-start.48 = (bf16[8,64,1408]{2,1,0:T(8,128)(2,1)}, bf16[8,64,1408]{2,1,0:T(8,128)(2,1)S(1)}, u32[]{:S(2)}, u32[]{:S(2)}) collective-permute-start(bf16[8,64,1408]{2,1,0:T(8,128)(2,1)} %get-tuple-element.265), channel_id=1, source_target_pairs={{0,16},{8,24},{16,0},{24,8},{1,17},{9,25},{17,1},{25,9},{2,18},{10... | collective-permute-start | bytes 4325384 | tf_op jit(solution)/shard_map/ppermute | solution.py:271
  519.8 34.0 %collective-permute-start.49 = (bf16[8,64,1408]{2,1,0:T(8,128)(2,1)}, bf16[8,64,1408]{2,1,0:T(8,128)(2,1)}, u32[]{:S(2)}, u32[]{:S(2)}) collective-permute-start(bf16[8,64,1408]{2,1,0:T(8,128)(2,1)} %get-tuple-element.280), channel_id=1, source_target_pairs={{0,8},{8,0},{16,24},{24,16},{1,9},{9,1},{17,25},{25,17},{2,10},{10... | collective-permute-start | bytes 4325384 | tf_op jit(solution)/shard_map/ppermute | solution.py:271
  559.3 37.1 %collective-permute-start.51 = (bf16[8,32,1408]{2,1,0:T(8,128)(2,1)}, bf16[8,32,1408]{2,1,0:T(8,128)(2,1)}, u32[]{:S(2)}, u32[]{:S(2)}) collective-permute-start(bf16[8,32,1408]{2,1,0:T(8,128)(2,1)} %get-tuple-element.281), channel_id=1, source_target_pairs={{0,8},{8,0},{16,24},{24,16},{1,9},{9,1},{17,25},{25,17},{2,10},{10... | collective-permute-start | bytes 2162696 | tf_op jit(solution)/shard_map/ppermute | solution.py:271
  560.3 37.9 %collective-permute-start.52 = (bf16[8,32,1408]{2,1,0:T(8,128)(2,1)}, bf16[8,32,1408]{2,1,0:T(8,128)(2,1)}, u32[]{:S(2)}, u32[]{:S(2)}) collective-permute-start(bf16[8,32,1408]{2,1,0:T(8,128)(2,1)} %get-tuple-element.282), channel_id=1, source_target_pairs={{0,16},{8,24},{16,0},{24,8},{1,17},{9,25},{17,1},{25,9},{2,18},{10... | collective-permute-start | bytes 2162696 | tf_op jit(solution)/shard_map/ppermute | solution.py:271
  561.1 31.8 %collective-permute-start.50 = (bf16[512,512]{1,0:T(8,128)(2,1)}, bf16[512,512]{1,0:T(8,128)(2,1)}, u32[]{:S(2)}, u32[]{:S(2)}) collective-permute-start(bf16[512,512]{1,0:T(8,128)(2,1)} %get-tuple-element.274), channel_id=1, source_target_pairs={{0,8},{8,0},{16,24},{24,16},{1,9},{9,1},{17,25},{25,17},{2,10},{10... | collective-permute-start | bytes 1572872 | tf_op jit(solution)/shard_map/ppermute | solution.py:271
  564.1 38.7 %collective-permute-start.53 = (bf16[352,512]{1,0:T(8,128)(2,1)}, bf16[352,512]{1,0:T(8,128)(2,1)S(1)}, u32[]{:S(2)}, u32[]{:S(2)}) collective-permute-start(bf16[352,512]{1,0:T(8,128)(2,1)} %get-tuple-element.363), channel_id=1, source_target_pairs={{0,16},{8,24},{16,0},{24,8},{1,17},{9,25},{17,1},{25,9},{2,18},{10... | collective-permute-start | bytes 1081352 | tf_op jit(solution)/shard_map/ppermute | solution.py:271
  592.0 27.4 %collective-permute-start.54 = (bf16[528,512]{1,0:T(8,128)(2,1)}, bf16[528,512]{1,0:T(8,128)(2,1)S(1)}, u32[]{:S(2)}, u32[]{:S(2)}) collective-permute-start(bf16[528,512]{1,0:T(8,128)(2,1)} %append.2.refs_0_), channel_id=1, source_target_pairs={{0,16},{8,24},{16,0},{24,8},{1,17},{9,25},{17,1},{25,9},{2,18},{10... | collective-permute-start | bytes 1622024 | tf_op jit(solution)/shard_map/ppermute | solution.py:271
  592.8 26.6 %collective-permute-start.55 = (bf16[528,512]{1,0:T(8,128)(2,1)}, bf16[528,512]{1,0:T(8,128)(2,1)S(1)}, u32[]{:S(2)}, u32[]{:S(2)}) collective-permute-start(bf16[528,512]{1,0:T(8,128)(2,1)} %append.2.refs_0_), channel_id=1, source_target_pairs={{0,8},{8,0},{16,24},{24,16},{1,9},{9,1},{17,25},{25,17},{2,10},{10... | collective-permute-start | bytes 1622024 | tf_op jit(solution)/shard_map/ppermute | solution.py:271
  596.5 23.4 %collective-permute-start.56 = (bf16[528,512]{1,0:T(8,128)(2,1)}, bf16[528,512]{1,0:T(8,128)(2,1)S(1)}, u32[]{:S(2)}, u32[]{:S(2)}) collective-permute-start(bf16[528,512]{1,0:T(8,128)(2,1)} %append.2.refs_0_), channel_id=1, source_target_pairs={{0,24},{8,16},{16,8},{24,0},{1,25},{9,17},{17,9},{25,1},{2,26},{10... | collective-permute-start | bytes 1622024 | tf_op jit(solution)/shard_map/ppermute | solution.py:271
  606.1 14.8 %collective-permute-start.57 = (bf16[352,256]{1,0:T(8,128)(2,1)}, bf16[352,256]{1,0:T(8,128)(2,1)S(1)}, u32[]{:S(2)}, u32[]{:S(2)}) collective-permute-start(bf16[352,256]{1,0:T(8,128)(2,1)} %get-tuple-element.302), channel_id=1, source_target_pairs={{0,8},{8,0},{16,24},{24,16},{1,9},{9,1},{17,25},{25,17},{2,10},{10... | collective-permute-start | bytes 540680 | tf_op jit(solution)/shard_map/ppermute | solution.py:271
  611.1 17.0 %collective-permute-start.28 = (bf16[512,1024]{1,0:T(8,128)(2,1)S(1)}, bf16[512,1024]{1,0:T(8,128)(2,1)}, u32[]{:S(2)}, u32[]{:S(2)}) collective-permute-start(bf16[512,1024]{1,0:T(8,128)(2,1)S(1)} %convolution_convert_fusion), channel_id=1, source_target_pairs={{0,1},{1,0},{2,3},{3,2},{4,5},{5,4},{6,7},{7,6},{8,9},{9,8},{10,11... | collective-permute-start | bytes 3145736 | tf_op jit(solution)/shard_map/ppermute | solution.py:266
  611.2 108.7 %reduce-scatter.17.cloned.1.call-start = ((), (), s32[]{:S(2)}) async-start(), calls=%async_computation.16 | async-start | bytes 1310720 | tf_op jit(solution)/shard_map/reduce_scatter | solution.py:1057
  625.5 20.1 %collective-permute-start.59 = (bf16[8,64,768]{2,1,0:T(8,128)(2,1)S(1)}, bf16[8,64,768]{2,1,0:T(8,128)(2,1)}, u32[]{:S(2)}, u32[]{:S(2)}) collective-permute-start(bf16[8,64,768]{2,1,0:T(8,128)(2,1)S(1)} %copy-done.92), channel_id=1, source_target_pairs={{0,8},{8,0},{16,24},{24,16},{1,9},{9,1},{17,25},{25,17},{2,10},{10... | collective-permute-start | bytes 2359304 | tf_op jit(solution)/shard_map/ppermute | solution.py:271
  626.6 20.5 %collective-permute-start.60 = (bf16[8,64,768]{2,1,0:T(8,128)(2,1)S(1)}, bf16[8,64,768]{2,1,0:T(8,128)(2,1)}, u32[]{:S(2)}, u32[]{:S(2)}) collective-permute-start(bf16[8,64,768]{2,1,0:T(8,128)(2,1)S(1)} %copy-done.91), channel_id=1, source_target_pairs={{0,16},{8,24},{16,0},{24,8},{1,17},{9,25},{17,1},{25,9},{2,18},{10... | collective-permute-start | bytes 2359304 | tf_op jit(solution)/shard_map/ppermute | solution.py:271
  632.3 29.2 %collective-permute-start.68 = (bf16[512,256]{1,0:T(8,128)(2,1)}, bf16[512,256]{1,0:T(8,128)(2,1)}, u32[]{:S(2)}, u32[]{:S(2)}) collective-permute-start(bf16[512,256]{1,0:T(8,128)(2,1)} %get-tuple-element.294), channel_id=1, source_target_pairs={{0,16},{8,24},{16,0},{24,8},{1,17},{9,25},{17,1},{25,9},{2,18},{10... | collective-permute-start | bytes 786440 | tf_op jit(solution)/shard_map/ppermute | solution.py:271
  671.7 17.7 %collective-permute-start.75 = (bf16[4,192,512]{2,1,0:T(8,128)(2,1)}, bf16[4,192,512]{2,1,0:T(8,128)(2,1)S(1)}, u32[]{:S(2)}, u32[]{:S(2)}) collective-permute-start(bf16[4,192,512]{2,1,0:T(8,128)(2,1)} %pick.4), channel_id=1, source_target_pairs={{0,1},{1,0},{2,3},{3,2},{4,5},{5,4},{6,7},{7,6},{8,9},{9,8},{10,11... | collective-permute-start | bytes 2359304 | tf_op jit(solution)/shard_map/ppermute | solution.py:266
  671.7 14.7 %collective-permute-start.77 = (bf16[528,512]{1,0:T(8,128)(2,1)S(1)}, bf16[528,512]{1,0:T(8,128)(2,1)S(1)}, u32[]{:S(2)}, u32[]{:S(2)}) collective-permute-start(bf16[528,512]{1,0:T(8,128)(2,1)S(1)} %copy-done.32), channel_id=1, source_target_pairs={{0,16},{8,24},{16,0},{24,8},{1,17},{9,25},{17,1},{25,9},{2,18},{10... | collective-permute-start | bytes 1622024 | tf_op jit(solution)/shard_map/ppermute | solution.py:271
  672.3 15.1 %collective-permute-start.78 = (bf16[528,512]{1,0:T(8,128)(2,1)S(1)}, bf16[528,512]{1,0:T(8,128)(2,1)S(1)}, u32[]{:S(2)}, u32[]{:S(2)}) collective-permute-start(bf16[528,512]{1,0:T(8,128)(2,1)S(1)} %copy-done.32), channel_id=1, source_target_pairs={{0,8},{8,0},{16,24},{24,16},{1,9},{9,1},{17,25},{25,17},{2,10},{10... | collective-permute-start | bytes 1622024 | tf_op jit(solution)/shard_map/ppermute | solution.py:271
  673.3 26.6 %collective-permute-start.79 = (bf16[528,512]{1,0:T(8,128)(2,1)S(1)}, bf16[528,512]{1,0:T(8,128)(2,1)S(1)}, u32[]{:S(2)}, u32[]{:S(2)}) collective-permute-start(bf16[528,512]{1,0:T(8,128)(2,1)S(1)} %copy-done.32), channel_id=1, source_target_pairs={{0,24},{8,16},{16,8},{24,0},{1,25},{9,17},{17,9},{25,1},{2,26},{10... | collective-permute-start | bytes 1622024 | tf_op jit(solution)/shard_map/ppermute | solution.py:271
  675.2 29.5 %collective-permute-start.72 = (bf16[256,512]{1,0:T(8,128)(2,1)S(1)}, bf16[256,512]{1,0:T(8,128)(2,1)S(1)}, u32[]{:S(2)}, u32[]{:S(2)}) collective-permute-start(bf16[256,512]{1,0:T(8,128)(2,1)S(1)} %copy-done.52), channel_id=1, source_target_pairs={{0,8},{8,0},{16,24},{24,16},{1,9},{9,1},{17,25},{25,17},{2,10},{10... | collective-permute-start | bytes 786440 | tf_op jit(solution)/shard_map/ppermute | solution.py:271
  686.4 19.0 %collective-permute-start.73 = (bf16[256,512]{1,0:T(8,128)(2,1)S(1)}, bf16[256,512]{1,0:T(8,128)(2,1)S(1)}, u32[]{:S(2)}, u32[]{:S(2)}) collective-permute-start(bf16[256,512]{1,0:T(8,128)(2,1)S(1)} %copy-done.52), channel_id=1, source_target_pairs={{0,16},{8,24},{16,0},{24,8},{1,17},{9,25},{17,1},{25,9},{2,18},{10... | collective-permute-start | bytes 786440 | tf_op jit(solution)/shard_map/ppermute | solution.py:271
  687.4 23.0 %collective-permute-start.74 = (bf16[256,512]{1,0:T(8,128)(2,1)S(1)}, bf16[256,512]{1,0:T(8,128)(2,1)S(1)}, u32[]{:S(2)}, u32[]{:S(2)}) collective-permute-start(bf16[256,512]{1,0:T(8,128)(2,1)S(1)} %copy-done.52), channel_id=1, source_target_pairs={{0,24},{8,16},{16,8},{24,0},{1,25},{9,17},{17,9},{25,1},{2,26},{10... | collective-permute-start | bytes 786440 | tf_op jit(solution)/shard_map/ppermute | solution.py:271
  689.4 14.4 %collective-permute-start.61 = (f32[4,1024]{1,0:T(4,128)S(1)}, f32[4,1024]{1,0:T(4,128)S(1)}, u32[]{:S(2)}, u32[]{:S(2)}) collective-permute-start(f32[4,1024]{1,0:T(4,128)S(1)} %pad_maximum_fusion.1), channel_id=1, source_target_pairs={{0,2},{2,0},{4,6},{6,4},{1,3},{3,1},{5,7},{7,5},{8,10},{10,8},{12,... | collective-permute-start | bytes 49160 | tf_op jit(solution)/shard_map/ppermute | solution.py:1274
  703.8 25.0 %collective-permute-start.80 = (bf16[4,192,512]{2,1,0:T(8,128)(2,1)}, bf16[4,192,512]{2,1,0:T(8,128)(2,1)S(1)}, u32[]{:S(2)}, u32[]{:S(2)}) collective-permute-start(bf16[4,192,512]{2,1,0:T(8,128)(2,1)} %pick.6), channel_id=1, source_target_pairs={{0,1},{1,0},{2,3},{3,2},{4,5},{5,4},{6,7},{7,6},{8,9},{9,8},{10,11... | collective-permute-start | bytes 2359304 | tf_op jit(solution)/shard_map/ppermute | solution.py:266
  719.9 14.9 %collective-permute-start.69 = (bf16[256,512]{1,0:T(8,128)(2,1)}, bf16[256,512]{1,0:T(8,128)(2,1)S(1)}, u32[]{:S(2)}, u32[]{:S(2)}) collective-permute-start(bf16[256,512]{1,0:T(8,128)(2,1)} %reduce-scatter.17.cloned.1.call-done.refs_0_), channel_id=1, source_target_pairs={{0,8},{8,0},{16,24},{24,16},{1,9},{9,1},{17,25},{25,17},{2,10},{10... | collective-permute-start | bytes 786440 | tf_op jit(solution)/shard_map/ppermute | solution.py:271
  (124 other events, 899.9 us)
Sparse Core Ops, SparseCore 0:
  15.1 31.6 all-gather.5
  48.9 46.7 all-gather.9
  97.8 26.6 all-gather.7
  126.5 46.7 all-gather.11
  175.2 45.6 all-gather.13
  349.6 54.7 reduce-scatter.6
  451.7 53.2 reduce-scatter.8
  511.7 24.4 reduce-scatter.10
  539.1 31.8 reduce-scatter.12
  611.3 30.8 reduce-scatter.14
  668.6 24.7 reduce-scatter.16

commit v3 on v2

--- a/solution.py
+++ b/solution.py
@@ -914,8 +914,13 @@
         return self.way_wide.sent[0]
 
     def proj(self, left, right):
-        self.way_proj = Way(grad_columns(left, right, self.near_bits), self.near_plan, self.near_bits)
-        return self.way_proj.sent[0]
+        self.proj_halves = grad_columns(left, right, self.near_bits)
+        return self.proj_halves[0]
+
+    def proj_way(self, value):
+        sent, kept = self.proj_halves
+        self.way_proj = Way([tie(sent, value), kept], self.near_plan, self.near_bits)
+        return ()
 
     def qkv(self, left, right):
         self.way_qkv = Way(grad_rows(left, right, self.groups, self.near_bits, 2), self.near_plan, self.near_bits)
@@ -1358,14 +1363,15 @@
 
             return hook
 
-        hooks_two.before_attention = at(two.got("way_wide"))
+        hooks_two.before_attention = at(two.proj_way)
         hooks_two.before_qkv = at(two.half("way_wide"), two.half("way_proj", 1))
-        hooks_two.after_qkv = at(two.got("way_wide"), two.got("way_proj"))
-        hooks_one.start = at(two.scatter_wide, two.down_way)
-        hooks_one.after_down = at(two.half("way_qkv"), two.half("way_down", 1))
-        hooks_one.before_wide = at(two.got("way_qkv"), two.got("way_down"))
-        hooks_one.after_wide = at(two.scatter_near)
-        hooks_one.before_attention = at(one.half("way_wide"), one.down_way)
+        hooks_one.start = at(two.down_way)
+        hooks_one.after_down = at(two.scatter_wide)
+        hooks_one.before_wide = at(two.half("way_qkv"))
+        hooks_one.after_wide = at(
+            lambda value: two.wide_sum, two.half("way_down", 1), two.scatter_near, two.got("way_down")
+        )
+        hooks_one.before_attention = at(one.proj_way, one.half("way_wide"), one.down_way)
         hooks_one.before_qkv = at(
             lambda value: two.near_sum,
             two.share_far,

time: 758 us -> 745 us (0.983)
  waiting for transfers between devices: 213 us -> 195 us
    ppermute x52, waiting for transfers between devices: 157 us -> 135 us  [exchange(): return lax.ppermute(x, 'rep', [(i, i ^ mask) for i in range(count)])]
    unnamed x190 -> x186, local copies, waits for them, and re-layouts: 20 us -> 20.7 us
  transfers between devices with their start and end apart: 93 -> 93, of which waited for: 43 -> 41; matrix products, arithmetic and copies ran while one was open for 12% -> 13% of each run, Pallas kernels for 38% -> 39%
where the time goes in v3:
time: 745 us; the launch traced here: 738 us
  Pallas kernels  339 us (46%)
  waiting for transfers between devices  195 us (26%)
  matrix products  71.4 us (10%)
  starting transfers between devices  64.5 us (9%)
  local copies, waits for them, and re-layouts  36.7 us (5%)
  other arithmetic  16.2 us (2%)
  between operations  15.2 us (2%)
    ppermute x52, waiting for transfers between devices, exchange(): return lax.ppermute(x, 'rep', [(i, i ^ mask) for i in range(count)])  135 us
    ppermute x52, starting transfers between devices, exchange(): return lax.ppermute(x, 'rep', [(i, i ^ mask) for i in range(count)])  56.7 us
    pallas_call x2, Pallas kernels, attend_ahead(): pl.pallas_call(functools.partial(ahead_kernel, blocks, mixed), out_shape=...  51.6 us
    dot_general x12, matrix products, dot_nt(): lax.dot_general(a, b, (((1,), (1,)), ((), ())), preferred_element_type=jn...  51.3 us
    pallas_call x2, Pallas kernels, attend_back(): pl.pallas_call(functools.partial(back_kernel, blocks, mixed), out_shape=t...  43.7 us
    all_gather x5, waiting for transfers between devices, gather_shard(): return lax.all_gather(x, 'shard', axis=0, tiled=True)  38.7 us
    pallas_call x4, Pallas kernels, grad_rows(): call(grad_rows_kernel, [shape_of(groups, rows, width // parts)] * (2 * pa...  38.6 us
    pallas_call x6, Pallas kernels, join(): pl.pallas_call(functools.partial(join_kernel, masks, parts, cores), out_s...  29.7 us
  transfers between devices with their start and end apart: 93, of which 41 were waited for; matrix products, arithmetic and copies ran while one was open for 13% of the time, Pallas kernels for 39%

profile of v3, /device:TPU:0, one launch (start us, length us, event | category | flops | bytes accessed | tf_op | source)
XLA Modules:
  0.0 737.7 jit_solution(1388156499146102112)
XLA Ops:
  37.5 2.8 far_merge.4
  43.7 3.1 all-gather.6.cloned.1.call-done
  49.9 23.2 %collective-permute-done.6 = bf16[1088,512]{1,0:T(8,128)(2,1)S(1)} collective-permute-done((bf16[1088,512]{1,0:T(8,128)(2,1)}, bf16[1088,512]{1,0:T(8,128)(2,1)S(1)}, u32[]{:S(2)}, u32[]{:S(2)}) %collective-permute-start.6) | collective-permute-done | bytes 1114144 | tf_op jit(solution)/shard_map/ppermute | solution.py:271
  76.2 19.5 %all-gather.10.cloned.1.call-done = bf16[2112,512]{1,0:T(8,128)(2,1)} async-done(((bf16[528,512]{1,0:T(8,128)(2,1)}), bf16[2112,512]{1,0:T(8,128)(2,1)}) %all-gather.10.cloned.1.call-update) | async-done | bytes 2162704 | tf_op jit(solution)/shard_map/all_gather | solution.py:396
  95.7 2.9 collective-permute-done.8
  109.2 4.7 join.6
  114.0 25.5 %attend_ahead.2 = (bf16[1024,1536]{1,0:T(8,128)(2,1)}, bf16[1024,512]{1,0:T(8,128)(2,1)S(1)}, f32[4,2,1024]{2,1,0:T(2,128)S(1)}) custom-call(s32[1]{0:T(128)} %bitcast.1.half_ref, bf16[512,1024]{1,0:T(8,128)(2,1)S(1)} %fusion.10.mine_ref.mine, bf16[512,1024]{1,0:T(8,128)(2,1)} %collective-permute-done.5.other_ref.other, bf16[1024,1536]{1,0:T(8,128)(2,1)} %bitcast.125, ...), custom_call_target="tpu_custom_call" | custom-call | tf_op jit(solution)/shard_map/attend_ahead/pallas_call | solution.py:205
  140.5 7.8 %collective-permute-done.12 = bf16[704,512]{1,0:T(8,128)(2,1)} collective-permute-done((bf16[704,512]{1,0:T(8,128)(2,1)S(1)}, bf16[704,512]{1,0:T(8,128)(2,1)}, u32[]{:S(2)}, u32[]{:S(2)}) %collective-permute-start.12) | collective-permute-done | bytes 720928 | tf_op jit(solution)/shard_map/ppermute | solution.py:271
  160.3 17.7 %collective-permute-done.16 = bf16[1024,512]{1,0:T(8,128)(2,1)} collective-permute-done((bf16[1024,512]{1,0:T(8,128)(2,1)}, bf16[1024,512]{1,0:T(8,128)(2,1)}, u32[]{:S(2)}, u32[]{:S(2)}) %collective-permute-start.16) | collective-permute-done | bytes 1048608 | tf_op jit(solution)/shard_map/ppermute | solution.py:271
  179.5 7.6 %collective-permute-done.15 = bf16[1408,512]{1,0:T(8,128)(2,1)} collective-permute-done((bf16[1408,512]{1,0:T(8,128)(2,1)}, bf16[1408,512]{1,0:T(8,128)(2,1)}, u32[]{:S(2)}, u32[]{:S(2)}) %collective-permute-start.15) | collective-permute-done | bytes 1441824 | tf_op jit(solution)/shard_map/ppermute | solution.py:271
  187.0 5.6 join.7
  192.7 12.1 %gated.2 = (bf16[1024,1408]{1,0:T(8,128)(2,1)}, bf16[1024,1408]{1,0:T(8,128)(2,1)}, bf16[1024,1408]{1,0:T(8,128)(2,1)}) custom-call(s32[2]{0:T(128)} %pad_add_fusion.place_ref.none_ref, bf16[512,1024]{1,0:T(8,128)(2,1)} %copy-done.26, bf16[512,1024]{1,0:T(8,128)(2,1)} %collective-permute-done.14.other, bf16[1024,2816]{1,0:T(8,128)(2,1)} %bitcast.109), custom_call_target="tpu_custom_call" | custom-call | tf_op jit(solution)/shard_map/gated/pallas_call | solution.py:582
  204.8 16.1 %all-gather.14.cloned.1.call-done = bf16[2112,512]{1,0:T(8,128)(2,1)} async-done(((bf16[528,512]{1,0:T(8,128)(2,1)}), bf16[2112,512]{1,0:T(8,128)(2,1)}) %all-gather.14.cloned.1.call-update) | async-done | bytes 2162704 | tf_op jit(solution)/shard_map/all_gather | solution.py:396
  221.8 4.4 join.8
  226.2 4.2 convolution_convert_fusion.1
  239.1 5.1 join.9
  244.2 26.1 %attend_ahead.3 = (bf16[1024,1536]{1,0:T(8,128)(2,1)}, bf16[1024,512]{1,0:T(8,128)(2,1)S(1)}, f32[4,2,1024]{2,1,0:T(2,128)S(1)}) custom-call(s32[1]{0:T(128)} %bitcast.1.half_ref, bf16[512,1024]{1,0:T(8,128)(2,1)S(1)} %multiply_convert_fusion.1.mine_ref.mine, bf16[512,1024]{1,0:T(8,128)(2,1)} %collective-permute-done.21.other_ref.other, ...), custom_call_target="tpu_custom_call" | custom-call | tf_op jit(solution)/shard_map/attend_ahead/pallas_call | solution.py:205
  281.1 5.6 join.10
  286.7 12.1 %gated.3 = (bf16[1024,1408]{1,0:T(8,128)(2,1)}, bf16[1024,1408]{1,0:T(8,128)(2,1)}, bf16[1024,1408]{1,0:T(8,128)(2,1)}) custom-call(s32[2]{0:T(128)} %pad_add_fusion.place_ref.none_ref, bf16[512,1024]{1,0:T(8,128)(2,1)} %copy-done.27, bf16[512,1024]{1,0:T(8,128)(2,1)} %collective-permute-done.25.other, bf16[1024,2816]{1,0:T(8,128)(2,1)} %bitcast.112), custom_call_target="tpu_custom_call" | custom-call | tf_op jit(solution)/shard_map/gated/pallas_call | solution.py:582
  298.8 7.6 %grad_whole.2 = bf16[1408,1024]{1,0:T(8,128)(2,1)} custom-call(s32[2]{0:T(128)} %pad_add_fusion.place_ref.none_ref, bf16[1024,1408]{1,0:T(8,128)(2,1)} %get-tuple-element.212.refs_4_.left, bf16[512,1024]{1,0:T(8,128)(2,1)} %bitcast.54.mine, bf16[512,1024]{1,0:T(8,128)(2,1)} %collective-permute-done.29.other), custom_call_target="tpu_custom_call" | custom-call | tf_op jit(solution)/shard_map/grad_whole/pallas_call | solution.py:657
  306.5 4.3 join.11
  310.8 10.8 %gated_back.2.right = bf16[1024,2816]{1,0:T(8,128)(2,1)} custom-call(s32[2]{0:T(128)} %pad_add_fusion.place_ref.none_ref, bf16[512,1024]{1,0:T(8,128)(2,1)} %bitcast.54.mine, bf16[512,1024]{1,0:T(8,128)(2,1)} %collective-permute-done.29.other, bf16[1408,1024]{1,0:T(8,128)(2,1)} %bitcast.115, bf16[1024,1408]{1,0:T(8,128)(2,1)} %get-tuple-element.215.gate, ...), custom_call_target="tpu_custom_call" | custom-call | tf_op jit(solution)/shard_map/gated_back/pallas_call | solution.py:606
  321.5 11.2 %grad_rows.4 = (bf16[8,64,1408]{2,1,0:T(8,128)(2,1)}, bf16[8,64,1408]{2,1,0:T(8,128)(2,1)}, bf16[8,64,1408]{2,1,0:T(8,128)(2,1)}, bf16[8,64,1408]{2,1,0:T(8,128)(2,1)}) custom-call(s32[2]{0:T(128)} %pad_add_fusion.3.bits_ref.none_ref, bf16[512,1024]{1,0:T(8,128)(2,1)} %copy-done.27, bf16[512,1024]{1,0:T(8,128)(2,1)} %collective-permute-done.25.other, ...), custom_call_target="tpu_custom_call" | custom-call | tf_op jit(solution)/shard_map/grad_rows/pallas_call | solution.py:638
  332.8 7.6 %fusion.34 = bf16[512,1024]{1,0:T(8,128)(2,1)} fusion(bf16[1024,2816]{1,0:T(8,128)(2,1)} %bitcast.113, bf16[1024,2816]{1,0:T(8,128)(2,1)} %gated_back.2.right), kind=kOutput, calls=%fused_computation.54 | convolution fusion | flops 2953314304 | bytes 9699328 | tf_op jit(solution)/shard_map/dot_general | solution.py:1094
  343.3 8.2 %multiply_reduce_fusion = (f32[1024]{0:T(1024)S(1)}, f32[512]{0:T(512)S(1)}, f32[512,1024]{1,0:T(8,128)S(1)}) fusion(f32[512,1024]{1,0:T(8,128)} %copy-done.11, f32[512]{0:T(512)S(1)} %get-tuple-element.379, f32[1024]{0:T(1024)S(1)} %bitcast.165, bf16[512,1024]{1,0:T(8,128)(2,1)S(1)} %collective-permute-done.30, bf16[1024,2816]{1,0:T(8,128)(2,1)} %bitcast.114, ...), kind=kOutput, calls=%fused_computation.24 | convolution fusion | flops 2956982784 | bytes 13905920 | tf_op jit(solution)/shard_map/dot_general | solution.py:1094
  351.5 3.3 fusion.63
  359.1 5.4 grad_columns.2
  367.1 21.6 %attend_back.2 = (bf16[1024,1536]{1,0:T(8,128)(2,1)}, f32[1024,512]{1,0:T(8,128)S(1)}) custom-call(s32[1]{0:T(128)} %bitcast.1.half_ref, bf16[1024,1536]{1,0:T(8,128)(2,1)} %get-tuple-element.219.kept_ref, bf16[512,512]{1,0:T(8,128)(2,1)S(1)} %convolution_convert_fusion.7.mine_ref, bf16[512,512]{1,0:T(8,128)(2,1)S(1)} %convolution_convert_fusion.6.other_ref, ...), custom_call_target="tpu_custom_call" | custom-call | tf_op jit(solution)/shard_map/attend_back/pallas_call | solution.py:240
  392.2 4.6 halve.8
  396.8 4.6 collective-permute-done.34.refs_1_
  404.1 8.0 %grad_rows.5 = (bf16[8,64,768]{2,1,0:T(8,128)(2,1)}, bf16[8,64,768]{2,1,0:T(8,128)(2,1)}, bf16[8,64,768]{2,1,0:T(8,128)(2,1)}, bf16[8,64,768]{2,1,0:T(8,128)(2,1)}) custom-call(s32[2]{0:T(128)} %pad_add_fusion.4.bits_ref.none_ref, bf16[512,1024]{1,0:T(8,128)(2,1)} %copy-done.1, bf16[512,1024]{1,0:T(8,128)(2,1)} %collective-permute-done.21.other_ref.other, ...), custom_call_target="tpu_custom_call" | custom-call | tf_op jit(solution)/shard_map/grad_rows/pallas_call | solution.py:638
  412.1 3.4 fusion.40
  426.5 7.4 grad_whole.3
  433.9 7.2 collective-permute-done.37.refs_1_
  442.4 4.7 flatten.4
  451.1 10.8 %gated_back.3.right = bf16[1024,2816]{1,0:T(8,128)(2,1)} custom-call(s32[2]{0:T(128)} %pad_add_fusion.place_ref.none_ref, bf16[512,1024]{1,0:T(8,128)(2,1)} %copy-done.25, bf16[512,1024]{1,0:T(8,128)(2,1)} %collective-permute-done.36.other, bf16[1408,1024]{1,0:T(8,128)(2,1)} %bitcast.119, bf16[1024,1408]{1,0:T(8,128)(2,1)} %get-tuple-element.247.gate, ...), custom_call_target="tpu_custom_call" | custom-call | tf_op jit(solution)/shard_map/gated_back/pallas_call | solution.py:606
  461.9 5.0 collective-permute-done.39.refs_1_
  470.4 3.5 halve.10
  477.0 11.2 %grad_rows.6 = (bf16[8,64,1408]{2,1,0:T(8,128)(2,1)}, bf16[8,64,1408]{2,1,0:T(8,128)(2,1)}, bf16[8,64,1408]{2,1,0:T(8,128)(2,1)}, bf16[8,64,1408]{2,1,0:T(8,128)(2,1)}) custom-call(s32[2]{0:T(128)} %pad_add_fusion.3.bits_ref.none_ref, bf16[512,1024]{1,0:T(8,128)(2,1)} %copy-done.26, bf16[512,1024]{1,0:T(8,128)(2,1)} %collective-permute-done.14.other, ...), custom_call_target="tpu_custom_call" | custom-call | tf_op jit(solution)/shard_map/grad_rows/pallas_call | solution.py:638
  494.1 4.2 flatten.5
  498.3 7.8 %fusion.37 = bf16[512,1024]{1,0:T(8,128)(2,1)} fusion(bf16[1024,2816]{1,0:T(8,128)(2,1)} %bitcast.110, bf16[1024,2816]{1,0:T(8,128)(2,1)} %gated_back.3.right), kind=kOutput, calls=%fused_computation.55 | convolution fusion | flops 2953314304 | bytes 9699328 | tf_op jit(solution)/shard_map/dot_general | solution.py:1094
  509.1 8.5 %multiply_reduce_fusion.2 = (f32[1024]{0:T(1024)}, f32[512]{0:T(512)S(1)}, f32[512,1024]{1,0:T(8,128)S(1)}) fusion(f32[512,1024]{1,0:T(8,128)} %copy-done.14, f32[512]{0:T(512)S(1)} %get-tuple-element.375, f32[1024]{0:T(1024)S(1)} %bitcast.159, bf16[512,1024]{1,0:T(8,128)(2,1)} %collective-permute-done.46, bf16[1024,2816]{1,0:T(8,128)(2,1)} %bitcast.111, ...), kind=kOutput, calls=%fused_computation.26 | convolution fusion | flops 2956982784 | bytes 13905920 | tf_op jit(solution)/shard_map/dot_general | solution.py:1094
  523.2 5.0 grad_columns.3
  528.2 12.2 %collective-permute-done.48.refs_1_ = bf16[8,64,1408]{2,1,0:T(8,128)(2,1)} collective-permute-done((bf16[8,64,1408]{2,1,0:T(8,128)(2,1)}, bf16[8,64,1408]{2,1,0:T(8,128)(2,1)}, u32[]{:S(2)}, u32[]{:S(2)}) %collective-permute-start.48) | collective-permute-done | bytes 1441824 | tf_op jit(solution)/shard_map/ppermute | solution.py:271
  540.7 4.8 halve.12
  553.6 22.0 %attend_back.3.right = bf16[1024,1536]{1,0:T(8,128)(2,1)} custom-call(s32[1]{0:T(128)} %bitcast.1.half_ref, bf16[1024,1536]{1,0:T(8,128)(2,1)} %get-tuple-element.207.rest_0_.kept_ref, bf16[512,512]{1,0:T(8,128)(2,1)S(1)} %convolution_convert_fusion.5.mine_ref, bf16[512,512]{1,0:T(8,128)(2,1)S(1)} %convolution_convert_fusion.4.other_ref, ...), custom_call_target="tpu_custom_call" | custom-call | tf_op jit(solution)/shard_map/attend_back/pallas_call | solution.py:240
  584.4 4.6 flatten.6
  593.2 4.0 convolution_convert_fusion
  597.4 8.2 %grad_rows.7 = (bf16[8,64,768]{2,1,0:T(8,128)(2,1)}, bf16[8,64,768]{2,1,0:T(8,128)(2,1)}, bf16[8,64,768]{2,1,0:T(8,128)(2,1)}, bf16[8,64,768]{2,1,0:T(8,128)(2,1)}) custom-call(s32[2]{0:T(128)} %pad_add_fusion.4.bits_ref.none_ref, bf16[512,1024]{1,0:T(8,128)(2,1)} %copy-done, bf16[512,1024]{1,0:T(8,128)(2,1)} %collective-permute-done.5.other_ref.other, ...), custom_call_target="tpu_custom_call" | custom-call | tf_op jit(solution)/shard_map/grad_rows/pallas_call | solution.py:638
  607.3 4.6 fusion.43
  613.9 4.2 fusion.50
  619.4 12.7 %collective-permute-done.59.refs_1_ = bf16[8,64,768]{2,1,0:T(8,128)(2,1)} collective-permute-done((bf16[8,64,768]{2,1,0:T(8,128)(2,1)S(1)}, bf16[8,64,768]{2,1,0:T(8,128)(2,1)}, u32[]{:S(2)}, u32[]{:S(2)}) %collective-permute-start.59) | collective-permute-done | bytes 786464 | tf_op jit(solution)/shard_map/ppermute | solution.py:271
  633.6 3.5 halve.15
  639.0 3.5 fusion.17
  650.0 4.2 flatten.7
  654.2 3.3 pick.4
  662.1 10.1 %collective-permute-done.77.refs_1_ = bf16[528,512]{1,0:T(8,128)(2,1)S(1)} collective-permute-done((bf16[528,512]{1,0:T(8,128)(2,1)S(1)}, bf16[528,512]{1,0:T(8,128)(2,1)S(1)}, u32[]{:S(2)}, u32[]{:S(2)}) %collective-permute-start.77) | collective-permute-done | bytes 540704 | tf_op jit(solution)/shard_map/ppermute | solution.py:271
  676.1 5.0 finish_far.2
  681.1 4.6 collective-permute-done.79.refs_3_
  686.5 3.1 pick.6
  691.2 5.0 collective-permute-done.74.refs_3_
  711.9 3.4 finish_near.2
  716.3 5.0 finish_far.3
  727.4 3.4 finish_near.3
  (442 shorter events, 209.0 us)
Async XLA Ops:
  7.2 39.6 %all-gather.6.cloned.1.call-start = ((), (), s32[]{:S(2)}) async-start(), calls=%async_computation.6 | async-start | bytes 1392640 | tf_op jit(solution)/shard_map/all_gather | solution.py:396
  15.0 80.7 %all-gather.10.cloned.1.call-start = ((), (), s32[]{:S(2)}) async-start(), calls=%async_computation.8 | async-start | bytes 2703360 | tf_op jit(solution)/shard_map/all_gather | solution.py:396
  22.7 117.8 %all-gather.8.cloned.1.call-start = ((), (), s32[]{:S(2)}) async-start(), calls=%async_computation.7 | async-start | bytes 1310720 | tf_op jit(solution)/shard_map/all_gather | solution.py:396
  29.8 149.7 %all-gather.12.cloned.1.call-start = ((), (), s32[]{:S(2)}) async-start(), calls=%async_computation.9 | async-start | bytes 2703360 | tf_op jit(solution)/shard_map/all_gather | solution.py:396
  46.8 26.3 %collective-permute-start.6 = (bf16[1088,512]{1,0:T(8,128)(2,1)}, bf16[1088,512]{1,0:T(8,128)(2,1)S(1)}, u32[]{:S(2)}, u32[]{:S(2)}) collective-permute-start(bf16[1088,512]{1,0:T(8,128)(2,1)} %all-gather.6.cloned.1.call-done), channel_id=1, source_target_pairs={{0,8},{8,0},{16,24},{24,16},{1,9},{9,1},{17,25},{25,17},{2,10},{10... | collective-permute-start | bytes 3342344 | tf_op jit(solution)/shard_map/ppermute | solution.py:271
  48.3 172.7 %all-gather.14.cloned.1.call-start = ((), (), s32[]{:S(2)}) async-start(), calls=%async_computation.10 | async-start | bytes 2703360 | tf_op jit(solution)/shard_map/all_gather | solution.py:396
  48.3 27.9 %collective-permute-start.7 = (bf16[1088,512]{1,0:T(8,128)(2,1)}, bf16[1088,512]{1,0:T(8,128)(2,1)}, u32[]{:S(2)}, u32[]{:S(2)}) collective-permute-start(bf16[1088,512]{1,0:T(8,128)(2,1)} %all-gather.6.cloned.1.call-done), channel_id=1, source_target_pairs={{0,16},{8,24},{16,0},{24,8},{1,17},{9,25},{17,1},{25,9},{2,18},{10... | collective-permute-start | bytes 3342344 | tf_op jit(solution)/shard_map/ppermute | solution.py:271
  73.1 25.4 %collective-permute-start.8 = (bf16[1088,512]{1,0:T(8,128)(2,1)S(1)}, bf16[1088,512]{1,0:T(8,128)(2,1)}, u32[]{:S(2)}, u32[]{:S(2)}) collective-permute-start(bf16[1088,512]{1,0:T(8,128)(2,1)S(1)} %collective-permute-done.6), channel_id=1, source_target_pairs={{0,16},{8,24},{16,0},{24,8},{1,17},{9,25},{17,1},{25,9},{2,18},{10... | collective-permute-start | bytes 3342344 | tf_op jit(solution)/shard_map/ppermute | solution.py:271
  101.1 48.4 %collective-permute-start.9 = (bf16[1408,512]{1,0:T(8,128)(2,1)}, bf16[1408,512]{1,0:T(8,128)(2,1)}, u32[]{:S(2)}, u32[]{:S(2)}) collective-permute-start(bf16[1408,512]{1,0:T(8,128)(2,1)} %bitcast.21), channel_id=1, source_target_pairs={{0,16},{8,24},{16,0},{24,8},{1,17},{9,25},{17,1},{25,9},{2,18},{10... | collective-permute-start | bytes 4325384 | tf_op jit(solution)/shard_map/ppermute | solution.py:271
  102.6 46.9 %collective-permute-start.10 = (bf16[1408,512]{1,0:T(8,128)(2,1)}, bf16[1408,512]{1,0:T(8,128)(2,1)}, u32[]{:S(2)}, u32[]{:S(2)}) collective-permute-start(bf16[1408,512]{1,0:T(8,128)(2,1)} %bitcast.21), channel_id=1, source_target_pairs={{0,8},{8,0},{16,24},{24,16},{1,9},{9,1},{17,25},{25,17},{2,10},{10... | collective-permute-start | bytes 4325384 | tf_op jit(solution)/shard_map/ppermute | solution.py:271
  106.0 42.3 %collective-permute-start.12 = (bf16[704,512]{1,0:T(8,128)(2,1)S(1)}, bf16[704,512]{1,0:T(8,128)(2,1)}, u32[]{:S(2)}, u32[]{:S(2)}) collective-permute-start(bf16[704,512]{1,0:T(8,128)(2,1)S(1)} %bitcast.131), channel_id=1, source_target_pairs={{0,16},{8,24},{16,0},{24,8},{1,17},{9,25},{17,1},{25,9},{2,18},{10... | collective-permute-start | bytes 2162696 | tf_op jit(solution)/shard_map/ppermute | solution.py:271
  106.6 42.9 %collective-permute-start.11 = (bf16[704,512]{1,0:T(8,128)(2,1)S(1)}, bf16[704,512]{1,0:T(8,128)(2,1)}, u32[]{:S(2)}, u32[]{:S(2)}) collective-permute-start(bf16[704,512]{1,0:T(8,128)(2,1)S(1)} %bitcast.132), channel_id=1, source_target_pairs={{0,8},{8,0},{16,24},{24,16},{1,9},{9,1},{17,25},{25,17},{2,10},{10... | collective-permute-start | bytes 2162696 | tf_op jit(solution)/shard_map/ppermute | solution.py:271
  108.7 315.9 %reduce-scatter.7.cloned.1.call-start = ((), (), s32[]{:S(2)}) async-start(), calls=%async_computation.11 | async-start | bytes 3604480 | tf_op jit(solution)/shard_map/reduce_scatter | solution.py:1062
  151.7 26.3 %collective-permute-start.16 = (bf16[1024,512]{1,0:T(8,128)(2,1)}, bf16[1024,512]{1,0:T(8,128)(2,1)}, u32[]{:S(2)}, u32[]{:S(2)}) collective-permute-start(bf16[1024,512]{1,0:T(8,128)(2,1)} %all-gather.8.cloned.1.call-done), channel_id=1, source_target_pairs={{0,16},{8,24},{16,0},{24,8},{1,17},{9,25},{17,1},{25,9},{2,18},{10... | collective-permute-start | bytes 3145736 | tf_op jit(solution)/shard_map/ppermute | solution.py:271
  152.3 34.7 %collective-permute-start.15 = (bf16[1408,512]{1,0:T(8,128)(2,1)}, bf16[1408,512]{1,0:T(8,128)(2,1)}, u32[]{:S(2)}, u32[]{:S(2)}) collective-permute-start(bf16[1408,512]{1,0:T(8,128)(2,1)} %collective-permute-done.9), channel_id=1, source_target_pairs={{0,8},{8,0},{16,24},{24,16},{1,9},{9,1},{17,25},{25,17},{2,10},{10... | collective-permute-start | bytes 4325384 | tf_op jit(solution)/shard_map/ppermute | solution.py:271
  158.1 34.6 %collective-permute-start.14 = (bf16[512,1024]{1,0:T(8,128)(2,1)S(1)}, bf16[512,1024]{1,0:T(8,128)(2,1)}, u32[]{:S(2)}, u32[]{:S(2)}) collective-permute-start(bf16[512,1024]{1,0:T(8,128)(2,1)S(1)} %multiply_convert_fusion.2.mine), channel_id=1, source_target_pairs={{0,1},{1,0},{2,3},{3,2},{4,5},{5,4},{6,7},{7,6},{8,9},{9,8},{10,11... | collective-permute-start | bytes 3145736 | tf_op jit(solution)/shard_map/ppermute | solution.py:266
  158.3 62.7 %collective-permute-start.17 = (bf16[1024,512]{1,0:T(8,128)(2,1)}, bf16[1024,512]{1,0:T(8,128)(2,1)}, u32[]{:S(2)}, u32[]{:S(2)}) collective-permute-start(bf16[1024,512]{1,0:T(8,128)(2,1)} %all-gather.8.cloned.1.call-done), channel_id=1, source_target_pairs={{0,8},{8,0},{16,24},{24,16},{1,9},{9,1},{17,25},{25,17},{2,10},{10... | collective-permute-start | bytes 3145736 | tf_op jit(solution)/shard_map/ppermute | solution.py:271
  159.8 61.2 %collective-permute-start.18 = (bf16[704,512]{1,0:T(8,128)(2,1)}, bf16[704,512]{1,0:T(8,128)(2,1)S(1)}, u32[]{:S(2)}, u32[]{:S(2)}) collective-permute-start(bf16[704,512]{1,0:T(8,128)(2,1)} %collective-permute-done.11), channel_id=1, source_target_pairs={{0,16},{8,24},{16,0},{24,8},{1,17},{9,25},{17,1},{25,9},{2,18},{10... | collective-permute-start | bytes 2162696 | tf_op jit(solution)/shard_map/ppermute | solution.py:271
  178.0 56.5 %collective-permute-start.20 = (bf16[1024,512]{1,0:T(8,128)(2,1)}, bf16[1024,512]{1,0:T(8,128)(2,1)}, u32[]{:S(2)}, u32[]{:S(2)}) collective-permute-start(bf16[1024,512]{1,0:T(8,128)(2,1)} %collective-permute-done.16), channel_id=1, source_target_pairs={{0,8},{8,0},{16,24},{24,16},{1,9},{9,1},{17,25},{25,17},{2,10},{10... | collective-permute-start | bytes 3145736 | tf_op jit(solution)/shard_map/ppermute | solution.py:271
  233.0 37.3 %collective-permute-start.23 = (bf16[1408,512]{1,0:T(8,128)(2,1)}, bf16[1408,512]{1,0:T(8,128)(2,1)}, u32[]{:S(2)}, u32[]{:S(2)}) collective-permute-start(bf16[1408,512]{1,0:T(8,128)(2,1)} %bitcast.42), channel_id=1, source_target_pairs={{0,16},{8,24},{16,0},{24,8},{1,17},{9,25},{17,1},{25,9},{2,18},{10... | collective-permute-start | bytes 4325384 | tf_op jit(solution)/shard_map/ppermute | solution.py:271
  234.5 35.8 %collective-permute-start.22 = (bf16[1408,512]{1,0:T(8,128)(2,1)}, bf16[1408,512]{1,0:T(8,128)(2,1)}, u32[]{:S(2)}, u32[]{:S(2)}) collective-permute-start(bf16[1408,512]{1,0:T(8,128)(2,1)} %bitcast.40), channel_id=1, source_target_pairs={{0,8},{8,0},{16,24},{24,16},{1,9},{9,1},{17,25},{25,17},{2,10},{10... | collective-permute-start | bytes 4325384 | tf_op jit(solution)/shard_map/ppermute | solution.py:271
  275.2 23.7 %collective-permute-start.29 = (bf16[512,1024]{1,0:T(8,128)(2,1)}, bf16[512,1024]{1,0:T(8,128)(2,1)}, u32[]{:S(2)}, u32[]{:S(2)}) collective-permute-start(bf16[512,1024]{1,0:T(8,128)(2,1)} %bitcast.54.mine), channel_id=1, source_target_pairs={{0,1},{1,0},{2,3},{3,2},{4,5},{5,4},{6,7},{7,6},{8,9},{9,8},{10,11... | collective-permute-start | bytes 3145736 | tf_op jit(solution)/shard_map/ppermute | solution.py:266
  279.2 27.2 %collective-permute-start.27 = (bf16[704,512]{1,0:T(8,128)(2,1)}, bf16[704,512]{1,0:T(8,128)(2,1)}, u32[]{:S(2)}, u32[]{:S(2)}) collective-permute-start(bf16[704,512]{1,0:T(8,128)(2,1)} %bitcast.50), channel_id=1, source_target_pairs={{0,16},{8,24},{16,0},{24,8},{1,17},{9,25},{17,1},{25,9},{2,18},{10... | collective-permute-start | bytes 2162696 | tf_op jit(solution)/shard_map/ppermute | solution.py:271
  279.8 26.7 %collective-permute-start.26 = (bf16[704,512]{1,0:T(8,128)(2,1)S(1)}, bf16[704,512]{1,0:T(8,128)(2,1)}, u32[]{:S(2)}, u32[]{:S(2)}) collective-permute-start(bf16[704,512]{1,0:T(8,128)(2,1)S(1)} %bitcast.133), channel_id=1, source_target_pairs={{0,8},{8,0},{16,24},{24,16},{1,9},{9,1},{17,25},{25,17},{2,10},{10... | collective-permute-start | bytes 2162696 | tf_op jit(solution)/shard_map/ppermute | solution.py:271
  340.4 147.8 %reduce-scatter.9.cloned.1.call-start = ((), (), s32[]{:S(2)}) async-start(), calls=%async_computation.12 | async-start | bytes 1802240 | tf_op jit(solution)/shard_map/reduce_scatter | solution.py:1062
  355.0 35.1 %collective-permute-start.32 = (bf16[8,64,1408]{2,1,0:T(8,128)(2,1)}, bf16[8,64,1408]{2,1,0:T(8,128)(2,1)S(1)}, u32[]{:S(2)}, u32[]{:S(2)}) collective-permute-start(bf16[8,64,1408]{2,1,0:T(8,128)(2,1)} %get-tuple-element.217), channel_id=1, source_target_pairs={{0,16},{8,24},{16,0},{24,8},{1,17},{9,25},{17,1},{25,9},{2,18},{10... | collective-permute-start | bytes 4325384 | tf_op jit(solution)/shard_map/ppermute | solution.py:271
  356.3 34.7 %collective-permute-start.33 = (bf16[8,64,1408]{2,1,0:T(8,128)(2,1)}, bf16[8,64,1408]{2,1,0:T(8,128)(2,1)S(1)}, u32[]{:S(2)}, u32[]{:S(2)}) collective-permute-start(bf16[8,64,1408]{2,1,0:T(8,128)(2,1)} %get-tuple-element.228), channel_id=1, source_target_pairs={{0,8},{8,0},{16,24},{24,16},{1,9},{9,1},{17,25},{25,17},{2,10},{10... | collective-permute-start | bytes 4325384 | tf_op jit(solution)/shard_map/ppermute | solution.py:271
  364.5 36.9 %collective-permute-start.34 = (bf16[512,512]{1,0:T(8,128)(2,1)}, bf16[512,512]{1,0:T(8,128)(2,1)}, u32[]{:S(2)}, u32[]{:S(2)}) collective-permute-start(bf16[512,512]{1,0:T(8,128)(2,1)} %get-tuple-element.234), channel_id=1, source_target_pairs={{0,8},{8,0},{16,24},{24,16},{1,9},{9,1},{17,25},{25,17},{2,10},{10... | collective-permute-start | bytes 1572872 | tf_op jit(solution)/shard_map/ppermute | solution.py:271
  422.5 18.6 %collective-permute-start.37 = (bf16[8,32,1408]{2,1,0:T(8,128)(2,1)}, bf16[8,32,1408]{2,1,0:T(8,128)(2,1)S(1)}, u32[]{:S(2)}, u32[]{:S(2)}) collective-permute-start(bf16[8,32,1408]{2,1,0:T(8,128)(2,1)} %get-tuple-element.229), channel_id=1, source_target_pairs={{0,8},{8,0},{16,24},{24,16},{1,9},{9,1},{17,25},{25,17},{2,10},{10... | collective-permute-start | bytes 2162696 | tf_op jit(solution)/shard_map/ppermute | solution.py:271
  424.0 18.4 %collective-permute-start.38 = (bf16[8,32,1408]{2,1,0:T(8,128)(2,1)}, bf16[8,32,1408]{2,1,0:T(8,128)(2,1)}, u32[]{:S(2)}, u32[]{:S(2)}) collective-permute-start(bf16[8,32,1408]{2,1,0:T(8,128)(2,1)} %get-tuple-element.230), channel_id=1, source_target_pairs={{0,16},{8,24},{16,0},{24,8},{1,17},{9,25},{17,1},{25,9},{2,18},{10... | collective-permute-start | bytes 2162696 | tf_op jit(solution)/shard_map/ppermute | solution.py:271
  447.2 101.8 %reduce-scatter.11.cloned.1.call-start = ((), (), s32[]{:S(2)}) async-start(), calls=%async_computation.13 | async-start | bytes 3604480 | tf_op jit(solution)/shard_map/reduce_scatter | solution.py:1062
  447.9 127.7 %reduce-scatter.13.cloned.1.call-start = ((), (), s32[]{:S(2)}) async-start(), calls=%async_computation.14 | async-start | bytes 1310720 | tf_op jit(solution)/shard_map/reduce_scatter | solution.py:1062
  448.0 19.0 %collective-permute-start.39 = (bf16[8,64,768]{2,1,0:T(8,128)(2,1)}, bf16[8,64,768]{2,1,0:T(8,128)(2,1)S(1)}, u32[]{:S(2)}, u32[]{:S(2)}) collective-permute-start(bf16[8,64,768]{2,1,0:T(8,128)(2,1)} %get-tuple-element.237), channel_id=1, source_target_pairs={{0,8},{8,0},{16,24},{24,16},{1,9},{9,1},{17,25},{25,17},{2,10},{10... | collective-permute-start | bytes 2359304 | tf_op jit(solution)/shard_map/ppermute | solution.py:271
  449.1 20.5 %collective-permute-start.40 = (bf16[8,64,768]{2,1,0:T(8,128)(2,1)S(1)}, bf16[8,64,768]{2,1,0:T(8,128)(2,1)S(1)}, u32[]{:S(2)}, u32[]{:S(2)}) collective-permute-start(bf16[8,64,768]{2,1,0:T(8,128)(2,1)S(1)} %copy-done.90), channel_id=1, source_target_pairs={{0,16},{8,24},{16,0},{24,8},{1,17},{9,25},{17,1},{25,9},{2,18},{10... | collective-permute-start | bytes 2359304 | tf_op jit(solution)/shard_map/ppermute | solution.py:271
  449.6 38.6 %collective-permute-start.41 = (bf16[352,512]{1,0:T(8,128)(2,1)S(1)}, bf16[352,512]{1,0:T(8,128)(2,1)S(1)}, u32[]{:S(2)}, u32[]{:S(2)}) collective-permute-start(bf16[352,512]{1,0:T(8,128)(2,1)S(1)} %copy-done.77), channel_id=1, source_target_pairs={{0,16},{8,24},{16,0},{24,8},{1,17},{9,25},{17,1},{25,9},{2,18},{10... | collective-permute-start | bytes 1081352 | tf_op jit(solution)/shard_map/ppermute | solution.py:271
  473.9 18.6 %collective-permute-start.42 = (bf16[8,32,768]{2,1,0:T(8,128)(2,1)}, bf16[8,32,768]{2,1,0:T(8,128)(2,1)S(1)}, u32[]{:S(2)}, u32[]{:S(2)}) collective-permute-start(bf16[8,32,768]{2,1,0:T(8,128)(2,1)} %get-tuple-element.254), channel_id=1, source_target_pairs={{0,16},{8,24},{16,0},{24,8},{1,17},{9,25},{17,1},{25,9},{2,18},{10... | collective-permute-start | bytes 1179656 | tf_op jit(solution)/shard_map/ppermute | solution.py:271
  474.5 18.1 %collective-permute-start.43 = (bf16[8,32,768]{2,1,0:T(8,128)(2,1)}, bf16[8,32,768]{2,1,0:T(8,128)(2,1)S(1)}, u32[]{:S(2)}, u32[]{:S(2)}) collective-permute-start(bf16[8,32,768]{2,1,0:T(8,128)(2,1)} %get-tuple-element.255), channel_id=1, source_target_pairs={{0,8},{8,0},{16,24},{24,16},{1,9},{9,1},{17,25},{25,17},{2,10},{10... | collective-permute-start | bytes 1179656 | tf_op jit(solution)/shard_map/ppermute | solution.py:271
  475.5 17.0 %collective-permute-start.44 = (bf16[512,256]{1,0:T(8,128)(2,1)}, bf16[512,256]{1,0:T(8,128)(2,1)S(1)}, u32[]{:S(2)}, u32[]{:S(2)}) collective-permute-start(bf16[512,256]{1,0:T(8,128)(2,1)} %get-tuple-element.235), channel_id=1, source_target_pairs={{0,16},{8,24},{16,0},{24,8},{1,17},{9,25},{17,1},{25,9},{2,18},{10... | collective-permute-start | bytes 786440 | tf_op jit(solution)/shard_map/ppermute | solution.py:271
  506.1 34.3 %collective-permute-start.48 = (bf16[8,64,1408]{2,1,0:T(8,128)(2,1)}, bf16[8,64,1408]{2,1,0:T(8,128)(2,1)}, u32[]{:S(2)}, u32[]{:S(2)}) collective-permute-start(bf16[8,64,1408]{2,1,0:T(8,128)(2,1)} %get-tuple-element.257), channel_id=1, source_target_pairs={{0,16},{8,24},{16,0},{24,8},{1,17},{9,25},{17,1},{25,9},{2,18},{10... | collective-permute-start | bytes 4325384 | tf_op jit(solution)/shard_map/ppermute | solution.py:271
  506.7 34.0 %collective-permute-start.49 = (bf16[8,64,1408]{2,1,0:T(8,128)(2,1)}, bf16[8,64,1408]{2,1,0:T(8,128)(2,1)}, u32[]{:S(2)}, u32[]{:S(2)}) collective-permute-start(bf16[8,64,1408]{2,1,0:T(8,128)(2,1)} %get-tuple-element.277), channel_id=1, source_target_pairs={{0,8},{8,0},{16,24},{24,16},{1,9},{9,1},{17,25},{25,17},{2,10},{10... | collective-permute-start | bytes 4325384 | tf_op jit(solution)/shard_map/ppermute | solution.py:271
  507.6 139.7 %reduce-scatter.15.cloned.1.call-start = ((), (), s32[]{:S(2)}) async-start(), calls=%async_computation.15 | async-start | bytes 1802240 | tf_op jit(solution)/shard_map/reduce_scatter | solution.py:1062
  545.5 37.8 %collective-permute-start.51 = (bf16[8,32,1408]{2,1,0:T(8,128)(2,1)}, bf16[8,32,1408]{2,1,0:T(8,128)(2,1)}, u32[]{:S(2)}, u32[]{:S(2)}) collective-permute-start(bf16[8,32,1408]{2,1,0:T(8,128)(2,1)} %get-tuple-element.278), channel_id=1, source_target_pairs={{0,8},{8,0},{16,24},{24,16},{1,9},{9,1},{17,25},{25,17},{2,10},{10... | collective-permute-start | bytes 2162696 | tf_op jit(solution)/shard_map/ppermute | solution.py:271
  546.3 38.1 %collective-permute-start.52 = (bf16[8,32,1408]{2,1,0:T(8,128)(2,1)}, bf16[8,32,1408]{2,1,0:T(8,128)(2,1)}, u32[]{:S(2)}, u32[]{:S(2)}) collective-permute-start(bf16[8,32,1408]{2,1,0:T(8,128)(2,1)} %get-tuple-element.279), channel_id=1, source_target_pairs={{0,16},{8,24},{16,0},{24,8},{1,17},{9,25},{17,1},{25,9},{2,18},{10... | collective-permute-start | bytes 2162696 | tf_op jit(solution)/shard_map/ppermute | solution.py:271
  547.8 31.8 %collective-permute-start.50 = (bf16[512,512]{1,0:T(8,128)(2,1)}, bf16[512,512]{1,0:T(8,128)(2,1)}, u32[]{:S(2)}, u32[]{:S(2)}) collective-permute-start(bf16[512,512]{1,0:T(8,128)(2,1)} %get-tuple-element.291), channel_id=1, source_target_pairs={{0,8},{8,0},{16,24},{24,16},{1,9},{9,1},{17,25},{25,17},{2,10},{10... | collective-permute-start | bytes 1572872 | tf_op jit(solution)/shard_map/ppermute | solution.py:271
  550.9 38.1 %collective-permute-start.53 = (bf16[352,512]{1,0:T(8,128)(2,1)}, bf16[352,512]{1,0:T(8,128)(2,1)S(1)}, u32[]{:S(2)}, u32[]{:S(2)}) collective-permute-start(bf16[352,512]{1,0:T(8,128)(2,1)} %get-tuple-element.361), channel_id=1, source_target_pairs={{0,16},{8,24},{16,0},{24,8},{1,17},{9,25},{17,1},{25,9},{2,18},{10... | collective-permute-start | bytes 1081352 | tf_op jit(solution)/shard_map/ppermute | solution.py:271
  578.2 27.3 %collective-permute-start.54 = (bf16[528,512]{1,0:T(8,128)(2,1)}, bf16[528,512]{1,0:T(8,128)(2,1)S(1)}, u32[]{:S(2)}, u32[]{:S(2)}) collective-permute-start(bf16[528,512]{1,0:T(8,128)(2,1)} %append.2.refs_0_), channel_id=1, source_target_pairs={{0,16},{8,24},{16,0},{24,8},{1,17},{9,25},{17,1},{25,9},{2,18},{10... | collective-permute-start | bytes 1622024 | tf_op jit(solution)/shard_map/ppermute | solution.py:271
  579.6 26.0 %collective-permute-start.55 = (bf16[528,512]{1,0:T(8,128)(2,1)}, bf16[528,512]{1,0:T(8,128)(2,1)S(1)}, u32[]{:S(2)}, u32[]{:S(2)}) collective-permute-start(bf16[528,512]{1,0:T(8,128)(2,1)} %append.2.refs_0_), channel_id=1, source_target_pairs={{0,8},{8,0},{16,24},{24,16},{1,9},{9,1},{17,25},{25,17},{2,10},{10... | collective-permute-start | bytes 1622024 | tf_op jit(solution)/shard_map/ppermute | solution.py:271
  583.3 22.4 %collective-permute-start.56 = (bf16[528,512]{1,0:T(8,128)(2,1)}, bf16[528,512]{1,0:T(8,128)(2,1)S(1)}, u32[]{:S(2)}, u32[]{:S(2)}) collective-permute-start(bf16[528,512]{1,0:T(8,128)(2,1)} %append.2.refs_0_), channel_id=1, source_target_pairs={{0,24},{8,16},{16,8},{24,0},{1,25},{9,17},{17,9},{25,1},{2,26},{10... | collective-permute-start | bytes 1622024 | tf_op jit(solution)/shard_map/ppermute | solution.py:271
  592.3 15.0 %collective-permute-start.57 = (bf16[352,256]{1,0:T(8,128)(2,1)}, bf16[352,256]{1,0:T(8,128)(2,1)S(1)}, u32[]{:S(2)}, u32[]{:S(2)}) collective-permute-start(bf16[352,256]{1,0:T(8,128)(2,1)} %get-tuple-element.300), channel_id=1, source_target_pairs={{0,8},{8,0},{16,24},{24,16},{1,9},{9,1},{17,25},{25,17},{2,10},{10... | collective-permute-start | bytes 540680 | tf_op jit(solution)/shard_map/ppermute | solution.py:271
  597.2 16.7 %collective-permute-start.28 = (bf16[512,1024]{1,0:T(8,128)(2,1)S(1)}, bf16[512,1024]{1,0:T(8,128)(2,1)}, u32[]{:S(2)}, u32[]{:S(2)}) collective-permute-start(bf16[512,1024]{1,0:T(8,128)(2,1)S(1)} %convolution_convert_fusion), channel_id=1, source_target_pairs={{0,1},{1,0},{2,3},{3,2},{4,5},{5,4},{6,7},{7,6},{8,9},{9,8},{10,11... | collective-permute-start | bytes 3145736 | tf_op jit(solution)/shard_map/ppermute | solution.py:266
  597.3 109.0 %reduce-scatter.17.cloned.1.call-start = ((), (), s32[]{:S(2)}) async-start(), calls=%async_computation.16 | async-start | bytes 1310720 | tf_op jit(solution)/shard_map/reduce_scatter | solution.py:1062
  612.0 20.1 %collective-permute-start.59 = (bf16[8,64,768]{2,1,0:T(8,128)(2,1)S(1)}, bf16[8,64,768]{2,1,0:T(8,128)(2,1)}, u32[]{:S(2)}, u32[]{:S(2)}) collective-permute-start(bf16[8,64,768]{2,1,0:T(8,128)(2,1)S(1)} %copy-done.92), channel_id=1, source_target_pairs={{0,8},{8,0},{16,24},{24,16},{1,9},{9,1},{17,25},{25,17},{2,10},{10... | collective-permute-start | bytes 2359304 | tf_op jit(solution)/shard_map/ppermute | solution.py:271
  613.1 20.5 %collective-permute-start.60 = (bf16[8,64,768]{2,1,0:T(8,128)(2,1)S(1)}, bf16[8,64,768]{2,1,0:T(8,128)(2,1)}, u32[]{:S(2)}, u32[]{:S(2)}) collective-permute-start(bf16[8,64,768]{2,1,0:T(8,128)(2,1)S(1)} %copy-done.91), channel_id=1, source_target_pairs={{0,16},{8,24},{16,0},{24,8},{1,17},{9,25},{17,1},{25,9},{2,18},{10... | collective-permute-start | bytes 2359304 | tf_op jit(solution)/shard_map/ppermute | solution.py:271
  618.1 29.2 %collective-permute-start.68 = (bf16[512,256]{1,0:T(8,128)(2,1)}, bf16[512,256]{1,0:T(8,128)(2,1)}, u32[]{:S(2)}, u32[]{:S(2)}) collective-permute-start(bf16[512,256]{1,0:T(8,128)(2,1)} %get-tuple-element.292), channel_id=1, source_target_pairs={{0,16},{8,24},{16,0},{24,8},{1,17},{9,25},{17,1},{25,9},{2,18},{10... | collective-permute-start | bytes 786440 | tf_op jit(solution)/shard_map/ppermute | solution.py:271
  657.5 17.7 %collective-permute-start.75 = (bf16[4,192,512]{2,1,0:T(8,128)(2,1)}, bf16[4,192,512]{2,1,0:T(8,128)(2,1)S(1)}, u32[]{:S(2)}, u32[]{:S(2)}) collective-permute-start(bf16[4,192,512]{2,1,0:T(8,128)(2,1)} %pick.4), channel_id=1, source_target_pairs={{0,1},{1,0},{2,3},{3,2},{4,5},{5,4},{6,7},{7,6},{8,9},{9,8},{10,11... | collective-permute-start | bytes 2359304 | tf_op jit(solution)/shard_map/ppermute | solution.py:266
  657.5 14.7 %collective-permute-start.77 = (bf16[528,512]{1,0:T(8,128)(2,1)S(1)}, bf16[528,512]{1,0:T(8,128)(2,1)S(1)}, u32[]{:S(2)}, u32[]{:S(2)}) collective-permute-start(bf16[528,512]{1,0:T(8,128)(2,1)S(1)} %copy-done.31), channel_id=1, source_target_pairs={{0,16},{8,24},{16,0},{24,8},{1,17},{9,25},{17,1},{25,9},{2,18},{10... | collective-permute-start | bytes 1622024 | tf_op jit(solution)/shard_map/ppermute | solution.py:271
  658.8 15.1 %collective-permute-start.78 = (bf16[528,512]{1,0:T(8,128)(2,1)S(1)}, bf16[528,512]{1,0:T(8,128)(2,1)S(1)}, u32[]{:S(2)}, u32[]{:S(2)}) collective-permute-start(bf16[528,512]{1,0:T(8,128)(2,1)S(1)} %copy-done.31), channel_id=1, source_target_pairs={{0,8},{8,0},{16,24},{24,16},{1,9},{9,1},{17,25},{25,17},{2,10},{10... | collective-permute-start | bytes 1622024 | tf_op jit(solution)/shard_map/ppermute | solution.py:271
  659.7 26.0 %collective-permute-start.79 = (bf16[528,512]{1,0:T(8,128)(2,1)S(1)}, bf16[528,512]{1,0:T(8,128)(2,1)S(1)}, u32[]{:S(2)}, u32[]{:S(2)}) collective-permute-start(bf16[528,512]{1,0:T(8,128)(2,1)S(1)} %copy-done.31), channel_id=1, source_target_pairs={{0,24},{8,16},{16,8},{24,0},{1,25},{9,17},{17,9},{25,1},{2,26},{10... | collective-permute-start | bytes 1622024 | tf_op jit(solution)/shard_map/ppermute | solution.py:271
  661.0 30.1 %collective-permute-start.72 = (bf16[256,512]{1,0:T(8,128)(2,1)S(1)}, bf16[256,512]{1,0:T(8,128)(2,1)S(1)}, u32[]{:S(2)}, u32[]{:S(2)}) collective-permute-start(bf16[256,512]{1,0:T(8,128)(2,1)S(1)} %copy-done.53), channel_id=1, source_target_pairs={{0,8},{8,0},{16,24},{24,16},{1,9},{9,1},{17,25},{25,17},{2,10},{10... | collective-permute-start | bytes 786440 | tf_op jit(solution)/shard_map/ppermute | solution.py:271
  672.2 19.0 %collective-permute-start.73 = (bf16[256,512]{1,0:T(8,128)(2,1)S(1)}, bf16[256,512]{1,0:T(8,128)(2,1)S(1)}, u32[]{:S(2)}, u32[]{:S(2)}) collective-permute-start(bf16[256,512]{1,0:T(8,128)(2,1)S(1)} %copy-done.53), channel_id=1, source_target_pairs={{0,16},{8,24},{16,0},{24,8},{1,17},{9,25},{17,1},{25,9},{2,18},{10... | collective-permute-start | bytes 786440 | tf_op jit(solution)/shard_map/ppermute | solution.py:271
  673.9 22.4 %collective-permute-start.74 = (bf16[256,512]{1,0:T(8,128)(2,1)S(1)}, bf16[256,512]{1,0:T(8,128)(2,1)S(1)}, u32[]{:S(2)}, u32[]{:S(2)}) collective-permute-start(bf16[256,512]{1,0:T(8,128)(2,1)S(1)} %copy-done.53), channel_id=1, source_target_pairs={{0,24},{8,16},{16,8},{24,0},{1,25},{9,17},{17,9},{25,1},{2,26},{10... | collective-permute-start | bytes 786440 | tf_op jit(solution)/shard_map/ppermute | solution.py:271
  675.2 14.4 %collective-permute-start.61 = (f32[4,1024]{1,0:T(4,128)S(1)}, f32[4,1024]{1,0:T(4,128)S(1)}, u32[]{:S(2)}, u32[]{:S(2)}) collective-permute-start(f32[4,1024]{1,0:T(4,128)S(1)} %pad_maximum_fusion.1), channel_id=1, source_target_pairs={{0,2},{2,0},{4,6},{6,4},{1,3},{3,1},{5,7},{7,5},{8,10},{10,8},{12,... | collective-permute-start | bytes 49160 | tf_op jit(solution)/shard_map/ppermute | solution.py:1279
  689.6 25.7 %collective-permute-start.80 = (bf16[4,192,512]{2,1,0:T(8,128)(2,1)}, bf16[4,192,512]{2,1,0:T(8,128)(2,1)S(1)}, u32[]{:S(2)}, u32[]{:S(2)}) collective-permute-start(bf16[4,192,512]{2,1,0:T(8,128)(2,1)} %pick.6), channel_id=1, source_target_pairs={{0,1},{1,0},{2,3},{3,2},{4,5},{5,4},{6,7},{7,6},{8,9},{9,8},{10,11... | collective-permute-start | bytes 2359304 | tf_op jit(solution)/shard_map/ppermute | solution.py:266
  706.3 14.9 %collective-permute-start.69 = (bf16[256,512]{1,0:T(8,128)(2,1)}, bf16[256,512]{1,0:T(8,128)(2,1)S(1)}, u32[]{:S(2)}, u32[]{:S(2)}) collective-permute-start(bf16[256,512]{1,0:T(8,128)(2,1)} %reduce-scatter.17.cloned.1.call-done.refs_0_), channel_id=1, source_target_pairs={{0,8},{8,0},{16,24},{24,16},{1,9},{9,1},{17,25},{25,17},{2,10},{10... | collective-permute-start | bytes 786440 | tf_op jit(solution)/shard_map/ppermute | solution.py:271
  (122 other events, 794.5 us)
Sparse Core Ops, SparseCore 0:
  15.1 31.6 all-gather.5
  48.9 46.7 all-gather.9
  97.8 26.6 all-gather.7
  126.5 46.7 all-gather.11
  175.3 45.6 all-gather.13
  340.6 54.8 reduce-scatter.6
  447.3 30.1 reduce-scatter.8
  479.8 55.0 reduce-scatter.10
  537.2 26.9 reduce-scatter.12
  597.5 31.1 reduce-scatter.14
  654.4 24.7 reduce-scatter.16

commit v4 on v3

--- a/solution.py
+++ b/solution.py
@@ -576,7 +576,7 @@
 
 
 def gated(tokens, weight, place):
-    length, width, tile = 2 * tokens[0].shape[0], weight.shape[1] // 2, 256
+    length, width, tile = 2 * tokens[0].shape[0], weight.shape[1] // 2, 512
     rows = pl.BlockSpec((tile, width), lambda i, s: (i, 0))
     maps = halves_of_rows(tile, length // tile // 2)
     return call(
@@ -600,7 +600,7 @@
 
 
 def gated_back(grad, weight, gate, upward, place):
-    (length, width), tile = gate.shape, 256
+    (length, width), tile = gate.shape, 512
     rows = pl.BlockSpec((tile, width), lambda i, s: (i, 0))
     maps = halves_of_rows(tile, length // tile // 2)
     return call(
@@ -630,7 +630,7 @@
             sent[g] = jnp.where(upper, two, one)
 
 
-def grad_rows(left, right, groups, bits, parts=1, tile=256):
+def grad_rows(left, right, groups, bits, parts=1, tile=512):
     half, features = left[0].shape
     length, width = right.shape
     per, rows = groups * tile // features, features // groups // 2

time: 745 us -> 744 us (level)
  transfers between devices with their start and end apart: 93 -> 93, of which waited for: 41 -> 42; matrix products, arithmetic and copies ran while one was open for 13% -> 13% of each run, Pallas kernels for 39% -> 39%
where the time goes in v4:
time: 744 us; the launch traced here: 738 us
  Pallas kernels  339 us (46%)
  waiting for transfers between devices  195 us (26%)
  matrix products  71.5 us (10%)
  starting transfers between devices  64.3 us (9%)
  local copies, waits for them, and re-layouts  36.5 us (5%)
  other arithmetic  16.2 us (2%)
  between operations  15.2 us (2%)
    ppermute x52, waiting for transfers between devices, exchange(): return lax.ppermute(x, 'rep', [(i, i ^ mask) for i in range(count)])  135 us
    ppermute x52, starting transfers between devices, exchange(): return lax.ppermute(x, 'rep', [(i, i ^ mask) for i in range(count)])  56.6 us
    pallas_call x2, Pallas kernels, attend_ahead(): pl.pallas_call(functools.partial(ahead_kernel, blocks, mixed), out_shape=...  51.6 us
    dot_general x12, matrix products, dot_nt(): lax.dot_general(a, b, (((1,), (1,)), ((), ())), preferred_element_type=jn...  51.3 us
    pallas_call x2, Pallas kernels, attend_back(): pl.pallas_call(functools.partial(back_kernel, blocks, mixed), out_shape=t...  43.6 us
    all_gather x5, waiting for transfers between devices, gather_shard(): return lax.all_gather(x, 'shard', axis=0, tiled=True)  38.7 us
    pallas_call x4, Pallas kernels, grad_rows(): call(grad_rows_kernel, [shape_of(groups, rows, width // parts)] * (2 * pa...  38.1 us
    pallas_call x6, Pallas kernels, join(): pl.pallas_call(functools.partial(join_kernel, masks, parts, cores), out_s...  30 us
  transfers between devices with their start and end apart: 93, of which 42 were waited for; matrix products, arithmetic and copies ran while one was open for 13% of the time, Pallas kernels for 39%

profile of v4, /device:TPU:0, one launch (start us, length us, event | category | flops | bytes accessed | tf_op | source)
XLA Modules:
  0.0 738.1 jit_solution(11135276093318449873)
XLA Ops:
  37.5 2.8 far_merge.4
  43.7 3.1 all-gather.6.cloned.1.call-done
  49.9 23.2 %collective-permute-done.6 = bf16[1088,512]{1,0:T(8,128)(2,1)S(1)} collective-permute-done((bf16[1088,512]{1,0:T(8,128)(2,1)}, bf16[1088,512]{1,0:T(8,128)(2,1)S(1)}, u32[]{:S(2)}, u32[]{:S(2)}) %collective-permute-start.6) | collective-permute-done | bytes 1114144 | tf_op jit(solution)/shard_map/ppermute | solution.py:271
  76.2 19.5 %all-gather.10.cloned.1.call-done = bf16[2112,512]{1,0:T(8,128)(2,1)} async-done(((bf16[528,512]{1,0:T(8,128)(2,1)}), bf16[2112,512]{1,0:T(8,128)(2,1)}) %all-gather.10.cloned.1.call-update) | async-done | bytes 2162704 | tf_op jit(solution)/shard_map/all_gather | solution.py:396
  95.7 2.9 collective-permute-done.8
  109.0 4.8 join.6
  113.8 25.5 %attend_ahead.2 = (bf16[1024,1536]{1,0:T(8,128)(2,1)}, bf16[1024,512]{1,0:T(8,128)(2,1)S(1)}, f32[4,2,1024]{2,1,0:T(2,128)S(1)}) custom-call(s32[1]{0:T(128)} %bitcast.1.half_ref, bf16[512,1024]{1,0:T(8,128)(2,1)S(1)} %fusion.10.mine_ref.mine, bf16[512,1024]{1,0:T(8,128)(2,1)} %collective-permute-done.5.other_ref.other, bf16[1024,1536]{1,0:T(8,128)(2,1)} %bitcast.125, ...), custom_call_target="tpu_custom_call" | custom-call | tf_op jit(solution)/shard_map/attend_ahead/pallas_call | solution.py:205
  140.3 8.0 %collective-permute-done.12 = bf16[704,512]{1,0:T(8,128)(2,1)} collective-permute-done((bf16[704,512]{1,0:T(8,128)(2,1)S(1)}, bf16[704,512]{1,0:T(8,128)(2,1)}, u32[]{:S(2)}, u32[]{:S(2)}) %collective-permute-start.12) | collective-permute-done | bytes 720928 | tf_op jit(solution)/shard_map/ppermute | solution.py:271
  160.3 17.7 %collective-permute-done.16 = bf16[1024,512]{1,0:T(8,128)(2,1)} collective-permute-done((bf16[1024,512]{1,0:T(8,128)(2,1)}, bf16[1024,512]{1,0:T(8,128)(2,1)}, u32[]{:S(2)}, u32[]{:S(2)}) %collective-permute-start.16) | collective-permute-done | bytes 1048608 | tf_op jit(solution)/shard_map/ppermute | solution.py:271
  179.5 7.5 %collective-permute-done.15 = bf16[1408,512]{1,0:T(8,128)(2,1)} collective-permute-done((bf16[1408,512]{1,0:T(8,128)(2,1)}, bf16[1408,512]{1,0:T(8,128)(2,1)}, u32[]{:S(2)}, u32[]{:S(2)}) %collective-permute-start.15) | collective-permute-done | bytes 1441824 | tf_op jit(solution)/shard_map/ppermute | solution.py:271
  187.0 5.6 join.7
  192.7 12.5 %gated.2 = (bf16[1024,1408]{1,0:T(8,128)(2,1)}, bf16[1024,1408]{1,0:T(8,128)(2,1)}, bf16[1024,1408]{1,0:T(8,128)(2,1)}) custom-call(s32[2]{0:T(128)} %pad_add_fusion.place_ref.none_ref, bf16[512,1024]{1,0:T(8,128)(2,1)} %copy-done.26, bf16[512,1024]{1,0:T(8,128)(2,1)} %collective-permute-done.14.other, bf16[1024,2816]{1,0:T(8,128)(2,1)} %bitcast.109), custom_call_target="tpu_custom_call" | custom-call | tf_op jit(solution)/shard_map/gated/pallas_call | solution.py:582
  205.2 16.1 %all-gather.14.cloned.1.call-done = bf16[2112,512]{1,0:T(8,128)(2,1)} async-done(((bf16[528,512]{1,0:T(8,128)(2,1)}), bf16[2112,512]{1,0:T(8,128)(2,1)}) %all-gather.14.cloned.1.call-update) | async-done | bytes 2162704 | tf_op jit(solution)/shard_map/all_gather | solution.py:396
  222.1 4.8 join.8
  226.9 4.2 convolution_convert_fusion.1
  239.8 5.1 join.9
  244.9 26.1 %attend_ahead.3 = (bf16[1024,1536]{1,0:T(8,128)(2,1)}, bf16[1024,512]{1,0:T(8,128)(2,1)S(1)}, f32[4,2,1024]{2,1,0:T(2,128)S(1)}) custom-call(s32[1]{0:T(128)} %bitcast.1.half_ref, bf16[512,1024]{1,0:T(8,128)(2,1)S(1)} %multiply_convert_fusion.1.mine_ref.mine, bf16[512,1024]{1,0:T(8,128)(2,1)} %collective-permute-done.21.other_ref.other, ...), custom_call_target="tpu_custom_call" | custom-call | tf_op jit(solution)/shard_map/attend_ahead/pallas_call | solution.py:205
  281.8 5.6 join.10
  287.4 12.6 %gated.3 = (bf16[1024,1408]{1,0:T(8,128)(2,1)}, bf16[1024,1408]{1,0:T(8,128)(2,1)}, bf16[1024,1408]{1,0:T(8,128)(2,1)}) custom-call(s32[2]{0:T(128)} %pad_add_fusion.place_ref.none_ref, bf16[512,1024]{1,0:T(8,128)(2,1)} %copy-done.27, bf16[512,1024]{1,0:T(8,128)(2,1)} %collective-permute-done.25.other, bf16[1024,2816]{1,0:T(8,128)(2,1)} %bitcast.112), custom_call_target="tpu_custom_call" | custom-call | tf_op jit(solution)/shard_map/gated/pallas_call | solution.py:582
  300.0 7.4 %grad_whole.2 = bf16[1408,1024]{1,0:T(8,128)(2,1)} custom-call(s32[2]{0:T(128)} %pad_add_fusion.place_ref.none_ref, bf16[1024,1408]{1,0:T(8,128)(2,1)} %get-tuple-element.212.refs_4_.left, bf16[512,1024]{1,0:T(8,128)(2,1)} %bitcast.54.mine, bf16[512,1024]{1,0:T(8,128)(2,1)} %collective-permute-done.29.other), custom_call_target="tpu_custom_call" | custom-call | tf_op jit(solution)/shard_map/grad_whole/pallas_call | solution.py:657
  307.4 4.3 join.11
  311.7 10.9 %gated_back.2.right = bf16[1024,2816]{1,0:T(8,128)(2,1)} custom-call(s32[2]{0:T(128)} %pad_add_fusion.place_ref.none_ref, bf16[512,1024]{1,0:T(8,128)(2,1)} %bitcast.54.mine, bf16[512,1024]{1,0:T(8,128)(2,1)} %collective-permute-done.29.other, bf16[1408,1024]{1,0:T(8,128)(2,1)} %bitcast.115, bf16[1024,1408]{1,0:T(8,128)(2,1)} %get-tuple-element.215.gate, ...), custom_call_target="tpu_custom_call" | custom-call | tf_op jit(solution)/shard_map/gated_back/pallas_call | solution.py:606
  322.6 11.2 %grad_rows.4 = (bf16[8,64,1408]{2,1,0:T(8,128)(2,1)}, bf16[8,64,1408]{2,1,0:T(8,128)(2,1)}, bf16[8,64,1408]{2,1,0:T(8,128)(2,1)}, bf16[8,64,1408]{2,1,0:T(8,128)(2,1)}) custom-call(s32[2]{0:T(128)} %pad_add_fusion.3.bits_ref.none_ref, bf16[512,1024]{1,0:T(8,128)(2,1)} %copy-done.27, bf16[512,1024]{1,0:T(8,128)(2,1)} %collective-permute-done.25.other, ...), custom_call_target="tpu_custom_call" | custom-call | tf_op jit(solution)/shard_map/grad_rows/pallas_call | solution.py:638
  333.8 7.6 %fusion.34 = bf16[512,1024]{1,0:T(8,128)(2,1)} fusion(bf16[1024,2816]{1,0:T(8,128)(2,1)} %bitcast.113, bf16[1024,2816]{1,0:T(8,128)(2,1)} %gated_back.2.right), kind=kOutput, calls=%fused_computation.54 | convolution fusion | flops 2953314304 | bytes 9699328 | tf_op jit(solution)/shard_map/dot_general | solution.py:1094
  344.3 8.2 %multiply_reduce_fusion = (f32[1024]{0:T(1024)S(1)}, f32[512]{0:T(512)S(1)}, f32[512,1024]{1,0:T(8,128)S(1)}) fusion(f32[512,1024]{1,0:T(8,128)} %copy-done.11, f32[512]{0:T(512)S(1)} %get-tuple-element.379, f32[1024]{0:T(1024)S(1)} %bitcast.165, bf16[512,1024]{1,0:T(8,128)(2,1)S(1)} %collective-permute-done.30, bf16[1024,2816]{1,0:T(8,128)(2,1)} %bitcast.114, ...), kind=kOutput, calls=%fused_computation.24 | convolution fusion | flops 2956982784 | bytes 13905920 | tf_op jit(solution)/shard_map/dot_general | solution.py:1094
  352.5 3.3 fusion.63
  360.1 5.2 grad_columns.2
  367.9 21.6 %attend_back.2 = (bf16[1024,1536]{1,0:T(8,128)(2,1)}, f32[1024,512]{1,0:T(8,128)S(1)}) custom-call(s32[1]{0:T(128)} %bitcast.1.half_ref, bf16[1024,1536]{1,0:T(8,128)(2,1)} %get-tuple-element.219.kept_ref, bf16[512,512]{1,0:T(8,128)(2,1)S(1)} %convolution_convert_fusion.7.mine_ref, bf16[512,512]{1,0:T(8,128)(2,1)S(1)} %convolution_convert_fusion.6.other_ref, ...), custom_call_target="tpu_custom_call" | custom-call | tf_op jit(solution)/shard_map/attend_back/pallas_call | solution.py:240
  393.0 4.6 halve.8
  397.6 4.8 collective-permute-done.34.refs_1_
  405.1 7.7 %grad_rows.5 = (bf16[8,64,768]{2,1,0:T(8,128)(2,1)}, bf16[8,64,768]{2,1,0:T(8,128)(2,1)}, bf16[8,64,768]{2,1,0:T(8,128)(2,1)}, bf16[8,64,768]{2,1,0:T(8,128)(2,1)}) custom-call(s32[2]{0:T(128)} %pad_add_fusion.4.bits_ref.none_ref, bf16[512,1024]{1,0:T(8,128)(2,1)} %copy-done.1, bf16[512,1024]{1,0:T(8,128)(2,1)} %collective-permute-done.21.other_ref.other, ...), custom_call_target="tpu_custom_call" | custom-call | tf_op jit(solution)/shard_map/grad_rows/pallas_call | solution.py:638
  412.8 3.4 fusion.40
  427.3 7.8 %grad_whole.3 = bf16[1408,1024]{1,0:T(8,128)(2,1)} custom-call(s32[2]{0:T(128)} %pad_add_fusion.place_ref.none_ref, bf16[1024,1408]{1,0:T(8,128)(2,1)} %get-tuple-element.203.refs_4_.left, bf16[512,1024]{1,0:T(8,128)(2,1)} %copy-done.25, bf16[512,1024]{1,0:T(8,128)(2,1)} %collective-permute-done.36.other), custom_call_target="tpu_custom_call" | custom-call | tf_op jit(solution)/shard_map/grad_whole/pallas_call | solution.py:657
  435.0 6.8 collective-permute-done.37.refs_1_
  443.2 4.6 flatten.4
  451.7 10.9 %gated_back.3.right = bf16[1024,2816]{1,0:T(8,128)(2,1)} custom-call(s32[2]{0:T(128)} %pad_add_fusion.place_ref.none_ref, bf16[512,1024]{1,0:T(8,128)(2,1)} %copy-done.25, bf16[512,1024]{1,0:T(8,128)(2,1)} %collective-permute-done.36.other, bf16[1408,1024]{1,0:T(8,128)(2,1)} %bitcast.119, bf16[1024,1408]{1,0:T(8,128)(2,1)} %get-tuple-element.247.gate, ...), custom_call_target="tpu_custom_call" | custom-call | tf_op jit(solution)/shard_map/gated_back/pallas_call | solution.py:606
  462.6 4.9 collective-permute-done.39.refs_1_
  471.0 3.5 halve.10
  477.5 11.2 %grad_rows.6 = (bf16[8,64,1408]{2,1,0:T(8,128)(2,1)}, bf16[8,64,1408]{2,1,0:T(8,128)(2,1)}, bf16[8,64,1408]{2,1,0:T(8,128)(2,1)}, bf16[8,64,1408]{2,1,0:T(8,128)(2,1)}) custom-call(s32[2]{0:T(128)} %pad_add_fusion.3.bits_ref.none_ref, bf16[512,1024]{1,0:T(8,128)(2,1)} %copy-done.26, bf16[512,1024]{1,0:T(8,128)(2,1)} %collective-permute-done.14.other, ...), custom_call_target="tpu_custom_call" | custom-call | tf_op jit(solution)/shard_map/grad_rows/pallas_call | solution.py:638
  494.6 4.2 flatten.5
  498.8 7.8 %fusion.37 = bf16[512,1024]{1,0:T(8,128)(2,1)} fusion(bf16[1024,2816]{1,0:T(8,128)(2,1)} %bitcast.110, bf16[1024,2816]{1,0:T(8,128)(2,1)} %gated_back.3.right), kind=kOutput, calls=%fused_computation.55 | convolution fusion | flops 2953314304 | bytes 9699328 | tf_op jit(solution)/shard_map/dot_general | solution.py:1094
  509.6 8.6 %multiply_reduce_fusion.2 = (f32[1024]{0:T(1024)}, f32[512]{0:T(512)S(1)}, f32[512,1024]{1,0:T(8,128)S(1)}) fusion(f32[512,1024]{1,0:T(8,128)} %copy-done.14, f32[512]{0:T(512)S(1)} %get-tuple-element.375, f32[1024]{0:T(1024)S(1)} %bitcast.159, bf16[512,1024]{1,0:T(8,128)(2,1)} %collective-permute-done.46, bf16[1024,2816]{1,0:T(8,128)(2,1)} %bitcast.111, ...), kind=kOutput, calls=%fused_computation.26 | convolution fusion | flops 2956982784 | bytes 13905920 | tf_op jit(solution)/shard_map/dot_general | solution.py:1094
  523.8 4.8 grad_columns.3
  528.6 12.3 %collective-permute-done.48.refs_1_ = bf16[8,64,1408]{2,1,0:T(8,128)(2,1)} collective-permute-done((bf16[8,64,1408]{2,1,0:T(8,128)(2,1)}, bf16[8,64,1408]{2,1,0:T(8,128)(2,1)}, u32[]{:S(2)}, u32[]{:S(2)}) %collective-permute-start.48) | collective-permute-done | bytes 1441824 | tf_op jit(solution)/shard_map/ppermute | solution.py:271
  541.2 4.8 halve.12
  554.1 22.0 %attend_back.3.right = bf16[1024,1536]{1,0:T(8,128)(2,1)} custom-call(s32[1]{0:T(128)} %bitcast.1.half_ref, bf16[1024,1536]{1,0:T(8,128)(2,1)} %get-tuple-element.207.rest_0_.kept_ref, bf16[512,512]{1,0:T(8,128)(2,1)S(1)} %convolution_convert_fusion.5.mine_ref, bf16[512,512]{1,0:T(8,128)(2,1)S(1)} %convolution_convert_fusion.4.other_ref, ...), custom_call_target="tpu_custom_call" | custom-call | tf_op jit(solution)/shard_map/attend_back/pallas_call | solution.py:240
  585.0 4.6 flatten.6
  593.7 4.0 convolution_convert_fusion
  597.9 8.0 %grad_rows.7 = (bf16[8,64,768]{2,1,0:T(8,128)(2,1)}, bf16[8,64,768]{2,1,0:T(8,128)(2,1)}, bf16[8,64,768]{2,1,0:T(8,128)(2,1)}, bf16[8,64,768]{2,1,0:T(8,128)(2,1)}) custom-call(s32[2]{0:T(128)} %pad_add_fusion.4.bits_ref.none_ref, bf16[512,1024]{1,0:T(8,128)(2,1)} %copy-done, bf16[512,1024]{1,0:T(8,128)(2,1)} %collective-permute-done.5.other_ref.other, ...), custom_call_target="tpu_custom_call" | custom-call | tf_op jit(solution)/shard_map/grad_rows/pallas_call | solution.py:638
  607.8 4.6 fusion.43
  614.4 4.2 fusion.50
  619.9 12.7 %collective-permute-done.59.refs_1_ = bf16[8,64,768]{2,1,0:T(8,128)(2,1)} collective-permute-done((bf16[8,64,768]{2,1,0:T(8,128)(2,1)S(1)}, bf16[8,64,768]{2,1,0:T(8,128)(2,1)}, u32[]{:S(2)}, u32[]{:S(2)}) %collective-permute-start.59) | collective-permute-done | bytes 786464 | tf_op jit(solution)/shard_map/ppermute | solution.py:271
  634.1 3.5 halve.15
  639.5 3.5 fusion.17
  650.5 4.2 flatten.7
  654.8 3.3 pick.4
  662.6 10.1 %collective-permute-done.77.refs_1_ = bf16[528,512]{1,0:T(8,128)(2,1)S(1)} collective-permute-done((bf16[528,512]{1,0:T(8,128)(2,1)S(1)}, bf16[528,512]{1,0:T(8,128)(2,1)S(1)}, u32[]{:S(2)}, u32[]{:S(2)}) %collective-permute-start.77) | collective-permute-done | bytes 540704 | tf_op jit(solution)/shard_map/ppermute | solution.py:271
  676.6 5.0 finish_far.2
  681.7 4.6 collective-permute-done.79.refs_3_
  687.0 3.1 pick.6
  691.8 5.0 collective-permute-done.74.refs_3_
  712.5 3.4 finish_near.2
  716.8 5.0 finish_far.3
  728.0 3.4 finish_near.3
  (442 shorter events, 208.9 us)
Async XLA Ops:
  7.2 39.6 %all-gather.6.cloned.1.call-start = ((), (), s32[]{:S(2)}) async-start(), calls=%async_computation.6 | async-start | bytes 1392640 | tf_op jit(solution)/shard_map/all_gather | solution.py:396
  15.0 80.7 %all-gather.10.cloned.1.call-start = ((), (), s32[]{:S(2)}) async-start(), calls=%async_computation.8 | async-start | bytes 2703360 | tf_op jit(solution)/shard_map/all_gather | solution.py:396
  22.7 117.5 %all-gather.8.cloned.1.call-start = ((), (), s32[]{:S(2)}) async-start(), calls=%async_computation.7 | async-start | bytes 1310720 | tf_op jit(solution)/shard_map/all_gather | solution.py:396
  29.8 149.7 %all-gather.12.cloned.1.call-start = ((), (), s32[]{:S(2)}) async-start(), calls=%async_computation.9 | async-start | bytes 2703360 | tf_op jit(solution)/shard_map/all_gather | solution.py:396
  46.8 26.3 %collective-permute-start.6 = (bf16[1088,512]{1,0:T(8,128)(2,1)}, bf16[1088,512]{1,0:T(8,128)(2,1)S(1)}, u32[]{:S(2)}, u32[]{:S(2)}) collective-permute-start(bf16[1088,512]{1,0:T(8,128)(2,1)} %all-gather.6.cloned.1.call-done), channel_id=1, source_target_pairs={{0,8},{8,0},{16,24},{24,16},{1,9},{9,1},{17,25},{25,17},{2,10},{10... | collective-permute-start | bytes 3342344 | tf_op jit(solution)/shard_map/ppermute | solution.py:271
  48.3 173.0 %all-gather.14.cloned.1.call-start = ((), (), s32[]{:S(2)}) async-start(), calls=%async_computation.10 | async-start | bytes 2703360 | tf_op jit(solution)/shard_map/all_gather | solution.py:396
  48.3 27.9 %collective-permute-start.7 = (bf16[1088,512]{1,0:T(8,128)(2,1)}, bf16[1088,512]{1,0:T(8,128)(2,1)}, u32[]{:S(2)}, u32[]{:S(2)}) collective-permute-start(bf16[1088,512]{1,0:T(8,128)(2,1)} %all-gather.6.cloned.1.call-done), channel_id=1, source_target_pairs={{0,16},{8,24},{16,0},{24,8},{1,17},{9,25},{17,1},{25,9},{2,18},{10... | collective-permute-start | bytes 3342344 | tf_op jit(solution)/shard_map/ppermute | solution.py:271
  73.1 25.4 %collective-permute-start.8 = (bf16[1088,512]{1,0:T(8,128)(2,1)S(1)}, bf16[1088,512]{1,0:T(8,128)(2,1)}, u32[]{:S(2)}, u32[]{:S(2)}) collective-permute-start(bf16[1088,512]{1,0:T(8,128)(2,1)S(1)} %collective-permute-done.6), channel_id=1, source_target_pairs={{0,16},{8,24},{16,0},{24,8},{1,17},{9,25},{17,1},{25,9},{2,18},{10... | collective-permute-start | bytes 3342344 | tf_op jit(solution)/shard_map/ppermute | solution.py:271
  101.1 48.4 %collective-permute-start.9 = (bf16[1408,512]{1,0:T(8,128)(2,1)}, bf16[1408,512]{1,0:T(8,128)(2,1)}, u32[]{:S(2)}, u32[]{:S(2)}) collective-permute-start(bf16[1408,512]{1,0:T(8,128)(2,1)} %bitcast.21), channel_id=1, source_target_pairs={{0,16},{8,24},{16,0},{24,8},{1,17},{9,25},{17,1},{25,9},{2,18},{10... | collective-permute-start | bytes 4325384 | tf_op jit(solution)/shard_map/ppermute | solution.py:271
  102.6 46.9 %collective-permute-start.10 = (bf16[1408,512]{1,0:T(8,128)(2,1)}, bf16[1408,512]{1,0:T(8,128)(2,1)}, u32[]{:S(2)}, u32[]{:S(2)}) collective-permute-start(bf16[1408,512]{1,0:T(8,128)(2,1)} %bitcast.21), channel_id=1, source_target_pairs={{0,8},{8,0},{16,24},{24,16},{1,9},{9,1},{17,25},{25,17},{2,10},{10... | collective-permute-start | bytes 4325384 | tf_op jit(solution)/shard_map/ppermute | solution.py:271
  106.0 42.3 %collective-permute-start.12 = (bf16[704,512]{1,0:T(8,128)(2,1)S(1)}, bf16[704,512]{1,0:T(8,128)(2,1)}, u32[]{:S(2)}, u32[]{:S(2)}) collective-permute-start(bf16[704,512]{1,0:T(8,128)(2,1)S(1)} %bitcast.131), channel_id=1, source_target_pairs={{0,16},{8,24},{16,0},{24,8},{1,17},{9,25},{17,1},{25,9},{2,18},{10... | collective-permute-start | bytes 2162696 | tf_op jit(solution)/shard_map/ppermute | solution.py:271
  106.6 42.9 %collective-permute-start.11 = (bf16[704,512]{1,0:T(8,128)(2,1)S(1)}, bf16[704,512]{1,0:T(8,128)(2,1)}, u32[]{:S(2)}, u32[]{:S(2)}) collective-permute-start(bf16[704,512]{1,0:T(8,128)(2,1)S(1)} %bitcast.132), channel_id=1, source_target_pairs={{0,8},{8,0},{16,24},{24,16},{1,9},{9,1},{17,25},{25,17},{2,10},{10... | collective-permute-start | bytes 2162696 | tf_op jit(solution)/shard_map/ppermute | solution.py:271
  108.7 316.6 %reduce-scatter.7.cloned.1.call-start = ((), (), s32[]{:S(2)}) async-start(), calls=%async_computation.11 | async-start | bytes 3604480 | tf_op jit(solution)/shard_map/reduce_scatter | solution.py:1062
  151.7 26.3 %collective-permute-start.16 = (bf16[1024,512]{1,0:T(8,128)(2,1)}, bf16[1024,512]{1,0:T(8,128)(2,1)}, u32[]{:S(2)}, u32[]{:S(2)}) collective-permute-start(bf16[1024,512]{1,0:T(8,128)(2,1)} %all-gather.8.cloned.1.call-done), channel_id=1, source_target_pairs={{0,16},{8,24},{16,0},{24,8},{1,17},{9,25},{17,1},{25,9},{2,18},{10... | collective-permute-start | bytes 3145736 | tf_op jit(solution)/shard_map/ppermute | solution.py:271
  152.3 34.7 %collective-permute-start.15 = (bf16[1408,512]{1,0:T(8,128)(2,1)}, bf16[1408,512]{1,0:T(8,128)(2,1)}, u32[]{:S(2)}, u32[]{:S(2)}) collective-permute-start(bf16[1408,512]{1,0:T(8,128)(2,1)} %collective-permute-done.9), channel_id=1, source_target_pairs={{0,8},{8,0},{16,24},{24,16},{1,9},{9,1},{17,25},{25,17},{2,10},{10... | collective-permute-start | bytes 4325384 | tf_op jit(solution)/shard_map/ppermute | solution.py:271
  158.1 34.6 %collective-permute-start.14 = (bf16[512,1024]{1,0:T(8,128)(2,1)S(1)}, bf16[512,1024]{1,0:T(8,128)(2,1)}, u32[]{:S(2)}, u32[]{:S(2)}) collective-permute-start(bf16[512,1024]{1,0:T(8,128)(2,1)S(1)} %multiply_convert_fusion.2.mine), channel_id=1, source_target_pairs={{0,1},{1,0},{2,3},{3,2},{4,5},{5,4},{6,7},{7,6},{8,9},{9,8},{10,11... | collective-permute-start | bytes 3145736 | tf_op jit(solution)/shard_map/ppermute | solution.py:266
  158.3 63.0 %collective-permute-start.17 = (bf16[1024,512]{1,0:T(8,128)(2,1)}, bf16[1024,512]{1,0:T(8,128)(2,1)}, u32[]{:S(2)}, u32[]{:S(2)}) collective-permute-start(bf16[1024,512]{1,0:T(8,128)(2,1)} %all-gather.8.cloned.1.call-done), channel_id=1, source_target_pairs={{0,8},{8,0},{16,24},{24,16},{1,9},{9,1},{17,25},{25,17},{2,10},{10... | collective-permute-start | bytes 3145736 | tf_op jit(solution)/shard_map/ppermute | solution.py:271
  159.8 61.5 %collective-permute-start.18 = (bf16[704,512]{1,0:T(8,128)(2,1)}, bf16[704,512]{1,0:T(8,128)(2,1)S(1)}, u32[]{:S(2)}, u32[]{:S(2)}) collective-permute-start(bf16[704,512]{1,0:T(8,128)(2,1)} %collective-permute-done.11), channel_id=1, source_target_pairs={{0,16},{8,24},{16,0},{24,8},{1,17},{9,25},{17,1},{25,9},{2,18},{10... | collective-permute-start | bytes 2162696 | tf_op jit(solution)/shard_map/ppermute | solution.py:271
  178.0 57.1 %collective-permute-start.20 = (bf16[1024,512]{1,0:T(8,128)(2,1)}, bf16[1024,512]{1,0:T(8,128)(2,1)}, u32[]{:S(2)}, u32[]{:S(2)}) collective-permute-start(bf16[1024,512]{1,0:T(8,128)(2,1)} %collective-permute-done.16), channel_id=1, source_target_pairs={{0,8},{8,0},{16,24},{24,16},{1,9},{9,1},{17,25},{25,17},{2,10},{10... | collective-permute-start | bytes 3145736 | tf_op jit(solution)/shard_map/ppermute | solution.py:271
  233.7 37.3 %collective-permute-start.23 = (bf16[1408,512]{1,0:T(8,128)(2,1)}, bf16[1408,512]{1,0:T(8,128)(2,1)}, u32[]{:S(2)}, u32[]{:S(2)}) collective-permute-start(bf16[1408,512]{1,0:T(8,128)(2,1)} %bitcast.42), channel_id=1, source_target_pairs={{0,16},{8,24},{16,0},{24,8},{1,17},{9,25},{17,1},{25,9},{2,18},{10... | collective-permute-start | bytes 4325384 | tf_op jit(solution)/shard_map/ppermute | solution.py:271
  235.2 35.8 %collective-permute-start.22 = (bf16[1408,512]{1,0:T(8,128)(2,1)}, bf16[1408,512]{1,0:T(8,128)(2,1)}, u32[]{:S(2)}, u32[]{:S(2)}) collective-permute-start(bf16[1408,512]{1,0:T(8,128)(2,1)} %bitcast.40), channel_id=1, source_target_pairs={{0,8},{8,0},{16,24},{24,16},{1,9},{9,1},{17,25},{25,17},{2,10},{10... | collective-permute-start | bytes 4325384 | tf_op jit(solution)/shard_map/ppermute | solution.py:271
  275.8 24.2 %collective-permute-start.29 = (bf16[512,1024]{1,0:T(8,128)(2,1)}, bf16[512,1024]{1,0:T(8,128)(2,1)}, u32[]{:S(2)}, u32[]{:S(2)}) collective-permute-start(bf16[512,1024]{1,0:T(8,128)(2,1)} %bitcast.54.mine), channel_id=1, source_target_pairs={{0,1},{1,0},{2,3},{3,2},{4,5},{5,4},{6,7},{7,6},{8,9},{9,8},{10,11... | collective-permute-start | bytes 3145736 | tf_op jit(solution)/shard_map/ppermute | solution.py:266
  279.9 27.6 %collective-permute-start.27 = (bf16[704,512]{1,0:T(8,128)(2,1)}, bf16[704,512]{1,0:T(8,128)(2,1)}, u32[]{:S(2)}, u32[]{:S(2)}) collective-permute-start(bf16[704,512]{1,0:T(8,128)(2,1)} %bitcast.50), channel_id=1, source_target_pairs={{0,16},{8,24},{16,0},{24,8},{1,17},{9,25},{17,1},{25,9},{2,18},{10... | collective-permute-start | bytes 2162696 | tf_op jit(solution)/shard_map/ppermute | solution.py:271
  280.5 27.0 %collective-permute-start.26 = (bf16[704,512]{1,0:T(8,128)(2,1)S(1)}, bf16[704,512]{1,0:T(8,128)(2,1)}, u32[]{:S(2)}, u32[]{:S(2)}) collective-permute-start(bf16[704,512]{1,0:T(8,128)(2,1)S(1)} %bitcast.133), channel_id=1, source_target_pairs={{0,8},{8,0},{16,24},{24,16},{1,9},{9,1},{17,25},{25,17},{2,10},{10... | collective-permute-start | bytes 2162696 | tf_op jit(solution)/shard_map/ppermute | solution.py:271
  341.5 147.3 %reduce-scatter.9.cloned.1.call-start = ((), (), s32[]{:S(2)}) async-start(), calls=%async_computation.12 | async-start | bytes 1802240 | tf_op jit(solution)/shard_map/reduce_scatter | solution.py:1062
  356.0 34.8 %collective-permute-start.32 = (bf16[8,64,1408]{2,1,0:T(8,128)(2,1)}, bf16[8,64,1408]{2,1,0:T(8,128)(2,1)S(1)}, u32[]{:S(2)}, u32[]{:S(2)}) collective-permute-start(bf16[8,64,1408]{2,1,0:T(8,128)(2,1)} %get-tuple-element.217), channel_id=1, source_target_pairs={{0,16},{8,24},{16,0},{24,8},{1,17},{9,25},{17,1},{25,9},{2,18},{10... | collective-permute-start | bytes 4325384 | tf_op jit(solution)/shard_map/ppermute | solution.py:271
  357.3 34.6 %collective-permute-start.33 = (bf16[8,64,1408]{2,1,0:T(8,128)(2,1)}, bf16[8,64,1408]{2,1,0:T(8,128)(2,1)S(1)}, u32[]{:S(2)}, u32[]{:S(2)}) collective-permute-start(bf16[8,64,1408]{2,1,0:T(8,128)(2,1)} %get-tuple-element.228), channel_id=1, source_target_pairs={{0,8},{8,0},{16,24},{24,16},{1,9},{9,1},{17,25},{25,17},{2,10},{10... | collective-permute-start | bytes 4325384 | tf_op jit(solution)/shard_map/ppermute | solution.py:271
  365.3 37.1 %collective-permute-start.34 = (bf16[512,512]{1,0:T(8,128)(2,1)}, bf16[512,512]{1,0:T(8,128)(2,1)}, u32[]{:S(2)}, u32[]{:S(2)}) collective-permute-start(bf16[512,512]{1,0:T(8,128)(2,1)} %get-tuple-element.234), channel_id=1, source_target_pairs={{0,8},{8,0},{16,24},{24,16},{1,9},{9,1},{17,25},{25,17},{2,10},{10... | collective-permute-start | bytes 1572872 | tf_op jit(solution)/shard_map/ppermute | solution.py:271
  423.2 18.6 %collective-permute-start.37 = (bf16[8,32,1408]{2,1,0:T(8,128)(2,1)}, bf16[8,32,1408]{2,1,0:T(8,128)(2,1)S(1)}, u32[]{:S(2)}, u32[]{:S(2)}) collective-permute-start(bf16[8,32,1408]{2,1,0:T(8,128)(2,1)} %get-tuple-element.229), channel_id=1, source_target_pairs={{0,8},{8,0},{16,24},{24,16},{1,9},{9,1},{17,25},{25,17},{2,10},{10... | collective-permute-start | bytes 2162696 | tf_op jit(solution)/shard_map/ppermute | solution.py:271
  424.7 18.4 %collective-permute-start.38 = (bf16[8,32,1408]{2,1,0:T(8,128)(2,1)}, bf16[8,32,1408]{2,1,0:T(8,128)(2,1)}, u32[]{:S(2)}, u32[]{:S(2)}) collective-permute-start(bf16[8,32,1408]{2,1,0:T(8,128)(2,1)} %get-tuple-element.230), channel_id=1, source_target_pairs={{0,16},{8,24},{16,0},{24,8},{1,17},{9,25},{17,1},{25,9},{2,18},{10... | collective-permute-start | bytes 2162696 | tf_op jit(solution)/shard_map/ppermute | solution.py:271
  447.8 101.7 %reduce-scatter.11.cloned.1.call-start = ((), (), s32[]{:S(2)}) async-start(), calls=%async_computation.13 | async-start | bytes 3604480 | tf_op jit(solution)/shard_map/reduce_scatter | solution.py:1062
  448.5 127.6 %reduce-scatter.13.cloned.1.call-start = ((), (), s32[]{:S(2)}) async-start(), calls=%async_computation.14 | async-start | bytes 1310720 | tf_op jit(solution)/shard_map/reduce_scatter | solution.py:1062
  448.5 19.0 %collective-permute-start.39 = (bf16[8,64,768]{2,1,0:T(8,128)(2,1)}, bf16[8,64,768]{2,1,0:T(8,128)(2,1)S(1)}, u32[]{:S(2)}, u32[]{:S(2)}) collective-permute-start(bf16[8,64,768]{2,1,0:T(8,128)(2,1)} %get-tuple-element.237), channel_id=1, source_target_pairs={{0,8},{8,0},{16,24},{24,16},{1,9},{9,1},{17,25},{25,17},{2,10},{10... | collective-permute-start | bytes 2359304 | tf_op jit(solution)/shard_map/ppermute | solution.py:271
  449.6 20.5 %collective-permute-start.40 = (bf16[8,64,768]{2,1,0:T(8,128)(2,1)S(1)}, bf16[8,64,768]{2,1,0:T(8,128)(2,1)S(1)}, u32[]{:S(2)}, u32[]{:S(2)}) collective-permute-start(bf16[8,64,768]{2,1,0:T(8,128)(2,1)S(1)} %copy-done.90), channel_id=1, source_target_pairs={{0,16},{8,24},{16,0},{24,8},{1,17},{9,25},{17,1},{25,9},{2,18},{10... | collective-permute-start | bytes 2359304 | tf_op jit(solution)/shard_map/ppermute | solution.py:271
  450.2 38.5 %collective-permute-start.41 = (bf16[352,512]{1,0:T(8,128)(2,1)S(1)}, bf16[352,512]{1,0:T(8,128)(2,1)S(1)}, u32[]{:S(2)}, u32[]{:S(2)}) collective-permute-start(bf16[352,512]{1,0:T(8,128)(2,1)S(1)} %copy-done.77), channel_id=1, source_target_pairs={{0,16},{8,24},{16,0},{24,8},{1,17},{9,25},{17,1},{25,9},{2,18},{10... | collective-permute-start | bytes 1081352 | tf_op jit(solution)/shard_map/ppermute | solution.py:271
  474.5 18.5 %collective-permute-start.42 = (bf16[8,32,768]{2,1,0:T(8,128)(2,1)}, bf16[8,32,768]{2,1,0:T(8,128)(2,1)S(1)}, u32[]{:S(2)}, u32[]{:S(2)}) collective-permute-start(bf16[8,32,768]{2,1,0:T(8,128)(2,1)} %get-tuple-element.254), channel_id=1, source_target_pairs={{0,16},{8,24},{16,0},{24,8},{1,17},{9,25},{17,1},{25,9},{2,18},{10... | collective-permute-start | bytes 1179656 | tf_op jit(solution)/shard_map/ppermute | solution.py:271
  475.0 18.0 %collective-permute-start.43 = (bf16[8,32,768]{2,1,0:T(8,128)(2,1)}, bf16[8,32,768]{2,1,0:T(8,128)(2,1)S(1)}, u32[]{:S(2)}, u32[]{:S(2)}) collective-permute-start(bf16[8,32,768]{2,1,0:T(8,128)(2,1)} %get-tuple-element.255), channel_id=1, source_target_pairs={{0,8},{8,0},{16,24},{24,16},{1,9},{9,1},{17,25},{25,17},{2,10},{10... | collective-permute-start | bytes 1179656 | tf_op jit(solution)/shard_map/ppermute | solution.py:271
  476.0 17.0 %collective-permute-start.44 = (bf16[512,256]{1,0:T(8,128)(2,1)}, bf16[512,256]{1,0:T(8,128)(2,1)S(1)}, u32[]{:S(2)}, u32[]{:S(2)}) collective-permute-start(bf16[512,256]{1,0:T(8,128)(2,1)} %get-tuple-element.235), channel_id=1, source_target_pairs={{0,16},{8,24},{16,0},{24,8},{1,17},{9,25},{17,1},{25,9},{2,18},{10... | collective-permute-start | bytes 786440 | tf_op jit(solution)/shard_map/ppermute | solution.py:271
  506.6 34.3 %collective-permute-start.48 = (bf16[8,64,1408]{2,1,0:T(8,128)(2,1)}, bf16[8,64,1408]{2,1,0:T(8,128)(2,1)}, u32[]{:S(2)}, u32[]{:S(2)}) collective-permute-start(bf16[8,64,1408]{2,1,0:T(8,128)(2,1)} %get-tuple-element.257), channel_id=1, source_target_pairs={{0,16},{8,24},{16,0},{24,8},{1,17},{9,25},{17,1},{25,9},{2,18},{10... | collective-permute-start | bytes 4325384 | tf_op jit(solution)/shard_map/ppermute | solution.py:271
  507.2 34.0 %collective-permute-start.49 = (bf16[8,64,1408]{2,1,0:T(8,128)(2,1)}, bf16[8,64,1408]{2,1,0:T(8,128)(2,1)}, u32[]{:S(2)}, u32[]{:S(2)}) collective-permute-start(bf16[8,64,1408]{2,1,0:T(8,128)(2,1)} %get-tuple-element.277), channel_id=1, source_target_pairs={{0,8},{8,0},{16,24},{24,16},{1,9},{9,1},{17,25},{25,17},{2,10},{10... | collective-permute-start | bytes 4325384 | tf_op jit(solution)/shard_map/ppermute | solution.py:271
  508.2 139.7 %reduce-scatter.15.cloned.1.call-start = ((), (), s32[]{:S(2)}) async-start(), calls=%async_computation.15 | async-start | bytes 1802240 | tf_op jit(solution)/shard_map/reduce_scatter | solution.py:1062
  546.0 37.8 %collective-permute-start.51 = (bf16[8,32,1408]{2,1,0:T(8,128)(2,1)}, bf16[8,32,1408]{2,1,0:T(8,128)(2,1)}, u32[]{:S(2)}, u32[]{:S(2)}) collective-permute-start(bf16[8,32,1408]{2,1,0:T(8,128)(2,1)} %get-tuple-element.278), channel_id=1, source_target_pairs={{0,8},{8,0},{16,24},{24,16},{1,9},{9,1},{17,25},{25,17},{2,10},{10... | collective-permute-start | bytes 2162696 | tf_op jit(solution)/shard_map/ppermute | solution.py:271
  546.8 38.1 %collective-permute-start.52 = (bf16[8,32,1408]{2,1,0:T(8,128)(2,1)}, bf16[8,32,1408]{2,1,0:T(8,128)(2,1)}, u32[]{:S(2)}, u32[]{:S(2)}) collective-permute-start(bf16[8,32,1408]{2,1,0:T(8,128)(2,1)} %get-tuple-element.279), channel_id=1, source_target_pairs={{0,16},{8,24},{16,0},{24,8},{1,17},{9,25},{17,1},{25,9},{2,18},{10... | collective-permute-start | bytes 2162696 | tf_op jit(solution)/shard_map/ppermute | solution.py:271
  548.4 31.8 %collective-permute-start.50 = (bf16[512,512]{1,0:T(8,128)(2,1)}, bf16[512,512]{1,0:T(8,128)(2,1)}, u32[]{:S(2)}, u32[]{:S(2)}) collective-permute-start(bf16[512,512]{1,0:T(8,128)(2,1)} %get-tuple-element.291), channel_id=1, source_target_pairs={{0,8},{8,0},{16,24},{24,16},{1,9},{9,1},{17,25},{25,17},{2,10},{10... | collective-permute-start | bytes 1572872 | tf_op jit(solution)/shard_map/ppermute | solution.py:271
  551.5 38.1 %collective-permute-start.53 = (bf16[352,512]{1,0:T(8,128)(2,1)}, bf16[352,512]{1,0:T(8,128)(2,1)S(1)}, u32[]{:S(2)}, u32[]{:S(2)}) collective-permute-start(bf16[352,512]{1,0:T(8,128)(2,1)} %get-tuple-element.361), channel_id=1, source_target_pairs={{0,16},{8,24},{16,0},{24,8},{1,17},{9,25},{17,1},{25,9},{2,18},{10... | collective-permute-start | bytes 1081352 | tf_op jit(solution)/shard_map/ppermute | solution.py:271
  578.8 27.2 %collective-permute-start.54 = (bf16[528,512]{1,0:T(8,128)(2,1)}, bf16[528,512]{1,0:T(8,128)(2,1)S(1)}, u32[]{:S(2)}, u32[]{:S(2)}) collective-permute-start(bf16[528,512]{1,0:T(8,128)(2,1)} %append.2.refs_0_), channel_id=1, source_target_pairs={{0,16},{8,24},{16,0},{24,8},{1,17},{9,25},{17,1},{25,9},{2,18},{10... | collective-permute-start | bytes 1622024 | tf_op jit(solution)/shard_map/ppermute | solution.py:271
  580.1 25.9 %collective-permute-start.55 = (bf16[528,512]{1,0:T(8,128)(2,1)}, bf16[528,512]{1,0:T(8,128)(2,1)S(1)}, u32[]{:S(2)}, u32[]{:S(2)}) collective-permute-start(bf16[528,512]{1,0:T(8,128)(2,1)} %append.2.refs_0_), channel_id=1, source_target_pairs={{0,8},{8,0},{16,24},{24,16},{1,9},{9,1},{17,25},{25,17},{2,10},{10... | collective-permute-start | bytes 1622024 | tf_op jit(solution)/shard_map/ppermute | solution.py:271
  583.8 22.4 %collective-permute-start.56 = (bf16[528,512]{1,0:T(8,128)(2,1)}, bf16[528,512]{1,0:T(8,128)(2,1)S(1)}, u32[]{:S(2)}, u32[]{:S(2)}) collective-permute-start(bf16[528,512]{1,0:T(8,128)(2,1)} %append.2.refs_0_), channel_id=1, source_target_pairs={{0,24},{8,16},{16,8},{24,0},{1,25},{9,17},{17,9},{25,1},{2,26},{10... | collective-permute-start | bytes 1622024 | tf_op jit(solution)/shard_map/ppermute | solution.py:271
  592.8 15.0 %collective-permute-start.57 = (bf16[352,256]{1,0:T(8,128)(2,1)}, bf16[352,256]{1,0:T(8,128)(2,1)S(1)}, u32[]{:S(2)}, u32[]{:S(2)}) collective-permute-start(bf16[352,256]{1,0:T(8,128)(2,1)} %get-tuple-element.300), channel_id=1, source_target_pairs={{0,8},{8,0},{16,24},{24,16},{1,9},{9,1},{17,25},{25,17},{2,10},{10... | collective-permute-start | bytes 540680 | tf_op jit(solution)/shard_map/ppermute | solution.py:271
  597.8 16.7 %collective-permute-start.28 = (bf16[512,1024]{1,0:T(8,128)(2,1)S(1)}, bf16[512,1024]{1,0:T(8,128)(2,1)}, u32[]{:S(2)}, u32[]{:S(2)}) collective-permute-start(bf16[512,1024]{1,0:T(8,128)(2,1)S(1)} %convolution_convert_fusion), channel_id=1, source_target_pairs={{0,1},{1,0},{2,3},{3,2},{4,5},{5,4},{6,7},{7,6},{8,9},{9,8},{10,11... | collective-permute-start | bytes 3145736 | tf_op jit(solution)/shard_map/ppermute | solution.py:266
  597.9 109.0 %reduce-scatter.17.cloned.1.call-start = ((), (), s32[]{:S(2)}) async-start(), calls=%async_computation.16 | async-start | bytes 1310720 | tf_op jit(solution)/shard_map/reduce_scatter | solution.py:1062
  612.5 20.1 %collective-permute-start.59 = (bf16[8,64,768]{2,1,0:T(8,128)(2,1)S(1)}, bf16[8,64,768]{2,1,0:T(8,128)(2,1)}, u32[]{:S(2)}, u32[]{:S(2)}) collective-permute-start(bf16[8,64,768]{2,1,0:T(8,128)(2,1)S(1)} %copy-done.92), channel_id=1, source_target_pairs={{0,8},{8,0},{16,24},{24,16},{1,9},{9,1},{17,25},{25,17},{2,10},{10... | collective-permute-start | bytes 2359304 | tf_op jit(solution)/shard_map/ppermute | solution.py:271
  613.6 20.5 %collective-permute-start.60 = (bf16[8,64,768]{2,1,0:T(8,128)(2,1)S(1)}, bf16[8,64,768]{2,1,0:T(8,128)(2,1)}, u32[]{:S(2)}, u32[]{:S(2)}) collective-permute-start(bf16[8,64,768]{2,1,0:T(8,128)(2,1)S(1)} %copy-done.91), channel_id=1, source_target_pairs={{0,16},{8,24},{16,0},{24,8},{1,17},{9,25},{17,1},{25,9},{2,18},{10... | collective-permute-start | bytes 2359304 | tf_op jit(solution)/shard_map/ppermute | solution.py:271
  618.6 29.2 %collective-permute-start.68 = (bf16[512,256]{1,0:T(8,128)(2,1)}, bf16[512,256]{1,0:T(8,128)(2,1)}, u32[]{:S(2)}, u32[]{:S(2)}) collective-permute-start(bf16[512,256]{1,0:T(8,128)(2,1)} %get-tuple-element.292), channel_id=1, source_target_pairs={{0,16},{8,24},{16,0},{24,8},{1,17},{9,25},{17,1},{25,9},{2,18},{10... | collective-permute-start | bytes 786440 | tf_op jit(solution)/shard_map/ppermute | solution.py:271
  658.0 17.7 %collective-permute-start.75 = (bf16[4,192,512]{2,1,0:T(8,128)(2,1)}, bf16[4,192,512]{2,1,0:T(8,128)(2,1)S(1)}, u32[]{:S(2)}, u32[]{:S(2)}) collective-permute-start(bf16[4,192,512]{2,1,0:T(8,128)(2,1)} %pick.4), channel_id=1, source_target_pairs={{0,1},{1,0},{2,3},{3,2},{4,5},{5,4},{6,7},{7,6},{8,9},{9,8},{10,11... | collective-permute-start | bytes 2359304 | tf_op jit(solution)/shard_map/ppermute | solution.py:266
  658.0 14.7 %collective-permute-start.77 = (bf16[528,512]{1,0:T(8,128)(2,1)S(1)}, bf16[528,512]{1,0:T(8,128)(2,1)S(1)}, u32[]{:S(2)}, u32[]{:S(2)}) collective-permute-start(bf16[528,512]{1,0:T(8,128)(2,1)S(1)} %copy-done.31), channel_id=1, source_target_pairs={{0,16},{8,24},{16,0},{24,8},{1,17},{9,25},{17,1},{25,9},{2,18},{10... | collective-permute-start | bytes 1622024 | tf_op jit(solution)/shard_map/ppermute | solution.py:271
  659.3 15.1 %collective-permute-start.78 = (bf16[528,512]{1,0:T(8,128)(2,1)S(1)}, bf16[528,512]{1,0:T(8,128)(2,1)S(1)}, u32[]{:S(2)}, u32[]{:S(2)}) collective-permute-start(bf16[528,512]{1,0:T(8,128)(2,1)S(1)} %copy-done.31), channel_id=1, source_target_pairs={{0,8},{8,0},{16,24},{24,16},{1,9},{9,1},{17,25},{25,17},{2,10},{10... | collective-permute-start | bytes 1622024 | tf_op jit(solution)/shard_map/ppermute | solution.py:271
  660.3 26.0 %collective-permute-start.79 = (bf16[528,512]{1,0:T(8,128)(2,1)S(1)}, bf16[528,512]{1,0:T(8,128)(2,1)S(1)}, u32[]{:S(2)}, u32[]{:S(2)}) collective-permute-start(bf16[528,512]{1,0:T(8,128)(2,1)S(1)} %copy-done.31), channel_id=1, source_target_pairs={{0,24},{8,16},{16,8},{24,0},{1,25},{9,17},{17,9},{25,1},{2,26},{10... | collective-permute-start | bytes 1622024 | tf_op jit(solution)/shard_map/ppermute | solution.py:271
  661.5 30.1 %collective-permute-start.72 = (bf16[256,512]{1,0:T(8,128)(2,1)S(1)}, bf16[256,512]{1,0:T(8,128)(2,1)S(1)}, u32[]{:S(2)}, u32[]{:S(2)}) collective-permute-start(bf16[256,512]{1,0:T(8,128)(2,1)S(1)} %copy-done.53), channel_id=1, source_target_pairs={{0,8},{8,0},{16,24},{24,16},{1,9},{9,1},{17,25},{25,17},{2,10},{10... | collective-permute-start | bytes 786440 | tf_op jit(solution)/shard_map/ppermute | solution.py:271
  672.7 19.0 %collective-permute-start.73 = (bf16[256,512]{1,0:T(8,128)(2,1)S(1)}, bf16[256,512]{1,0:T(8,128)(2,1)S(1)}, u32[]{:S(2)}, u32[]{:S(2)}) collective-permute-start(bf16[256,512]{1,0:T(8,128)(2,1)S(1)} %copy-done.53), channel_id=1, source_target_pairs={{0,16},{8,24},{16,0},{24,8},{1,17},{9,25},{17,1},{25,9},{2,18},{10... | collective-permute-start | bytes 786440 | tf_op jit(solution)/shard_map/ppermute | solution.py:271
  674.4 22.4 %collective-permute-start.74 = (bf16[256,512]{1,0:T(8,128)(2,1)S(1)}, bf16[256,512]{1,0:T(8,128)(2,1)S(1)}, u32[]{:S(2)}, u32[]{:S(2)}) collective-permute-start(bf16[256,512]{1,0:T(8,128)(2,1)S(1)} %copy-done.53), channel_id=1, source_target_pairs={{0,24},{8,16},{16,8},{24,0},{1,25},{9,17},{17,9},{25,1},{2,26},{10... | collective-permute-start | bytes 786440 | tf_op jit(solution)/shard_map/ppermute | solution.py:271
  675.8 14.4 %collective-permute-start.61 = (f32[4,1024]{1,0:T(4,128)S(1)}, f32[4,1024]{1,0:T(4,128)S(1)}, u32[]{:S(2)}, u32[]{:S(2)}) collective-permute-start(f32[4,1024]{1,0:T(4,128)S(1)} %pad_maximum_fusion.1), channel_id=1, source_target_pairs={{0,2},{2,0},{4,6},{6,4},{1,3},{3,1},{5,7},{7,5},{8,10},{10,8},{12,... | collective-permute-start | bytes 49160 | tf_op jit(solution)/shard_map/ppermute | solution.py:1279
  690.2 25.7 %collective-permute-start.80 = (bf16[4,192,512]{2,1,0:T(8,128)(2,1)}, bf16[4,192,512]{2,1,0:T(8,128)(2,1)S(1)}, u32[]{:S(2)}, u32[]{:S(2)}) collective-permute-start(bf16[4,192,512]{2,1,0:T(8,128)(2,1)} %pick.6), channel_id=1, source_target_pairs={{0,1},{1,0},{2,3},{3,2},{4,5},{5,4},{6,7},{7,6},{8,9},{9,8},{10,11... | collective-permute-start | bytes 2359304 | tf_op jit(solution)/shard_map/ppermute | solution.py:266
  706.8 14.9 %collective-permute-start.69 = (bf16[256,512]{1,0:T(8,128)(2,1)}, bf16[256,512]{1,0:T(8,128)(2,1)S(1)}, u32[]{:S(2)}, u32[]{:S(2)}) collective-permute-start(bf16[256,512]{1,0:T(8,128)(2,1)} %reduce-scatter.17.cloned.1.call-done.refs_0_), channel_id=1, source_target_pairs={{0,8},{8,0},{16,24},{24,16},{1,9},{9,1},{17,25},{25,17},{2,10},{10... | collective-permute-start | bytes 786440 | tf_op jit(solution)/shard_map/ppermute | solution.py:271
  (122 other events, 794.7 us)
Sparse Core Ops, SparseCore 0:
  15.1 31.6 all-gather.5
  48.9 46.7 all-gather.9
  97.8 26.6 all-gather.7
  126.5 46.7 all-gather.11
  175.3 45.9 all-gather.13
  341.6 54.8 reduce-scatter.6
  447.9 30.0 reduce-scatter.8
  480.3 55.0 reduce-scatter.10
  537.7 26.9 reduce-scatter.12
  598.0 31.0 reduce-scatter.14
  654.9 24.7 reduce-scatter.16
